TPU v7x, 32 devices: a whole 2x2x4 slice. The times are simulated.
32 devices in a mesh: dp: 2 (over y), ctx: 4 (over x, core), exp: 4 (over z).
Axes of the slice: x: 2, y: 2, z: 4, core: 2. Of those that a mesh axis runs over, the one named last changes fastest.
Arguments:
- hidden_in: bfloat16 [2, 4, 1536, 2048], P('dp', 'exp', 'ctx'), may hold values from -6 to 6
- segments: int32 [2, 4, 1536], P('dp', 'exp'), may hold values from 0 to 3, as said below
- routes: int32 [2, 4, 1536, 8], P('dp', 'exp', 'ctx'), may hold values from 0 to 15, all different within a row; in each aligned block of 384 rows (0 to 383, 384 to 767, ..., all dimensions but the last counted through in order) at most 240 rows name the same one
- attn_gain: bfloat16 [2048], replicated, may hold values from 0.5 to 1.5
- query_weight: bfloat16 [2048, 2048], P(('dp', 'ctx', 'exp')), may hold values from -0.125 to 0.125
- key_weight: bfloat16 [2048, 2048], P(('dp', 'ctx', 'exp')), may hold values from -0.125 to 0.125
- value_weight: bfloat16 [2048, 2048], P(('dp', 'ctx', 'exp')), may hold values from -0.125 to 0.125
- query_gain: bfloat16 [2048], replicated, may hold values from 0.5 to 1.5
- key_gain: bfloat16 [2048], replicated, may hold values from 0.5 to 1.5
- output_weight: bfloat16 [2048, 2048], P(('dp', 'ctx', 'exp')), may hold values from -1.5 to 1.5
- ffn_gain: bfloat16 [2048], replicated, may hold values from 0.5 to 1.5
- router_weight: bfloat16 [2048, 16], replicated, may hold values from -0.0625 to 0.0625
- gate_weight: bfloat16 [16, 2048, 1024], P(('ctx', 'exp')), may hold values from -0.125 to 0.125
- up_weight: bfloat16 [16, 2048, 1024], P(('ctx', 'exp')), may hold values from -0.125 to 0.125
- down_weight: bfloat16 [16, 1024, 2048], P(('ctx', 'exp')), may hold values from -7.1875 to 7.1875
- cotangent: bfloat16 [2, 4, 1536, 2048], P('dp', 'exp', 'ctx'), may hold values from -6 to 6
Outputs:
- output: bfloat16 [2, 4, 1536, 2048], P('dp', 'exp', 'ctx')
- hidden_grad: bfloat16 [2, 4, 1536, 2048], P('dp', 'exp', 'ctx')
- attn_gain_grad: float32 [2048], replicated
- query_weight_grad: float32 [2048, 2048], P(('dp', 'ctx', 'exp'))
- key_weight_grad: float32 [2048, 2048], P(('dp', 'ctx', 'exp'))
- value_weight_grad: float32 [2048, 2048], P(('dp', 'ctx', 'exp'))
- query_gain_grad: float32 [2048], replicated
- key_gain_grad: float32 [2048], replicated
- output_weight_grad: float32 [2048, 2048], P(('dp', 'ctx', 'exp'))
- ffn_gain_grad: float32 [2048], replicated
- router_weight_grad: float32 [2048, 16], replicated
- gate_weight_grad: float32 [16, 2048, 1024], P(('ctx', 'exp'))
- up_weight_grad: float32 [16, 2048, 1024], P(('ctx', 'exp'))
- down_weight_grad: float32 [16, 1024, 2048], P(('ctx', 'exp'))
Inputs may be any that keep to these rules, and one draw needn't show every extreme that they name: `segments`: in each group the first 512 tokens have id 0; the others form (1024 + 512 - 1) // 512 + 1 continuations numbered 1, 2, ... in order, each of consecutive tokens and of 1 to 512 tokens, one of them exactly 512. `routes`: each row names 8 different experts; among the 384 rows of one device no expert is named more than 240 times.
All inputs are finite; a program needn't handle non-finite values.
Results may differ from a plain program's by a relative error of at most 0.022.
Values may be sent and summed in bfloat16 or wider, within the bound.
A program may use at most 448 MiB of HBM per device.

v0:
```python
from functools import partial

import jax
import jax.numpy as jnp
from jax import lax
from jax.sharding import PartitionSpec as P

HEAD = 128
PROMPT = 512


epsilon = 1e-05
theta_base = 10000.0
masked_score = -1e30


def rms_scale(values, gain_vec):
    return (
        values * lax.rsqrt(jnp.mean(values * values, axis=-1, keepdims=True) + epsilon) * gain_vec
    )


def rotate(values, angles):
    half_size = values.shape[-1] // 2
    cosine = jnp.cos(angles)[:, None, :]
    sine_table = jnp.sin(angles)[:, None, :]
    front_half = values[..., :half_size]
    back_half = values[..., half_size:]
    return jnp.concatenate(
        [
            front_half * cosine - back_half * sine_table,
            back_half * cosine + front_half * sine_table,
        ],
        axis=-1,
    )


def query_prep(raw_values, gain_vec, angles):
    row_count = raw_values.shape[0]
    normed = rms_scale(raw_values, gain_vec).reshape(row_count, raw_values.shape[1] // HEAD, HEAD)
    return rotate(normed, angles).reshape(row_count, raw_values.shape[1])


def route_tokens(blocks):
    moved = lax.all_to_all(blocks, ("ctx", "exp"), split_axis=0, concat_axis=0, tiled=True)
    return moved


def contract_rows(left, right):
    return lax.dot_general(
        left, right, (((0,), (0,)), ((), ())), preferred_element_type=jnp.float32
    )


def contract_cols(left, right):
    return lax.dot_general(
        left, right, (((1,), (1,)), ((), ())), preferred_element_type=jnp.float32
    )


def per_device(
    hidden_in,
    segments,
    routes,
    attn_gain,
    query_weight,
    key_weight,
    value_weight,
    query_gain,
    key_gain,
    output_weight,
    ffn_gain,
    router_weight,
    gate_weight,
    up_weight,
    down_weight,
    cotangent,
):
    tok_rows = hidden_in.shape[2]
    model_width = hidden_in.shape[3]
    head_count = model_width // HEAD
    topk_count = routes.shape[3]
    experts = lax.axis_size("ctx") * lax.axis_size("exp")
    capacity = (5 * tok_rows * topk_count + 4 * experts - 1) // (4 * experts)
    slot_total = experts * capacity
    scale_factor = HEAD ** (-0.5)
    hidden_float = hidden_in[0, 0].astype(jnp.float32)
    labels_all = segments[0, 0]
    group_len = labels_all.shape[0]
    row_start = lax.axis_index("ctx") * tok_rows
    labels_own = lax.dynamic_slice_in_dim(labels_all, row_start, tok_rows)
    own_index = row_start + jnp.arange(tok_rows, dtype=jnp.int32)
    all_index = jnp.arange(group_len, dtype=jnp.int32)
    before = jnp.sum((labels_all[None, :] < labels_own[:, None]).astype(jnp.int32), axis=1)
    positions = own_index - before + jnp.where(labels_own > 0, PROMPT, 0).astype(jnp.int32)
    half_size = HEAD // 2
    frequency = theta_base ** (-(jnp.arange(half_size, dtype=jnp.float32) * 2.0 / HEAD))
    angles = positions.astype(jnp.float32)[:, None] * frequency[None, :]
    attn_gain_f = attn_gain.astype(jnp.float32)
    query_gain_f = query_gain.astype(jnp.float32)
    key_gain_f = key_gain.astype(jnp.float32)
    ffn_gain_f = ffn_gain.astype(jnp.float32)
    query_full, key_full, value_full, output_full = (
        lax.all_gather(query_weight, ("dp", "ctx", "exp"), axis=0, tiled=True),
        lax.all_gather(key_weight, ("dp", "ctx", "exp"), axis=0, tiled=True),
        lax.all_gather(value_weight, ("dp", "ctx", "exp"), axis=0, tiled=True),
        lax.all_gather(output_weight, ("dp", "ctx", "exp"), axis=0, tiled=True),
    )
    normed_float, attn_pullback = jax.vjp(rms_scale, hidden_float, attn_gain_f)
    normed = normed_float.astype(jnp.bfloat16)
    query_raw = jnp.dot(normed, query_full, preferred_element_type=jnp.float32)
    key_raw = jnp.dot(normed, key_full, preferred_element_type=jnp.float32)
    value_raw = jnp.dot(normed, value_full, preferred_element_type=jnp.float32)
    query_float, query_pullback = jax.vjp(
        partial(query_prep, angles=angles), query_raw, query_gain_f
    )
    key_float, key_pullback = jax.vjp(partial(query_prep, angles=angles), key_raw, key_gain_f)
    query_rot = query_float.astype(jnp.bfloat16)
    key_rot = key_float.astype(jnp.bfloat16)
    value_low = value_raw.astype(jnp.bfloat16)
    key_group, value_group = (
        lax.all_gather(key_rot, "ctx", axis=0, tiled=True),
        lax.all_gather(value_low, "ctx", axis=0, tiled=True),
    )
    query_heads = query_rot.reshape(tok_rows, head_count, HEAD)
    key_heads = key_group.reshape(group_len, head_count, HEAD)
    value_heads = value_group.reshape(group_len, head_count, HEAD)
    allowed = (all_index[None, :] <= own_index[:, None]) & (
        (labels_all[None, :] == 0) | (labels_all[None, :] == labels_own[:, None])
    )
    scores = (
        jnp.einsum("qhd,khd->hqk", query_heads, key_heads, preferred_element_type=jnp.float32)
        * scale_factor
    )
    masked = jnp.where(allowed[None], scores, masked_score)
    attn_prob = jax.nn.softmax(masked, axis=-1)
    prob_low = attn_prob.astype(jnp.bfloat16)
    mixed = jnp.einsum("hqk,khd->qhd", prob_low, value_heads, preferred_element_type=jnp.float32)
    mix_low = mixed.reshape(tok_rows, model_width).astype(jnp.bfloat16)
    residual_mid = hidden_float + jnp.dot(mix_low, output_full, preferred_element_type=jnp.float32)
    ffn_float, ffn_pullback = jax.vjp(rms_scale, residual_mid, ffn_gain_f)
    ffn_normed = ffn_float.astype(jnp.bfloat16)
    logits = jnp.dot(ffn_normed, router_weight, preferred_element_type=jnp.float32)
    router_prob = jax.nn.softmax(logits, axis=-1)
    own_routes = routes[0, 0]
    gate_low = jnp.take_along_axis(router_prob, own_routes, axis=1).astype(jnp.bfloat16)
    expert_ids = jnp.arange(experts, dtype=jnp.int32)
    route_match = own_routes[:, :, None] == expert_ids[None, None, :]
    route_hits = jnp.sum(route_match.astype(jnp.int32), axis=1)
    tokens_at = jnp.arange(tok_rows, dtype=jnp.int32)
    lower_mask = (tokens_at[:, None] > tokens_at[None, :]).astype(jnp.int32)
    earlier = jnp.dot(lower_mask, route_hits, preferred_element_type=jnp.int32)
    slot_index = jnp.take_along_axis(earlier, own_routes, axis=1)
    flat_slot = own_routes * capacity + slot_index
    slot_ids = jnp.arange(slot_total, dtype=jnp.int32)
    matches = slot_ids[:, None, None] == flat_slot[None, :, :]
    dispatch = jnp.any(matches, axis=2).astype(jnp.bfloat16)
    combine = jnp.sum(jnp.where(matches, gate_low[None].astype(jnp.float32), 0.0), axis=2).astype(
        jnp.bfloat16
    )
    dispatched = jnp.dot(dispatch, ffn_normed, preferred_element_type=jnp.float32).astype(
        jnp.bfloat16
    )
    received = route_tokens(dispatched.reshape(experts, capacity, model_width)).reshape(
        slot_total, model_width
    )
    gate_mat = gate_weight[0]
    up_mat = up_weight[0]
    down_mat = down_weight[0]
    gate_pre = jnp.dot(received, gate_mat, preferred_element_type=jnp.float32)
    up_pre = jnp.dot(received, up_mat, preferred_element_type=jnp.float32)
    expert_hidden = (jax.nn.silu(gate_pre) * up_pre).astype(jnp.bfloat16)
    expert_out = jnp.dot(expert_hidden, down_mat, preferred_element_type=jnp.float32).astype(
        jnp.bfloat16
    )
    returned = route_tokens(expert_out.reshape(experts, capacity, model_width)).reshape(
        slot_total, model_width
    )
    moe_out = jnp.einsum("ft,fd->td", combine, returned, preferred_element_type=jnp.float32)
    output = (residual_mid + moe_out).astype(jnp.bfloat16)
    cot_low = cotangent[0, 0]
    d_expert_out = jnp.dot(combine, cot_low, preferred_element_type=jnp.float32).astype(
        jnp.bfloat16
    )
    d_received = route_tokens(d_expert_out.reshape(experts, capacity, model_width)).reshape(
        slot_total, model_width
    )
    gate_scores = jnp.einsum("td,fd->tf", cot_low, returned, preferred_element_type=jnp.float32)
    d_gate = jnp.take_along_axis(gate_scores, flat_slot, axis=1)
    d_hidden_e = contract_cols(d_received, down_mat)
    down_grad = contract_rows(expert_hidden, d_received)
    sigmoid_gate = jax.nn.sigmoid(gate_pre)
    d_gate_pre = (
        d_hidden_e * up_pre * sigmoid_gate * (1.0 + gate_pre * (1.0 - sigmoid_gate))
    ).astype(jnp.bfloat16)
    d_up_pre = (d_hidden_e * jax.nn.silu(gate_pre)).astype(jnp.bfloat16)
    gate_grad = contract_rows(received, d_gate_pre)
    up_grad = contract_rows(received, d_up_pre)
    d_dispatched = (contract_cols(d_gate_pre, gate_mat) + contract_cols(d_up_pre, up_mat)).astype(
        jnp.bfloat16
    )
    d_sent_rows = route_tokens(d_dispatched.reshape(experts, capacity, model_width)).reshape(
        slot_total, model_width
    )
    d_router = jnp.sum(jnp.where(route_match, d_gate[:, :, None], 0.0), axis=1)
    d_logits = (
        router_prob * (d_router - jnp.sum(router_prob * d_router, axis=-1, keepdims=True))
    ).astype(jnp.bfloat16)
    router_grad = contract_rows(ffn_normed, d_logits)
    d_ffn_normed = jnp.einsum(
        "ft,fd->td", dispatch, d_sent_rows, preferred_element_type=jnp.float32
    ) + contract_cols(d_logits, router_weight)
    d_mid_norm, ffn_gain_grad = ffn_pullback(d_ffn_normed)
    d_residual = cot_low.astype(jnp.float32) + d_mid_norm
    d_branch = d_residual.astype(jnp.bfloat16)
    query_use, key_use, value_use, output_use = (query_full, key_full, value_full, output_full)
    output_grad = contract_rows(mix_low, d_branch)
    d_mix = contract_cols(d_branch, output_use).astype(jnp.bfloat16)
    d_mix_heads = d_mix.reshape(tok_rows, head_count, HEAD)
    d_prob = jnp.einsum(
        "qhd,khd->hqk", d_mix_heads, value_heads, preferred_element_type=jnp.float32
    )
    row_total = jnp.sum(attn_prob * d_prob, axis=-1)
    d_scores = (attn_prob * (d_prob - row_total[..., None])).astype(jnp.bfloat16)
    d_query_rot = (
        jnp.einsum("hqk,khd->qhd", d_scores, key_heads, preferred_element_type=jnp.float32).reshape(
            tok_rows, model_width
        )
        * scale_factor
    )
    d_key_group = (
        jnp.einsum(
            "hqk,qhd->khd", d_scores, query_heads, preferred_element_type=jnp.float32
        ).reshape(group_len, model_width)
        * scale_factor
    )
    d_value_group = jnp.einsum(
        "hqk,qhd->khd", prob_low, d_mix_heads, preferred_element_type=jnp.float32
    ).reshape(group_len, model_width)
    d_key_rot, d_value_own = (
        lax.psum_scatter(
            d_key_group.astype(jnp.bfloat16), "ctx", scatter_dimension=0, tiled=True
        ).astype(jnp.float32),
        lax.psum_scatter(
            d_value_group.astype(jnp.bfloat16), "ctx", scatter_dimension=0, tiled=True
        ).astype(jnp.float32),
    )
    d_query_raw, query_gain_grad = query_pullback(d_query_rot)
    d_key_raw, key_gain_grad = key_pullback(d_key_rot)
    d_query_low = d_query_raw.astype(jnp.bfloat16)
    d_key_low = d_key_raw.astype(jnp.bfloat16)
    d_value_low = d_value_own.astype(jnp.bfloat16)
    query_grad = contract_rows(normed, d_query_low)
    key_grad = contract_rows(normed, d_key_low)
    value_grad = contract_rows(normed, d_value_low)
    d_normed = (
        contract_cols(d_query_low, query_use)
        + contract_cols(d_key_low, key_use)
        + contract_cols(d_value_low, value_use)
    )
    d_hidden_norm, attn_gain_grad = attn_pullback(d_normed)
    hidden_grad = (d_residual + d_hidden_norm).astype(jnp.bfloat16)
    query_sum, key_sum, value_sum, output_sum = (
        lax.psum_scatter(query_grad, ("dp", "ctx", "exp"), scatter_dimension=0, tiled=True),
        lax.psum_scatter(key_grad, ("dp", "ctx", "exp"), scatter_dimension=0, tiled=True),
        lax.psum_scatter(value_grad, ("dp", "ctx", "exp"), scatter_dimension=0, tiled=True),
        lax.psum_scatter(output_grad, ("dp", "ctx", "exp"), scatter_dimension=0, tiled=True),
    )
    gate_sum, up_sum, down_sum = (
        lax.psum(gate_grad.astype(jnp.bfloat16), "dp").astype(jnp.float32),
        lax.psum(up_grad.astype(jnp.bfloat16), "dp").astype(jnp.float32),
        lax.psum(down_grad.astype(jnp.bfloat16), "dp").astype(jnp.float32),
    )
    router_sum, attn_gain_sum, query_gain_sum, key_gain_sum, ffn_gain_sum = lax.psum(
        (router_grad, attn_gain_grad, query_gain_grad, key_gain_grad, ffn_gain_grad),
        ("dp", "ctx", "exp"),
    )
    return (
        output[None, None],
        hidden_grad[None, None],
        attn_gain_sum,
        query_sum,
        key_sum,
        value_sum,
        query_gain_sum,
        key_gain_sum,
        output_sum,
        ffn_gain_sum,
        router_sum,
        gate_sum[None],
        up_sum[None],
        down_sum[None],
    )


def solution(mesh):
    return jax.shard_map(
        per_device,
        mesh=mesh,
        in_specs=(
            P("dp", "exp", "ctx", None),
            P("dp", "exp", None),
            P("dp", "exp", "ctx", None),
            P(),
            P(("dp", "ctx", "exp"), None),
            P(("dp", "ctx", "exp"), None),
            P(("dp", "ctx", "exp"), None),
            P(),
            P(),
            P(("dp", "ctx", "exp"), None),
            P(),
            P(),
            P(("ctx", "exp"), None, None),
            P(("ctx", "exp"), None, None),
            P(("ctx", "exp"), None, None),
            P("dp", "exp", "ctx", None),
        ),
        out_specs=(
            P("dp", "exp", "ctx", None),
            P("dp", "exp", "ctx", None),
            P(),
            P(("dp", "ctx", "exp"), None),
            P(("dp", "ctx", "exp"), None),
            P(("dp", "ctx", "exp"), None),
            P(),
            P(),
            P(("dp", "ctx", "exp"), None),
            P(),
            P(),
            P(("ctx", "exp"), None, None),
            P(("ctx", "exp"), None, None),
            P(("ctx", "exp"), None, None),
        ),
        check_vma=False,
    )
```

profile of v0, /device:TPU:8, one launch (start us, length us, event | category | flops | bytes accessed | tf_op | source)
XLA Modules:
  0.0 4191.4 jit_solution(2944350176354347365)
XLA Ops:
  16.7 72.9 %all-gather.11.cloned.1.call-done = bf16[2048,2048]{1,0:T(8,128)(2,1)} async-done(((bf16[64,2048]{1,0:T(8,128)(2,1)}), bf16[2048,2048]{1,0:T(8,128)(2,1)}) %all-gather.11.cloned.1.call-update) | async-done | bytes 8388624 | tf_op jit(solution)/shard_map/all_gather | solution.py:104
  100.1 68.4 %all-gather.13.cloned.1.call-done = bf16[2048,2048]{1,0:T(8,128)(2,1)} async-done(((bf16[64,2048]{1,0:T(8,128)(2,1)}), bf16[2048,2048]{1,0:T(8,128)(2,1)}) %all-gather.13.cloned.1.call-update) | async-done | bytes 8388624 | tf_op jit(solution)/shard_map/all_gather | solution.py:105
  203.6 43.7 %all-gather.7.cloned.1.call-done = bf16[2048,2048]{1,0:T(8,128)(2,1)} async-done(((bf16[64,2048]{1,0:T(8,128)(2,1)}), bf16[2048,2048]{1,0:T(8,128)(2,1)}) %all-gather.7.cloned.1.call-update) | async-done | bytes 8388624 | tf_op jit(solution)/shard_map/all_gather | solution.py:106
  258.7 24.9 gather_fusion
  285.5 24.2 fusion.1
  359.6 63.3 %all-gather.17.cloned.1.call-done = bf16[2048,2048]{1,0:T(8,128)(2,1)} async-done(((bf16[64,2048]{1,0:T(8,128)(2,1)}), bf16[2048,2048]{1,0:T(8,128)(2,1)}) %all-gather.17.cloned.1.call-update) | async-done | bytes 8388624 | tf_op jit(solution)/shard_map/all_gather | solution.py:107
  449.9 344.2 %all_to_all.20 = bf16[16,240,2048]{2,1,0:T(8,128)(2,1)S(1)} all-to-all(bf16[16,240,2048]{2,1,0:T(8,128)(2,1)S(1)} %bitcast.210), channel_id=1, replica_groups=mesh['dp'=2,'ctx'=4,'exp'=4] {'ctx','exp'}, dimensions={0} | all-to-all | bytes 31457280 | tf_op jit(solution)/shard_map/all_to_all | solution.py:45
  821.2 29.1 multiply_convert_fusion.3
  884.5 333.6 %all-to-all-done.1 = bf16[16,240,2048]{2,1,0:T(8,128)(2,1)} async-done(((bf16[16,240,2048]{2,1,0:T(8,128)(2,1)}), bf16[16,240,2048]{2,1,0:T(8,128)(2,1)}, u32[]{:S(2)}, u32[]{:S(2)}) %all-to-all-start.1) | async-done | bytes 15728672 | tf_op jit(solution)/shard_map/all_to_all | solution.py:45
  1231.6 42.8 %gather_fusion.2 = f32[3072]{0:T(1024)S(1)} fusion(f32[384,3840]{0,1:T(8,128)} %convolution_bitcast_fusion, s32[3072]{0:T(1024)S(1)} %reshape.514), kind=kCustom, calls=%fused_computation.2 | custom fusion | bytes 49152 | tf_op jit(solution)/shard_map/jit(take_along_axis)/gather | solution.py:189
  1275.3 24.6 gather_fusion.1
  1333.7 347.8 %all_to_all.21 = bf16[16,240,2048]{2,1,0:T(8,128)(2,1)} all-to-all(bf16[16,240,2048]{2,1,0:T(8,128)(2,1)S(1)} %bitcast.211), channel_id=1, replica_groups=mesh['dp'=2,'ctx'=4,'exp'=4] {'ctx','exp'}, dimensions={0} | all-to-all | bytes 31457280 | tf_op jit(solution)/shard_map/all_to_all | solution.py:45
  1681.5 33.9 multiply_convert_fusion.1
  1739.2 26.2 add_convert_fusion
  1772.7 337.7 %all-to-all-done.3 = bf16[16,240,2048]{2,1,0:T(8,128)(2,1)} async-done(((bf16[16,240,2048]{2,1,0:T(8,128)(2,1)}), bf16[16,240,2048]{2,1,0:T(8,128)(2,1)}, u32[]{:S(2)}, u32[]{:S(2)}) %all-to-all-start.3) | async-done | bytes 15728672 | tf_op jit(solution)/shard_map/all_to_all | solution.py:45
  2156.8 31.6 multiply_reduce_fusion
  2188.3 31.7 multiply_convert_fusion
  2405.0 192.5 %all-reduce.11.cloned.1.call-done = (bf16[1,2048,1024]{2,1,0:T(8,128)(2,1)}, bf16[1,2048,1024]{2,1,0:T(8,128)(2,1)}, bf16[1,1024,2048]{2,1,0:T(8,128)(2,1)}) async-done(((bf16[1,2048,1024]{2,1,0:T(8,128)(2,1)}, bf16[1,2048,1024]{2,1,0:T(8,128)(2,1)}, bf16[1,1024,2048]{2,1,0:T(8,128)(2,1)}), (bf16[1,2048,1024]{2,1,0:T(8,128)(2,1)}, bf16[1,2048,1024]{2,1,0:T(8,128)(2,1)}, ...) | async-done | bytes 12582928 | tf_op jit(solution)/shard_map/psum | solution.py:270
  2635.0 40.3 all-reduce.4
  2680.2 45.7 %all-reduce.9.cloned.1.call-done = f32[2048,16]{0,1:T(8,128)} async-done(((f32[2048,16]{0,1:T(8,128)}), f32[2048,16]{0,1:T(8,128)}) %all-reduce.9.cloned.1.call-update) | async-done | bytes 131088 | tf_op jit(solution)/shard_map/psum | solution.py:274
  2726.0 362.2 %reduce-scatter.17.cloned.1.call-done = f32[64,2048]{1,0:T(8,128)} async-done(((f32[2048,2048]{1,0:T(8,128)}), f32[64,2048]{1,0:T(8,128)}) %reduce-scatter.17.cloned.1.call-update) | async-done | bytes 524304 | tf_op jit(solution)/shard_map/reduce_scatter | solution.py:267
  3088.2 364.9 %reduce-scatter.15.cloned.1.call-done = f32[64,2048]{1,0:T(8,128)} async-done(((f32[2048,2048]{1,0:T(8,128)}), f32[64,2048]{1,0:T(8,128)}) %reduce-scatter.15.cloned.1.call-update) | async-done | bytes 524304 | tf_op jit(solution)/shard_map/reduce_scatter | solution.py:266
  3453.1 365.1 %reduce-scatter.11.cloned.1.call-done = f32[64,2048]{1,0:T(8,128)} async-done(((f32[2048,2048]{1,0:T(8,128)}), f32[64,2048]{1,0:T(8,128)}) %reduce-scatter.11.cloned.1.call-update) | async-done | bytes 524304 | tf_op jit(solution)/shard_map/reduce_scatter | solution.py:264
  3818.1 364.9 %reduce-scatter.13.cloned.1.call-done = f32[64,2048]{1,0:T(8,128)} async-done(((f32[2048,2048]{1,0:T(8,128)}), f32[64,2048]{1,0:T(8,128)}) %reduce-scatter.13.cloned.1.call-update) | async-done | bytes 524304 | tf_op jit(solution)/shard_map/reduce_scatter | solution.py:265
  (324 shorter events, 559.8 us)
Async XLA Ops:
  7.2 876.7 %copy-start = (bf16[2048,16]{0,1:T(8,128)(2,1)S(1)}, bf16[2048,16]{0,1:T(8,128)(2,1)}, u32[]{:S(2)}) copy-start(bf16[2048,16]{0,1:T(8,128)(2,1)} %param.27) | copy-start | bytes 196612
  7.2 82.4 %all-gather.11.cloned.1.call-start = ((), (), s32[]{:S(2)}) async-start(), calls=%async_computation.12 | async-start | bytes 8650752 | tf_op jit(solution)/shard_map/all_gather | solution.py:104
  7.9 160.6 %all-gather.13.cloned.1.call-start = ((), (), s32[]{:S(2)}) async-start(), calls=%async_computation.13 | async-start | bytes 8650752 | tf_op jit(solution)/shard_map/all_gather | solution.py:105
  8.7 238.7 %all-gather.7.cloned.1.call-start = ((), (), s32[]{:S(2)}) async-start(), calls=%async_computation.10 | async-start | bytes 8650752 | tf_op jit(solution)/shard_map/all_gather | solution.py:106
  9.4 300.3 %all-gather.15.cloned.1.call-start = ((), (), s32[]{:S(2)}) async-start(), calls=%async_computation.14 | async-start | bytes 7864320 | tf_op jit(solution)/shard_map/all_gather | solution.py:122
  10.2 237.2 %copy-start.43 = (f32[2048]{0:T(1024)}, f32[2048]{0:T(1024)S(1)}, u32[]{:S(2)}) copy-start(f32[2048]{0:T(1024)S(1)} %convert_element_type.161) | copy-start | bytes 24580
  15.2 232.2 %copy-start.47 = (f32[384]{0:T(512)}, f32[384]{0:T(512)S(1)}, u32[]{:S(2)}) copy-start(f32[384]{0:T(512)S(1)} %fusion.67) | copy-start | bytes 4612
  203.6 139.0 %all-gather.9.cloned.1.call-start = ((), (), s32[]{:S(2)}) async-start(), calls=%async_computation.11 | async-start | bytes 7864320 | tf_op jit(solution)/shard_map/all_gather | solution.py:123
  255.7 167.2 %all-gather.17.cloned.1.call-start = ((), (), s32[]{:S(2)}) async-start(), calls=%async_computation.15 | async-start | bytes 8650752 | tf_op jit(solution)/shard_map/all_gather | solution.py:107
  256.3 182.5 %copy-start.53 = (f32[2048]{0:T(1024)}, f32[2048]{0:T(1024)S(1)}, u32[]{:S(2)}) copy-start(f32[2048]{0:T(1024)S(1)} %convert_element_type.174) | copy-start | bytes 24580
  441.2 442.7 %copy-start.19 = (bf16[384,2048]{1,0:T(8,128)(2,1)}, bf16[384,2048]{1,0:T(8,128)(2,1)S(1)}, u32[]{:S(2)}) copy-start(bf16[384,2048]{1,0:T(8,128)(2,1)S(1)} %multiply_convert_fusion.5) | copy-start | bytes 4718596
  873.1 345.0 %copy-start.39 = (bf16[1,1,384,2048]{3,2,1,0:T(8,128)(2,1)S(1)}, bf16[1,1,384,2048]{3,2,1,0:T(8,128)(2,1)}, u32[]{:S(2)}) copy-start(bf16[1,1,384,2048]{3,2,1,0:T(8,128)(2,1)} %param.31) | copy-start | bytes 4718596
  873.1 345.0 %all-to-all-start.1 = ((bf16[16,240,2048]{2,1,0:T(8,128)(2,1)}), bf16[16,240,2048]{2,1,0:T(8,128)(2,1)}, u32[]{:S(2)}, u32[]{:S(2)}) async-start(bf16[16,240,2048]{2,1,0:T(8,128)(2,1)} %bitcast.208), calls=%async_computation.1 | async-start | bytes 31457280 | tf_op jit(solution)/shard_map/all_to_all | solution.py:45
  1765.4 345.0 %copy-start.42 = (pred[3840,384]{1,0:T(8,128)(4,1)S(1)}, pred[3840,384]{1,0:T(8,128)(4,1)}, u32[]{:S(2)}) copy-start(pred[3840,384]{1,0:T(8,128)(4,1)} %fusion.1) | copy-start | bytes 4423684
  1765.4 345.0 %all-to-all-start.3 = ((bf16[16,240,2048]{2,1,0:T(8,128)(2,1)}), bf16[16,240,2048]{2,1,0:T(8,128)(2,1)}, u32[]{:S(2)}, u32[]{:S(2)}) async-start(bf16[16,240,2048]{2,1,0:T(8,128)(2,1)} %bitcast.209), calls=%async_computation.3 | async-start | bytes 31457280 | tf_op jit(solution)/shard_map/all_to_all | solution.py:45
  1772.6 547.1 %reduce-scatter.21.cloned.1.call-start = ((), (), s32[]{:S(2)}) async-start(), calls=%async_computation.22 | async-start | bytes 7864320
  1772.7 348.1 %copy-start.59 = (bf16[384,16]{0,1:T(8,128)(2,1)}, bf16[384,16]{0,1:T(8,128)(2,1)S(1)}, u32[]{:S(2)}) copy-start(bf16[384,16]{0,1:T(8,128)(2,1)S(1)} %multiply_convert_fusion.6) | copy-start | bytes 36868
  2156.7 186.8 %reduce-scatter.19.cloned.1.call-start = ((), (), s32[]{:S(2)}) async-start(), calls=%async_computation.21 | async-start | bytes 7864320
  2241.4 356.2 %all-reduce.11.cloned.1.call-start = ((), (), s32[]{:S(2)}) async-start(), calls=%async_computation.23 | async-start | bytes 25165824 | tf_op jit(solution)/shard_map/psum | solution.py:270
  2306.7 419.3 %all-reduce.9.cloned.1.call-start = ((), (), s32[]{:S(2)}) async-start(), calls=%async_computation.20 | async-start | bytes 262144 | tf_op jit(solution)/shard_map/psum | solution.py:274
  2310.0 778.1 %reduce-scatter.17.cloned.1.call-start = ((), (), s32[]{:S(2)}) async-start(), calls=%async_computation.19 | async-start | bytes 17301504 | tf_op jit(solution)/shard_map/reduce_scatter | solution.py:267
  2319.7 1133.4 %reduce-scatter.15.cloned.1.call-start = ((), (), s32[]{:S(2)}) async-start(), calls=%async_computation.18 | async-start | bytes 17301504 | tf_op jit(solution)/shard_map/reduce_scatter | solution.py:266
  2331.1 1487.0 %reduce-scatter.11.cloned.1.call-start = ((), (), s32[]{:S(2)}) async-start(), calls=%async_computation.16 | async-start | bytes 17301504 | tf_op jit(solution)/shard_map/reduce_scatter | solution.py:264
  2373.2 1809.8 %reduce-scatter.13.cloned.1.call-start = ((), (), s32[]{:S(2)}) async-start(), calls=%async_computation.17 | async-start | bytes 17301504 | tf_op jit(solution)/shard_map/reduce_scatter | solution.py:265
  (84 other events, 1776.7 us)
Sparse Core Ops, SparseCore 0:
  11.0 78.5 all-gather.10
  92.5 75.9 all-gather.12
  171.4 75.8 all-gather.6
  249.3 44.8 all-gather.14
  296.2 46.3 all-gather.8
  345.4 77.4 all-gather.16
  2156.9 59.7 reduce-scatter.20
  2241.5 59.8 reduce-scatter.18
  2306.8 290.7 all-reduce.10
  2603.5 122.4 all-reduce.8
  2728.8 359.2 reduce-scatter.16
  3090.9 362.1 reduce-scatter.14
  3455.9 362.1 reduce-scatter.10
  3820.9 362.1 reduce-scatter.12
where the time goes:
time: 4200 us; the launch traced here: 4190 us
  waiting for transfers between devices  2630 us (63%)
  blocking collectives  732 us (17%)
  matrix products  493 us (12%)
  local copies, waits for them, and re-layouts  163 us (4%)
  other arithmetic  142 us (3%)
    all_to_all x2, blocking collectives, route_tokens(): lax.all_to_all(blocks, ('ctx', 'exp'), split_axis=0, concat_axis=0, tiled...  692 us
    all_to_all x2, waiting for transfers between devices, route_tokens(): lax.all_to_all(blocks, ('ctx', 'exp'), split_axis=0, concat_axis=0, tiled...  671 us
    reduce_scatter x1, waiting for transfers between devices, per_device(): lax.psum_scatter(query_grad, ('dp', 'ctx', 'exp'), scatter_dimension=0, t...  365 us
    reduce_scatter x1, waiting for transfers between devices, per_device(): lax.psum_scatter(value_grad, ('dp', 'ctx', 'exp'), scatter_dimension=0, t...  365 us
    reduce_scatter x1, waiting for transfers between devices, per_device(): lax.psum_scatter(key_grad, ('dp', 'ctx', 'exp'), scatter_dimension=0, til...  365 us
    reduce_scatter x1, waiting for transfers between devices, per_device(): lax.psum_scatter(output_grad, ('dp', 'ctx', 'exp'), scatter_dimension=0,...  362 us
    psum x1, waiting for transfers between devices, per_device(): lax.psum(gate_grad.astype(jnp.bfloat16), 'dp').astype(jnp.float32)  193 us
    dot_general x8, matrix products, contract_cols(): lax.dot_general(left, right, (((1,), (1,)), ((), ())), preferred_element_...  111 us
  transfers between devices with their start and end apart: 16, of which 13 were waited for; matrix products, arithmetic and copies ran while one was open for 10% of the time, Pallas kernels for 0%

commit v1 on v0

v1 whole, which is shorter than its diff:
```python
import jax
import jax.numpy as jnp
from jax import lax
from jax.sharding import PartitionSpec as P

HEAD = 128
PROMPT = 512
EPS = 1e-05
THETA = 10000.0
MASKED = -1e30
BF = jnp.bfloat16
F32 = jnp.float32
ALL = ("dp", "ctx", "exp")
MOE = ("ctx", "exp")
ROWS = ("dp", "exp")


def dot_nn(a, b):
    return lax.dot_general(a, b, (((1,), (0,)), ((), ())), preferred_element_type=F32)


def dot_tn(a, b):
    return lax.dot_general(a, b, (((0,), (0,)), ((), ())), preferred_element_type=F32)


def dot_nt(a, b):
    return lax.dot_general(a, b, (((1,), (1,)), ((), ())), preferred_element_type=F32)


def rope(v, cos, sin, sign):
    rows, width = v.shape
    half = HEAD // 2
    v = v.reshape(rows, width // HEAD, HEAD)
    a, b = v[..., :half], v[..., half:]
    c, s = cos[:, None, :], sin[:, None, :] * sign
    return jnp.concatenate([a * c - b * s, b * c + a * s], axis=-1).reshape(rows, width)


def per_device(
    hidden_in,
    segments,
    routes,
    attn_gain,
    query_weight,
    key_weight,
    value_weight,
    query_gain,
    key_gain,
    output_weight,
    ffn_gain,
    router_weight,
    gate_weight,
    up_weight,
    down_weight,
    cotangent,
):
    n_dp, n_ctx, n_exp = (lax.axis_size(a) for a in ALL)
    tok, width = hidden_in.shape[2:]
    topk = routes.shape[3]
    experts = n_ctx * n_exp
    cap = (5 * tok * topk + 4 * experts - 1) // (4 * experts)
    group = segments.shape[2]
    shard = query_weight.shape[0]
    cols = width // n_ctx
    piece = cols // n_dp
    heads = cols // HEAD
    scale = HEAD**-0.5
    ctx_me = lax.axis_index("ctx")
    exp_me = lax.axis_index("exp")
    expert_me = ctx_me * n_exp + exp_me

    def own_cols(vec):
        return lax.dynamic_index_in_dim(
            vec.reshape(n_dp, n_ctx, piece), ctx_me, 1, keepdims=False
        ).reshape(cols)

    packed = jnp.stack([query_weight, key_weight, value_weight], axis=1)
    packed = packed.reshape(shard, 3, n_dp, n_ctx, piece).transpose(3, 0, 1, 2, 4)
    packed = lax.all_to_all(packed, "ctx", split_axis=0, concat_axis=0, tiled=True)
    packed = packed.reshape(n_ctx * shard, 3 * cols)
    qkv_w = lax.all_gather(packed, ROWS, axis=0, tiled=True)
    qkv_w = (
        qkv_w.reshape(n_dp, n_exp, n_ctx, shard, 3 * cols)
        .transpose(0, 2, 1, 3, 4)
        .reshape(width, 3 * cols)
    )
    out_w = lax.all_gather(output_weight, ROWS, axis=0, tiled=True)

    own_routes = routes[0, 0]
    expert_ids = jnp.arange(experts, dtype=jnp.int32)
    hits = jnp.sum((own_routes[:, :, None] == expert_ids).astype(jnp.int32), axis=1)
    tokens = jnp.arange(tok, dtype=jnp.int32)
    lower = (tokens[:, None] > tokens[None, :]).astype(BF)
    earlier = dot_nn(lower, hits.astype(BF)).astype(jnp.int32)
    slot_local = jnp.where(hits > 0, earlier, -1).T
    slot = lax.all_to_all(slot_local, MOE, split_axis=0, concat_axis=0, tiled=True)
    pick = (
        slot[:, None, :] == jnp.arange(cap, dtype=jnp.int32)[None, :, None]
    )

    hidden = hidden_in[0, 0].astype(F32)
    labels = segments[0, 0]
    index = jnp.arange(group, dtype=jnp.int32)
    before = jnp.sum((labels[None, :] < labels[:, None]).astype(jnp.int32), axis=1)
    positions = index - before + jnp.where(labels > 0, PROMPT, 0).astype(jnp.int32)
    half = HEAD // 2
    frequency = THETA ** (-(jnp.arange(half, dtype=F32) * 2.0 / HEAD))
    angles = positions.astype(F32)[:, None] * frequency[None, :]
    cos, sin = jnp.cos(angles), jnp.sin(angles)
    attn_gain_f = attn_gain.astype(F32)
    ffn_gain_f = ffn_gain.astype(F32)
    q_gain = own_cols(query_gain.astype(F32))
    k_gain = own_cols(key_gain.astype(F32))

    attn_r = lax.rsqrt(jnp.mean(hidden * hidden, axis=-1, keepdims=True) + EPS)
    normed = (hidden * attn_r * attn_gain_f).astype(BF)
    normed_g = lax.all_gather(normed, "ctx", axis=0, tiled=True)
    raw = dot_nn(normed_g, qkv_w)
    q_raw, k_raw, v_raw = raw[:, :cols], raw[:, cols : 2 * cols], raw[:, 2 * cols :]
    squares = lax.psum(
        jnp.stack([jnp.sum(q_raw * q_raw, axis=1), jnp.sum(k_raw * k_raw, axis=1)]), "ctx"
    )
    inv = lax.rsqrt(squares / width + EPS)
    q_r, k_r = inv[0][:, None], inv[1][:, None]
    q_rot = rope(q_raw * q_r * q_gain, cos, sin, 1.0).astype(BF)
    k_rot = rope(k_raw * k_r * k_gain, cos, sin, 1.0).astype(BF)
    v_low = v_raw.astype(BF)
    q_h, k_h, v_h = (x.reshape(group, heads, HEAD) for x in (q_rot, k_rot, v_low))
    allowed = (index[None, :] <= index[:, None]) & (
        (labels[None, :] == 0) | (labels[None, :] == labels[:, None])
    )
    scores = jnp.einsum("qhd,khd->hqk", q_h, k_h, preferred_element_type=F32) * scale
    prob = jax.nn.softmax(jnp.where(allowed[None], scores, MASKED), axis=-1)
    prob_low = prob.astype(BF)
    mix = (
        jnp.einsum("hqk,khd->qhd", prob_low, v_h, preferred_element_type=F32)
        .reshape(group, cols)
        .astype(BF)
    )
    branch = lax.psum_scatter(
        dot_nn(mix, out_w).astype(BF), "ctx", scatter_dimension=0, tiled=True
    )
    residual = hidden + branch.astype(F32)

    ffn_r = lax.rsqrt(jnp.mean(residual * residual, axis=-1, keepdims=True) + EPS)
    ffn_normed = (residual * ffn_r * ffn_gain_f).astype(BF)
    logits = dot_nn(ffn_normed, router_weight)
    router_prob = jax.nn.softmax(logits, axis=-1)
    gates = jnp.where(hits > 0, router_prob, 0.0).astype(BF)
    rows_all = lax.all_gather(ffn_normed, MOE, axis=0, tiled=False)
    gate_at = lax.all_to_all(gates.T, MOE, split_axis=0, concat_axis=0, tiled=True)
    cot = cotangent[0, 0]
    cot_all = lax.all_gather(cot, MOE, axis=0, tiled=False)

    pick_low = pick.astype(BF)
    combine = jnp.where(pick, gate_at[:, None, :], jnp.zeros((), BF))
    gate_row = jnp.sum(jnp.where(pick, gate_at[:, None, :].astype(F32), 0.0), axis=2)

    def pick_rows(x):
        return lax.dot_general(
            pick_low, x, (((2,), (1,)), ((0,), (0,))), preferred_element_type=F32
        )

    def place_rows(table, x):
        return lax.dot_general(
            table, x, (((1,), (1,)), ((0,), (0,))), preferred_element_type=F32
        )

    total = experts * cap
    received = pick_rows(rows_all).astype(BF).reshape(total, width)
    gate_mat, up_mat, down_mat = gate_weight[0], up_weight[0], down_weight[0]
    gate_pre = dot_nn(received, gate_mat)
    up_pre = dot_nn(received, up_mat)
    sig = jax.nn.sigmoid(gate_pre)
    silu = gate_pre * sig
    expert_hidden = (silu * up_pre).astype(BF)
    expert_out = dot_nn(expert_hidden, down_mat).astype(BF)
    moe_part = place_rows(combine, expert_out.reshape(experts, cap, width)).astype(BF)
    moe_out = lax.psum_scatter(
        moe_part.reshape(experts * tok, width), MOE, scatter_dimension=0, tiled=True
    )
    output = (residual + moe_out.astype(F32)).astype(BF)

    cot_rows = pick_rows(cot_all)
    d_out = (cot_rows * gate_row[:, :, None]).astype(BF).reshape(total, width)
    d_gate_rows = jnp.sum(cot_rows * expert_out.reshape(experts, cap, width).astype(F32), axis=2)
    d_gate_at = jnp.sum(jnp.where(pick, d_gate_rows[:, :, None], 0.0), axis=1)
    d_gate = lax.all_to_all(d_gate_at, MOE, split_axis=0, concat_axis=0, tiled=True).T
    d_hidden_e = dot_nt(d_out, down_mat)
    d_gate_pre = (d_hidden_e * up_pre * sig * (1.0 + gate_pre * (1.0 - sig))).astype(BF)
    d_up_pre = (d_hidden_e * silu).astype(BF)
    d_disp = (dot_nt(d_gate_pre, gate_mat) + dot_nt(d_up_pre, up_mat)).astype(BF)
    d_part = place_rows(pick_low, d_disp.reshape(experts, cap, width)).astype(BF)
    d_tokens = lax.psum_scatter(
        d_part.reshape(experts * tok, width), MOE, scatter_dimension=0, tiled=True
    )
    down_grad = dot_tn(expert_hidden, d_out)
    gate_grad = dot_tn(received, d_gate_pre)
    up_grad = dot_tn(received, d_up_pre)
    gate_sum, up_sum, down_sum = (
        lax.psum(g.astype(BF), "dp").astype(F32) for g in (gate_grad, up_grad, down_grad)
    )

    d_router = d_gate
    d_logits = (
        router_prob * (d_router - jnp.sum(router_prob * d_router, axis=-1, keepdims=True))
    ).astype(BF)
    router_grad = dot_tn(d_logits, ffn_normed)
    d_ffn = d_tokens.astype(F32) + dot_nt(d_logits, router_weight)
    ffn_gain_grad = jnp.sum(d_ffn * residual * ffn_r, axis=0)
    weighted = d_ffn * ffn_gain_f
    d_residual = cot.astype(F32) + (
        weighted * ffn_r
        - residual * ffn_r**3 * jnp.mean(residual * weighted, axis=-1, keepdims=True)
    )
    d_branch = d_residual.astype(BF)

    d_branch_g = lax.all_gather(d_branch, "ctx", axis=0, tiled=True)
    out_grad = dot_tn(mix, d_branch_g)
    d_mix_h = dot_nt(d_branch_g, out_w).astype(BF).reshape(group, heads, HEAD)
    d_prob = jnp.einsum("qhd,khd->hqk", d_mix_h, v_h, preferred_element_type=F32)
    row_total = jnp.sum(prob * d_prob, axis=-1, keepdims=True)
    d_scores = (prob * (d_prob - row_total)).astype(BF)
    d_q = jnp.einsum("hqk,khd->qhd", d_scores, k_h, preferred_element_type=F32)
    d_k = jnp.einsum("hqk,qhd->khd", d_scores, q_h, preferred_element_type=F32)
    d_v = jnp.einsum("hqk,qhd->khd", prob_low, d_mix_h, preferred_element_type=F32)
    d_qn = rope(d_q.reshape(group, cols) * scale, cos, sin, -1.0)
    d_kn = rope(d_k.reshape(group, cols) * scale, cos, sin, -1.0)
    q_gain_part = jnp.sum(d_qn * q_raw * q_r, axis=0)
    k_gain_part = jnp.sum(d_kn * k_raw * k_r, axis=0)
    d_qw, d_kw = d_qn * q_gain, d_kn * k_gain
    dots = (
        lax.psum(jnp.stack([jnp.sum(q_raw * d_qw, axis=1), jnp.sum(k_raw * d_kw, axis=1)]), "ctx")
        / width
    )
    d_q_raw = d_qw * q_r - q_raw * q_r**3 * dots[0][:, None]
    d_k_raw = d_kw * k_r - k_raw * k_r**3 * dots[1][:, None]
    d_raw = jnp.concatenate(
        [d_q_raw.astype(BF), d_k_raw.astype(BF), d_v.reshape(group, cols).astype(BF)], axis=1
    )
    d_normed = lax.psum_scatter(
        dot_nt(d_raw, qkv_w).astype(BF), "ctx", scatter_dimension=0, tiled=True
    ).astype(F32)
    attn_gain_grad = jnp.sum(d_normed * hidden * attn_r, axis=0)
    weighted = d_normed * attn_gain_f
    hidden_grad = (
        d_residual
        + weighted * attn_r
        - hidden * attn_r**3 * jnp.mean(hidden * weighted, axis=-1, keepdims=True)
    ).astype(BF)

    qkv_grad = dot_tn(normed_g, d_raw).astype(BF)
    qkv_grad = (
        qkv_grad.reshape(n_dp, n_ctx, n_exp, shard, 3 * cols)
        .transpose(0, 2, 1, 3, 4)
        .reshape(width, 3 * cols)
    )
    qkv_sum = lax.psum_scatter(qkv_grad, ROWS, scatter_dimension=0, tiled=True)
    qkv_sum = lax.all_to_all(
        qkv_sum.reshape(n_ctx, shard, 3, n_dp, piece), "ctx", split_axis=0, concat_axis=0, tiled=True
    )
    qkv_sum = qkv_sum.transpose(2, 1, 3, 0, 4).reshape(3, shard, width).astype(F32)
    out_sum = lax.psum_scatter(
        out_grad.astype(BF), ROWS, scatter_dimension=0, tiled=True
    ).astype(F32)

    spread = jnp.zeros((2, n_dp, n_ctx, piece), F32)
    spread = lax.dynamic_update_slice(
        spread,
        jnp.stack([q_gain_part, k_gain_part]).reshape(2, n_dp, 1, piece),
        (0, 0, ctx_me, 0),
    ).reshape(2, width)
    early = lax.psum(jnp.concatenate([router_grad, ffn_gain_grad[None]], axis=0), ALL)
    late = lax.psum(jnp.concatenate([spread, attn_gain_grad[None]], axis=0), ALL)
    return (
        output[None, None],
        hidden_grad[None, None],
        late[2],
        qkv_sum[0],
        qkv_sum[1],
        qkv_sum[2],
        late[0],
        late[1],
        out_sum,
        early[experts],
        early[:experts].T,
        gate_sum[None],
        up_sum[None],
        down_sum[None],
    )


def solution(mesh):
    tokens = P("dp", "exp", "ctx", None)
    rows = P(ALL, None)
    expert = P(MOE, None, None)
    return jax.shard_map(
        per_device,
        mesh=mesh,
        in_specs=(
            tokens,
            P("dp", "exp", None),
            tokens,
            P(),
            rows,
            rows,
            rows,
            P(),
            P(),
            rows,
            P(),
            P(),
            expert,
            expert,
            expert,
            tokens,
        ),
        out_specs=(
            tokens,
            tokens,
            P(),
            rows,
            rows,
            rows,
            P(),
            P(),
            rows,
            P(),
            P(),
            expert,
            expert,
            expert,
        ),
        check_vma=False,
    )
```

time: 4200 us -> 2070 us (0.49)
  waiting for transfers between devices: 2630 us -> 1270 us
  blocking collectives: 732 us -> 89.2 us
  local copies, waits for them, and re-layouts: 163 us -> 65.1 us
    reduce_scatter x4 -> x6, waiting for transfers between devices: 1460 us -> 774 us  [the longest x1 244 us: per_device(): lax.psum_scatter(moe_part.reshape(experts * tok, width), MOE, scatter_dim...]
    all_to_all x2, blocking collectives: 692 us -> 24.6 us  [the longest x1 14.2 us: per_device(): lax.all_to_all(packed, 'ctx', split_axis=0, concat_axis=0, tiled=True)]
    all_to_all x2 -> x3, waiting for transfers between devices: 671 us -> 6.43 us  [the longest x1 5.02 us: per_device(): lax.all_to_all(gates.T, MOE, split_axis=0, concat_axis=0, tiled=True)]
    gather x12 -> x0, local copies, waits for them, and re-layouts: 95.9 us -> none  [the longest x4 44.1 us: per_device(): d_gate = jnp.take_along_axis(gate_scores, flat_slot, axis=1)]
    dot_general x35 -> x28, matrix products: 472 us -> 454 us  [the longest x6 109 us: dot_nt(): lax.dot_general(a, b, (((1,), (1,)), ((), ())), preferred_element_type=F32)]
  transfers between devices with their start and end apart: 16 -> 17, of which waited for: 13 -> 14; matrix products, arithmetic and copies ran while one was open for 10% -> 24% of each run, Pallas kernels for 0% -> 0%
where the time goes in v1:
time: 2070 us
  waiting for transfers between devices  1270 us (61%)
  matrix products  479 us (23%)
  other arithmetic  136 us (7%)
  blocking collectives  89.2 us (4%)
  local copies, waits for them, and re-layouts  65.1 us (3%)
    reduce_scatter x1, waiting for transfers between devices, per_device(): lax.psum_scatter(moe_part.reshape(experts * tok, width), MOE, scatter_dim...  244 us
    reduce_scatter x1, waiting for transfers between devices, per_device(): lax.psum_scatter(d_part.reshape(experts * tok, width), MOE, scatter_dimen...  232 us
    reduce_scatter x1, waiting for transfers between devices, per_device(): qkv_sum = lax.psum_scatter(qkv_grad, ROWS, scatter_dimension=0, tiled=True)  119 us
    psum x1, waiting for transfers between devices, per_device(): lax.psum(jnp.concatenate([router_grad, ffn_gain_grad[None]], axis=0), ALL)  116 us
    all_gather x1, waiting for transfers between devices, per_device(): rows_all = lax.all_gather(ffn_normed, MOE, axis=0, tiled=False)  115 us
    dot_general x6, matrix products, dot_nt(): lax.dot_general(a, b, (((1,), (1,)), ((), ())), preferred_element_type=F32)  109 us
    dot_general x7, matrix products, dot_nn(): lax.dot_general(a, b, (((1,), (0,)), ((), ())), preferred_element_type=F32)  98.3 us
    dot_general x6, matrix products, dot_tn(): lax.dot_general(a, b, (((0,), (0,)), ((), ())), preferred_element_type=F32)  85.9 us
  transfers between devices with their start and end apart: 17, of which 14 were waited for; matrix products, arithmetic and copies ran while one was open for 24% of the time, Pallas kernels for 0%

profile of v1, /device:TPU:8, one launch (start us, length us, event | category | flops | bytes accessed | tf_op | source)
XLA Modules:
  0.0 2067.8 jit_solution(11113607522126898722)
XLA Ops:
  41.7 84.3 %all-gather.11.cloned.1.call-done = bf16[2048,1536]{1,0:T(8,128)(2,1)} async-done(((bf16[256,1536]{1,0:T(8,128)(2,1)}), bf16[2048,1536]{1,0:T(8,128)(2,1)}) %all-gather.11.cloned.1.call-update) | async-done | bytes 6291472 | tf_op jit(solution)/shard_map/all_gather | solution.py:81
  132.1 42.1 %all-gather.9.cloned.1.call-done = bf16[1536,2048]{1,0:T(8,128)(2,1)} async-done(((bf16[384,2048]{1,0:T(8,128)(2,1)}), bf16[1536,2048]{1,0:T(8,128)(2,1)}) %all-gather.9.cloned.1.call-update) | async-done | bytes 6291472 | tf_op jit(solution)/shard_map/all_gather | solution.py:117
  236.0 25.3 %exponential_reduce_fusion = (f32[4,1536]{1,0:T(4,128)S(1)}, f32[4,1536,1536]{1,2,0:T(8,128)}) fusion(pred[1536,1536]{0,1:T(8,128)(4,1)} %fusion.10, bf16[1536,4,64]{2,0,1:T(8,128)(2,1)} %get-tuple-element.62, bf16[1536,4,64]{2,0,1:T(8,128)(2,1)} %get-tuple-element.63, bf16[1536,4,64]{2,0,1:T(8,128)(2,1)} %get-tuple-element.44, ...), kind=kOutput, calls=%fused_computation.7 | convolution fusion | flops 2459960832 | bytes 43278336 | tf_op jit(solution)/shard_map/sub | solution.py:133
  286.3 58.4 %reduce-scatter.7.cloned.1.call-done = bf16[384,2048]{1,0:T(8,128)(2,1)} async-done(((bf16[1536,2048]{1,0:T(8,128)(2,1)}), bf16[384,2048]{1,0:T(8,128)(2,1)}) %reduce-scatter.7.cloned.1.call-update) | async-done | bytes 1572880 | tf_op jit(solution)/shard_map/reduce_scatter | solution.py:140
  372.2 114.6 %all-gather.17.cloned.1.call-done = bf16[6144,2048]{1,0:T(8,128)(2,1)} async-done(((bf16[384,2048]{1,0:T(8,128)(2,1)}), bf16[6144,2048]{1,0:T(8,128)(2,1)}) %all-gather.17.cloned.1.call-update) | async-done | bytes 25165840 | tf_op jit(solution)/shard_map/all_gather | solution.py:150
  525.5 29.6 %multiply_convert_fusion.4 = (bf16[3840,1024]{1,0:T(8,128)(2,1)}, f32[3840,1024]{1,0:T(8,128)}) fusion(f32[3840,1024]{1,0:T(8,128)} %fusion.20, bf16[3840,2048]{1,0:T(8,128)(2,1)} %bitcast.201, bf16[1,2048,1024]{2,1,0:T(8,128)(2,1)S(1)} %copy-done.72), kind=kOutput, calls=%fused_computation.15 | convolution fusion | flops 16129720320 | bytes 59244544 | tf_op jit(solution)/shard_map/dot_general | solution.py:19
  555.1 22.6 %convolution_convert_fusion = bf16[3840,2048]{1,0:T(8,128)(2,1)} fusion(bf16[3840,1024]{1,0:T(8,128)(2,1)} %get-tuple-element.76, bf16[1,1024,2048]{2,1,0:T(8,128)(2,1)S(1)} %copy-done.71), kind=kOutput, calls=%fused_computation.18 | convolution fusion | flops 16113991680 | bytes 27787264 | tf_op jit(solution)/shard_map/dot_general | solution.py:19
  577.7 46.2 %all-gather.19.cloned.1.call-done = bf16[16,1,384,2048]{3,2,1,0:T(8,128)(2,1)} async-done(((bf16[1,1,384,2048]{3,2,1,0:T(8,128)(2,1)}), bf16[16,1,384,2048]{3,2,1,0:T(8,128)(2,1)}) %all-gather.19.cloned.1.call-update) | async-done | bytes 25165840 | tf_op jit(solution)/shard_map/all_gather | solution.py:153
  623.9 27.5 %multiply_reduce_fusion.1 = (f32[16,240]{1,0:T(8,128)S(1)}, f32[16,240,2048]{2,1,0:T(8,128)}) fusion(bf16[16,240,2048]{2,1,0:T(8,128)(2,1)} %bitcast.197, bf16[16,1,384,2048]{3,2,1,0:T(8,128)(2,1)} %all-gather.19.cloned.1.call-done, s32[16,384]{1,0:T(8,128)S(1)} %bitcast.217), kind=kOutput, calls=%fused_computation.8 | convolution fusion | flops 6064861184 | bytes 72391680 | tf_op jit(solution)/shard_map/dot_general | solution.py:160
  670.9 33.9 %multiply_convert_fusion.2 = (bf16[3840,1024]{1,0:T(8,128)(2,1)}, bf16[3840,1024]{1,0:T(8,128)(2,1)}) fusion(f32[3840,1024]{1,0:T(8,128)} %fusion.20, f32[3840,1024]{1,0:T(8,128)} %get-tuple-element.77, bf16[3840,2048]{1,0:T(8,128)(2,1)} %bitcast.208, bf16[1,1024,2048]{2,1,0:T(8,128)(2,1)} %param.30), kind=kOutput, calls=%fused_computation.13 | convolution fusion | flops 16157245440 | bytes 67108864 | tf_op jit(solution)/shard_map/dot_general | solution.py:27
  704.8 24.2 %fusion.18 = f32[3840,2048]{1,0:T(8,128)} fusion(bf16[3840,1024]{1,0:T(8,128)(2,1)} %get-tuple-element.38, bf16[1,2048,1024]{2,1,0:T(8,128)(2,1)} %param.28), kind=kOutput, calls=%fused_computation.49 | convolution fusion | flops 16106127360 | bytes 43515904 | tf_op jit(solution)/shard_map/dot_general | solution.py:27
  729.1 26.2 %add_convert_fusion = bf16[3840,2048]{1,0:T(8,128)(2,1)} fusion(f32[3840,2048]{1,0:T(8,128)} %fusion.18, bf16[3840,1024]{1,0:T(8,128)(2,1)} %get-tuple-element.37, bf16[1,2048,1024]{2,1,0:T(8,128)(2,1)} %param.29), kind=kOutput, calls=%fused_computation.9 | convolution fusion | flops 16121856000 | bytes 59244544 | tf_op jit(solution)/shard_map/dot_general | solution.py:27
  782.7 231.6 %reduce-scatter.11.cloned.1.call-done = bf16[384,2048]{1,0:T(8,128)(2,1)} async-done(((bf16[6144,2048]{1,0:T(8,128)(2,1)}), bf16[384,2048]{1,0:T(8,128)(2,1)}) %reduce-scatter.11.cloned.1.call-update) | async-done | bytes 1572880 | tf_op jit(solution)/shard_map/reduce_scatter | solution.py:194
  1021.5 22.7 %convert_bitcast_fusion = bf16[1,1024,2048]{2,1,0:T(8,128)(2,1)} fusion(bf16[3840,1024]{1,0:T(8,128)(2,1)} %get-tuple-element.76, bf16[3840,2048]{1,0:T(8,128)(2,1)} %bitcast.209), kind=kOutput, calls=%fused_computation.53 | convolution fusion | flops 16108224512 | bytes 27787264 | tf_op jit(solution)/shard_map/dot_general | solution.py:23
  1044.2 22.6 %convert_bitcast_fusion.1 = bf16[1,2048,1024]{2,1,0:T(8,128)(2,1)} fusion(bf16[3840,2048]{1,0:T(8,128)(2,1)} %bitcast.202, bf16[3840,1024]{1,0:T(8,128)(2,1)} %get-tuple-element.37), kind=kOutput, calls=%fused_computation.54 | convolution fusion | flops 16108224512 | bytes 27787264 | tf_op jit(solution)/shard_map/dot_general | solution.py:23
  1095.9 28.7 %multiply_reduce_fusion = (f32[4,1536]{1,0:T(4,128)S(1)}, f32[4,1536,1536]{1,2,0:T(8,128)}) fusion(f32[4,1536]{1,0:T(4,128)S(1)} %copy-done.59, f32[4,1536,1536]{1,2,0:T(8,128)} %get-tuple-element.75, bf16[1536,4,128]{0,2,1:T(8,128)(2,1)S(1)} %bitcast.242, bf16[1536,4,128]{0,2,1:T(8,128)(2,1)S(1)} %bitcast.222), kind=kOutput, calls=%fused_computation.5 | convolution fusion | flops 2444224512 | bytes 78692352 | tf_op jit(solution)/shard_map/qhd,khd->hqk/dot_general | solution.py:221
  1124.7 32.4 %multiply_convert_fusion = bf16[4,1536,1536]{1,2,0:T(8,128)(2,1)} fusion(f32[4,1536,1536]{1,2,0:T(8,128)} %get-tuple-element.84, f32[4,1536]{1,0:T(4,128)S(1)} %get-tuple-element.83, f32[4,1536]{1,0:T(4,128)S(1)} %copy-done.59, f32[4,1536,1536]{1,2,0:T(8,128)} %get-tuple-element.75), kind=kLoop, calls=%fused_computation.4 | loop fusion | flops 37748736 | bytes 94420992 | tf_op jit(solution)/shard_map/convert_element_type | solution.py:223
  1293.6 83.3 %all-reduce.6.cloned.1.call-done = (bf16[1,2048,1024]{2,1,0:T(8,128)(2,1)}, bf16[1,2048,1024]{2,1,0:T(8,128)(2,1)}, bf16[1,1024,2048]{2,1,0:T(8,128)(2,1)}) async-done(((bf16[1,2048,1024]{2,1,0:T(8,128)(2,1)}, bf16[1,2048,1024]{2,1,0:T(8,128)(2,1)}, bf16[1,1024,2048]{2,1,0:T(8,128)(2,1)}), (bf16[1,2048,1024]{2,1,0:T(8,128)(2,1)}, bf16[1,2048,1024]{2,1,0:T(8,128)(2,1)}, ...) | async-done | bytes 12582928 | tf_op jit(solution)/shard_map/psum | solution.py:201
  1392.6 116.0 %all-reduce.4.cloned.1.call-done = f32[17,2048]{1,0:T(8,128)} async-done(((f32[17,2048]{1,0:T(8,128)}), f32[17,2048]{1,0:T(8,128)}) %all-reduce.4.cloned.1.call-update) | async-done | bytes 139280 | tf_op jit(solution)/shard_map/psum | solution.py:273
  1511.7 67.2 %reduce-scatter.17.cloned.1.call-done = bf16[64,2048]{1,0:T(8,128)(2,1)} async-done(((bf16[512,2048]{1,0:T(8,128)(2,1)}), bf16[64,2048]{1,0:T(8,128)(2,1)}) %reduce-scatter.17.cloned.1.call-update) | async-done | bytes 262160 | tf_op jit(solution)/shard_map/reduce_scatter | solution.py:263
  1580.7 118.9 %reduce-scatter.15.cloned.1.call-done = bf16[256,1536]{1,0:T(8,128)(2,1)} async-done(((bf16[2048,1536]{1,0:T(8,128)(2,1)}), bf16[256,1536]{1,0:T(8,128)(2,1)}) %reduce-scatter.15.cloned.1.call-update) | async-done | bytes 786448 | tf_op jit(solution)/shard_map/reduce_scatter | solution.py:258
  1706.7 53.9 %reduce-scatter.13.cloned.1.call-done = bf16[384,2048]{1,0:T(8,128)(2,1)} async-done(((bf16[1536,2048]{1,0:T(8,128)(2,1)}), bf16[384,2048]{1,0:T(8,128)(2,1)}) %reduce-scatter.13.cloned.1.call-update) | async-done | bytes 1572880 | tf_op jit(solution)/shard_map/reduce_scatter | solution.py:241
  1763.0 243.6 %reduce-scatter.9.cloned.1.call-done = bf16[384,2048]{1,0:T(8,128)(2,1)} async-done(((bf16[6144,2048]{1,0:T(8,128)(2,1)}), bf16[384,2048]{1,0:T(8,128)(2,1)}) %reduce-scatter.9.cloned.1.call-update) | async-done | bytes 1572880 | tf_op jit(solution)/shard_map/reduce_scatter | solution.py:179
  2012.5 41.4 %psum.51 = f32[3,2048]{1,0:T(4,128)S(1)} all-reduce(f32[3,2048]{1,0:T(4,128)S(1)} %pad_maximum_fusion.8), channel_id=1, replica_groups=mesh['dp'=2,'ctx'=4,'exp'=4] {'dp','ctx','exp'}, use_global_device_ids=true, to_apply=%region_28.29 | all-reduce | flops 6144 | bytes 49152 | tf_op jit(solution)/shard_map/psum | solution.py:274
  (322 shorter events, 455.2 us)
Async XLA Ops:
  7.2 118.8 %all-gather.11.cloned.1.call-start = ((), (), s32[]{:S(2)}) async-start(), calls=%async_computation.12 | async-start | bytes 7077888 | tf_op jit(solution)/shard_map/all_gather | solution.py:81
  28.0 146.2 %all-gather.9.cloned.1.call-start = ((), (), s32[]{:S(2)}) async-start(), calls=%async_computation.11 | async-start | bytes 7864320 | tf_op jit(solution)/shard_map/all_gather | solution.py:117
  31.3 246.1 %all-gather.13.cloned.1.call-start = ((), (), s32[]{:S(2)}) async-start(), calls=%async_computation.13 | async-start | bytes 2359296 | tf_op jit(solution)/shard_map/all_gather | solution.py:87
  32.0 312.7 %reduce-scatter.7.cloned.1.call-start = ((), (), s32[]{:S(2)}) async-start(), calls=%async_computation.14 | async-start | bytes 7864320 | tf_op jit(solution)/shard_map/reduce_scatter | solution.py:140
  285.7 201.1 %all-gather.17.cloned.1.call-start = ((), (), s32[]{:S(2)}) async-start(), calls=%async_computation.22 | async-start | bytes 26738688 | tf_op jit(solution)/shard_map/all_gather | solution.py:150
  350.0 273.9 %all-gather.19.cloned.1.call-start = ((), (), s32[]{:S(2)}) async-start(), calls=%async_computation.23 | async-start | bytes 26738688 | tf_op jit(solution)/shard_map/all_gather | solution.py:153
  351.4 10.2 all-to-all-start.1
  361.6 9.9 all-to-all-start.2
  366.4 647.9 %reduce-scatter.11.cloned.1.call-start = ((), (), s32[]{:S(2)}) async-start(), calls=%async_computation.16 | async-start | bytes 26738688 | tf_op jit(solution)/shard_map/reduce_scatter | solution.py:194
  366.5 388.8 %copy-start.18 = (s32[16,1,384]{2,0,1:T(8,128)}, s32[16,1,384]{2,0,1:T(8,128)S(1)}, u32[]{:S(2)}) copy-start(s32[16,1,384]{2,0,1:T(8,128)S(1)} %copy.201) | copy-start | bytes 73732
  772.2 316.7 %all-gather.15.cloned.1.call-start = ((), (), s32[]{:S(2)}) async-start(), calls=%async_computation.17 | async-start | bytes 7864320 | tf_op jit(solution)/shard_map/all_gather | solution.py:218
  1021.4 355.5 %all-reduce.6.cloned.1.call-start = ((), (), s32[]{:S(2)}) async-start(), calls=%async_computation.24 | async-start | bytes 25165824 | tf_op jit(solution)/shard_map/psum | solution.py:201
  1086.4 422.2 %all-reduce.4.cloned.1.call-start = ((), (), s32[]{:S(2)}) async-start(), calls=%async_computation.21 | async-start | bytes 393216 | tf_op jit(solution)/shard_map/psum | solution.py:273
  1088.9 490.1 %reduce-scatter.17.cloned.1.call-start = ((), (), s32[]{:S(2)}) async-start(), calls=%async_computation.20 | async-start | bytes 2359296 | tf_op jit(solution)/shard_map/reduce_scatter | solution.py:263
  1220.0 479.7 %reduce-scatter.15.cloned.1.call-start = ((), (), s32[]{:S(2)}) async-start(), calls=%async_computation.19 | async-start | bytes 7077888 | tf_op jit(solution)/shard_map/reduce_scatter | solution.py:258
  1259.1 501.5 %reduce-scatter.13.cloned.1.call-start = ((), (), s32[]{:S(2)}) async-start(), calls=%async_computation.18 | async-start | bytes 7864320 | tf_op jit(solution)/shard_map/reduce_scatter | solution.py:241
  1275.5 731.1 %reduce-scatter.9.cloned.1.call-start = ((), (), s32[]{:S(2)}) async-start(), calls=%async_computation.15 | async-start | bytes 26738688 | tf_op jit(solution)/shard_map/reduce_scatter | solution.py:179
  1580.7 425.9 %copy-start.10 = (bf16[384,2048]{1,0:T(8,128)(2,1)S(1)}, bf16[384,2048]{1,0:T(8,128)(2,1)}, u32[]{:S(2)}) copy-start(bf16[384,2048]{1,0:T(8,128)(2,1)} %reduce-scatter.7.cloned.1.call-done) | copy-start | bytes 4718596
  1580.7 425.9 %copy-start.42 = (f32[2048]{0:T(1024)S(1)}, f32[2048]{0:T(1024)}, u32[]{:S(2)}) copy-start(f32[2048]{0:T(1024)} %copy-done.40) | copy-start | bytes 24580
  1580.7 425.9 %copy-start.53 = (f32[384]{0:T(512)S(1)}, f32[384]{0:T(512)}, u32[]{:S(2)}) copy-start(f32[384]{0:T(512)} %copy-done.51) | copy-start | bytes 4612
  1580.7 425.9 %copy-start.61 = (f32[384]{0:T(512)S(1)}, f32[384]{0:T(512)}, u32[]{:S(2)}) copy-start(f32[384]{0:T(512)} %get-tuple-element.72) | copy-start | bytes 4612
  1580.7 425.9 %copy-start.63 = (f32[384]{0:T(512)S(1)}, f32[384]{0:T(512)}, u32[]{:S(2)}) copy-start(f32[384]{0:T(512)} %copy-done.62) | copy-start | bytes 4612
  1580.7 425.9 %copy-start.65 = (f32[384]{0:T(512)S(1)}, f32[384]{0:T(512)}, u32[]{:S(2)}) copy-start(f32[384]{0:T(512)} %get-tuple-element.70) | copy-start | bytes 4612
  1702.5 352.0 %all-to-all-start.4 = ((bf16[4,64,3,2,256]{4,3,2,1,0:T(2,128)(2,1)}), bf16[4,64,3,2,256]{4,3,2,1,0:T(2,128)(2,1)}, u32[]{:S(2)}, u32[]{:S(2)}) async-start(bf16[4,64,3,2,256]{4,3,2,1,0:T(2,128)(2,1)} %reshape.409), calls=%async_computation.9 | async-start | bytes 1572864 | tf_op jit(solution)/shard_map/all_to_all | solution.py:259
  (75 other events, 3911.5 us)
Sparse Core Ops, SparseCore 0:
  28.2 97.8 all-gather.10
  128.2 45.9 all-gather.8
  176.3 49.2 all-gather.12
  285.8 58.8 reduce-scatter.6
  350.1 136.6 all-gather.16
  488.3 135.5 all-gather.18
  772.3 241.9 reduce-scatter.10
  1021.6 47.3 all-gather.14
  1086.5 290.3 all-reduce.5
  1383.8 124.7 all-reduce.3
  1512.5 66.3 reduce-scatter.16
  1582.8 116.8 reduce-scatter.14
  1702.3 58.2 reduce-scatter.12
  1764.6 241.9 reduce-scatter.8

commit v2 on v1

v2 whole, which is shorter than its diff:
```python
import functools

import jax
import jax.numpy as jnp
from jax import lax
from jax.experimental import pallas as pl
from jax.experimental.pallas import tpu as pltpu
from jax.sharding import PartitionSpec as P

HEAD = 128
PROMPT = 512
EPS = 1e-05
THETA = 10000.0
MASKED = -1e30
BF = jnp.bfloat16
F32 = jnp.float32
ALL = ("dp", "ctx", "exp")
MOE = ("ctx", "exp")
ROWS = ("dp", "exp")
MESH = pl.DeviceIdType.MESH


def by_distance(me, n):
    far=[jnp.abs(me-j)*n+j for j in range(n)]
    rank=[sum(((far[i]>far[j]).astype(jnp.int32) for i in range(n) if i!=j), jnp.int32(0)) for j in range(n)]
    def at(k):
        v=jnp.int32(0)
        for j in range(n): v=v+jnp.where(rank[j]==k,j,0)
        return v
    return at


def loop(n, body):
    def step(i,_):
        body(i)
        return 0
    lax.fori_loop(0,n,step,0)


def add_into(dst, src, rows=16):
    n=dst.shape[-2]//rows
    lead=dst.shape[:-2]
    assert not lead
    def body(i,_):
        sl=pl.ds(pl.multiple_of(i*rows,rows),rows)
        dst[sl,:]=(dst[sl,:].astype(F32)+src[sl,:].astype(F32)).astype(dst.dtype)
        return 0
    lax.fori_loop(0,n,body,0)


def add3(dst,src):
    if len(dst.shape)==2: add_into(dst,src); return
    def body(i,_):
        add_into(dst.at[i],src.at[i]); return 0
    lax.fori_loop(0,dst.shape[0],body,0)

def tail_kernel(N,C,E,gq,go,dn,oq,oo,od,own_q,own_o,own_d,yq,yo,uq,uo,vq,vo,d1,d2,ld,ldd,ys,yr,zs,zu,zd,s1,r1,s2,r2,a_s,a_r,osem):
    p=lax.axis_index("dp"); c=lax.axis_index("ctx"); e=lax.axis_index("exp")
    H=C//2; h=c//2; l=c%2
    def dpeer(j): return lax.rem(p+j,N)
    def cpeer(j): return lax.rem(c+j,C)
    def hpeer(j): return lax.rem(h+j,H)
    bar=pltpu.get_barrier_semaphore()
    def sig(**kw): pl.semaphore_signal(bar,inc=1,device_id=kw,device_id_type=MESH)
    for j in range(1,N): sig(dp=dpeer(j))
    for j in range(1,C): sig(ctx=cpeer(j))
    @pl.when(e>0)
    def _(): sig(exp=e-1)
    @pl.when(e<E-1)
    def _(): sig(exp=e+1)
    order=by_distance(e,E)
    def rc(src,dst,ss,rs,**kw): return pltpu.make_async_remote_copy(src,dst,ss,rs,device_id=kw,device_id_type=MESH)
    def loads(o): return [pltpu.make_async_copy(gq.at[p,:,o],own_q.at[o],ld.at[0,o]),pltpu.make_async_copy(go.at[p,o],own_o.at[o],ld.at[1,o])]
    def cy(j,o):
        q=dpeer(j)
        return [rc(gq.at[q,:,o],yq.at[j-1,o],ys.at[0,j-1,o],yr.at[0,j-1,o],dp=q), rc(go.at[q,o],yo.at[j-1,o],ys.at[1,j-1,o],yr.at[1,j-1,o],dp=q)]
    def cu(o): return [rc(own_q.at[o],uq.at[o],zs.at[0,o],zu.at[0,o],exp=e+1), rc(own_o.at[o],uo.at[o],zs.at[1,o],zu.at[1,o],exp=e+1)]
    def cd(o): return [rc(own_q.at[o],vq.at[o],zs.at[0,o],zd.at[0,o],exp=e-1), rc(own_o.at[o],vo.at[o],zs.at[1,o],zd.at[1,o],exp=e-1)]
    def loadd(hh): return pltpu.make_async_copy(dn.at[hh*2+l],own_d.at[hh],ldd.at[hh])
    def c1(hh): return rc(dn.at[hh*2+1-l],d1.at[hh],s1.at[hh],r1.at[hh],ctx=h*2+1-l)
    def c2(j):
        hh=hpeer(j); return rc(own_d.at[hh],d2.at[j-1],s2.at[j-1],r2.at[j-1],ctx=hh*2+l)
    hs=[hpeer(j) for j in range(1,H)]+[h]
    def start_loads(k):
        for x in loads(k): x.start()
    loop(E,start_loads)
    for hh in hs: loadd(hh).start()
    pl.semaphore_wait(bar,(N-1)+(C-1)+(e>0).astype(jnp.int32)+(e<E-1).astype(jnp.int32))
    for j in range(1,N):
        for x in cy(j,order(0)): x.start()
    for hh in hs: c1(hh).start()
    def start_dp(k):
        for j in range(1,N):
            for x in cy(j,order(k+1)): x.start()
    loop(E-1,start_dp)
    for i,hh in enumerate(hs):
        loadd(hh).wait(); c1(hh).wait_recv(); add_into(own_d.at[hh],d1.at[hh])
        if i<H-1: c2(i+1).start()
    def line(k):
        o=order(k)
        for x in loads(o): x.wait()
        for j in range(1,N):
            for x in cy(j,o): x.wait_recv()
            add3(own_q.at[o],yq.at[j-1,o]); add3(own_o.at[o],yo.at[j-1,o])
        if True:
            @pl.when(o>e)
            def _():
                @pl.when(e>0)
                def _():
                    for x in cu(o): x.wait_recv()
                    add3(own_q.at[o],uq.at[o]); add3(own_o.at[o],uo.at[o])
                for x in cu(o): x.start()
            @pl.when(o<e)
            def _():
                @pl.when(e<E-1)
                def _():
                    for x in cd(o): x.wait_recv()
                    add3(own_q.at[o],vq.at[o]); add3(own_o.at[o],vo.at[o])
                for x in cd(o): x.start()
    def lines(k):
        line(k)
        @pl.when(k==0)
        def _():
            for j in range(1,H):
                c2(j).wait_recv(); add_into(own_d.at[h],d2.at[j-1])
            pltpu.make_async_copy(own_d.at[h],od,osem.at[0]).start()
    loop(E,lines)
    @pl.when(e>0)
    def _():
        for x in cu(e): x.wait_recv()
        add3(own_q.at[e],uq.at[e]); add3(own_o.at[e],uo.at[e])
    @pl.when(e<E-1)
    def _():
        for x in cd(e): x.wait_recv()
        add3(own_q.at[e],vq.at[e]); add3(own_o.at[e],vo.at[e])
    def ca(j):
        q=cpeer(j); return rc(own_q.at[e,q],oq.at[c],a_s.at[j-1],a_r.at[j-1],ctx=q)
    for j in range(1,C): ca(j).start()
    l1=pltpu.make_async_copy(own_q.at[e,c],oq.at[c],osem.at[1]); l1.start()
    l2=pltpu.make_async_copy(own_o.at[e],oo,osem.at[2]); l2.start()
    def drain(k):
        for j in range(1,N):
            for x in cy(j,k): x.wait_send()
        @pl.when(k!=e)
        def _():
            for x in cu(k): x.wait_send()
    loop(E,drain)
    for hh in hs: c1(hh).wait_send()
    for j in range(1,H): c2(j).wait_send()
    for j in range(1,C):
        ca(j).wait_send();
        src=lax.rem(c+C-j,C)
        rc(own_q.at[e,c],oq.at[src],a_s.at[j-1],a_r.at[j-1],ctx=src).wait_recv()
    pltpu.make_async_copy(own_d.at[h],od,osem.at[0]).wait(); l1.wait(); l2.wait()

def tail(gq,go,dn,cid=2):
    N,C,E,S,W3=gq.shape; D=go.shape[-1]; T=dn.shape[1]; H=C//2
    dma=pltpu.SemaphoreType.DMA; V=lambda *s: pltpu.VMEM(s,BF)
    return pl.pallas_call(functools.partial(tail_kernel,N,C,E),
        out_shape=[jax.ShapeDtypeStruct((C,S,W3),BF),jax.ShapeDtypeStruct((S,D),BF),jax.ShapeDtypeStruct((T,D),BF)],
        in_specs=[pl.BlockSpec(memory_space=pl.ANY)]*3,
        out_specs=[pl.BlockSpec(memory_space=pl.ANY)]*3,
        scratch_shapes=[V(E,C,S,W3),V(E,S,D),V(H,T,D),V(N-1,E,C,S,W3),V(N-1,E,S,D),V(E,C,S,W3),V(E,S,D),V(E,C,S,W3),V(E,S,D),V(H,T,D),V(H-1,T,D),
            dma((2,E)),dma((H,)),dma((2,N-1,E)),dma((2,N-1,E)),dma((2,E)),dma((2,E)),dma((2,E)),dma((H,)),dma((H,)),dma((H-1,)),dma((H-1,)),dma((C-1,)),dma((C-1,)),dma((3,))],
        compiler_params=pltpu.CompilerParams(collective_id=cid,has_side_effects=True,vmem_limit_bytes=60*2**20),
        name="tail")(gq,go,dn)

def sums_kernel(sizes,x_ref,o_ref,*scr):
    names=("dp","ctx","exp")
    bufs=scr[:3]; ss=scr[3:6]; rs=scr[6:9]
    bar=pltpu.get_barrier_semaphore(); cnt=0
    me=[lax.axis_index(a) for a in names]
    for a,n,i in zip(names,sizes,me):
        for j in range(1,n):
            pl.semaphore_signal(bar,inc=1,device_id={a:lax.rem(i+j,n)},device_id_type=MESH); cnt+=1
    pl.semaphore_wait(bar,cnt)
    for t,(a,n,i) in enumerate(zip(names,sizes,me)):
        buf=bufs[t]
        buf[i]=x_ref[...] if t==0 else o_ref[...]
        def cp(j): return pltpu.make_async_remote_copy(buf.at[i],buf.at[i],ss[t].at[j-1],rs[t].at[j-1],device_id={a:lax.rem(i+j,n)},device_id_type=MESH)
        for j in range(1,n): cp(j).start()
        for j in range(1,n):
            src=lax.rem(i+n-j,n)
            pltpu.make_async_remote_copy(buf.at[src],buf.at[src],ss[t].at[j-1],rs[t].at[j-1],device_id={a:src},device_id_type=MESH).wait_recv()
        acc=buf[0]
        for j in range(1,n): acc=acc+buf[j]
        o_ref[...]=acc
        for j in range(1,n): cp(j).wait_send()

def sums(x,sizes,cid=3):
    R,D=x.shape; dma=pltpu.SemaphoreType.DMA
    return pl.pallas_call(functools.partial(sums_kernel,sizes),out_shape=jax.ShapeDtypeStruct((R,D),F32),
        in_specs=[pl.BlockSpec(memory_space=pltpu.VMEM)],out_specs=pl.BlockSpec(memory_space=pltpu.VMEM),
        scratch_shapes=[pltpu.VMEM((n,R,D),F32) for n in sizes]+[dma((n-1,)) for n in sizes]*2,
        compiler_params=pltpu.CompilerParams(collective_id=cid,has_side_effects=True,vmem_limit_bytes=32*2**20),name="sums")(x)


def nn(a,b): return lax.dot_general(a,b,(((1,),(0,)),((),())),preferred_element_type=F32)
def tn(a,b): return lax.dot_general(a,b,(((0,),(0,)),((),())),preferred_element_type=F32)
def nt(a,b): return lax.dot_general(a,b,(((1,),(1,)),((),())),preferred_element_type=F32)

def pick_of(slot_row, cap):
    T=slot_row.shape[1]
    return jnp.broadcast_to(slot_row,(cap,T))==lax.broadcasted_iota(jnp.int32,(cap,T),0)

def back_kernel(H,E,cap,slot,dgp,dup,gw,uw,o_ref,own,r1,r2,rz,snd,gb,ub,slv,wg,wu,ld_sem,w_sem,s1,q1,s2,q2,s3,qz,o_sem):
    c=lax.axis_index("ctx"); e=lax.axis_index("exp")
    h=c//2; l=c%2
    T,W=own.shape[2:]; FF=wg.shape[1]
    sib={"ctx":h*2+1-l}
    def xpeer(j): return lax.rem(h+j,H)
    bar=pltpu.get_barrier_semaphore()
    pl.semaphore_signal(bar,inc=1,device_id=sib,device_id_type=MESH)
    for j in range(1,H):
        pl.semaphore_signal(bar,inc=1,device_id={"ctx":xpeer(j)*2+l},device_id_type=MESH)
    @pl.when(e>0)
    def _(): pl.semaphore_signal(bar,inc=1,device_id={"exp":e-1},device_id_type=MESH)
    @pl.when(e<E-1)
    def _(): pl.semaphore_signal(bar,inc=1,device_id={"exp":e+1},device_id_type=MESH)
    order=by_distance(e,E)
    wl=[pltpu.make_async_copy(gw,wg,w_sem.at[0]),pltpu.make_async_copy(uw,wu,w_sem.at[1])]
    for x in wl: x.start()
    NS=snd.shape[0]; M=H*E
    def place(m):
        return lax.rem(h+1+m//E,H),order(lax.rem(m,E))
    def loads(n):
        hh,o=place(n//2)
        s=(hh*2+jnp.where(lax.rem(n,2)==0,1-l,l))*E+o; b=lax.rem(n,2)
        return [pltpu.make_async_copy(dgp.at[s],gb.at[b],ld_sem.at[0,b]),pltpu.make_async_copy(dup.at[s],ub.at[b],ld_sem.at[1,b])],s
    for x in loads(0)[0]: x.start()
    def c1(m):
        hh,o=place(m)
        return pltpu.make_async_remote_copy(snd.at[lax.rem(m,NS)],r1.at[hh,o],s1.at[m],q1.at[hh,o],device_id=sib,device_id_type=MESH)
    def c2(j,o):
        hh=xpeer(j)
        return pltpu.make_async_remote_copy(own.at[hh,o],r2.at[j-1,o],s2.at[j-1,o],q2.at[j-1,o],device_id={"ctx":hh*2+l},device_id_type=MESH)
    def cz(o,to,slot_): return pltpu.make_async_remote_copy(own.at[h,o],rz.at[slot_],s3.at[o],qz.at[slot_],device_id={"exp":to},device_id_type=MESH)
    step=min(512,W)
    def compute(n,dst):
        x,s=loads(n); b=lax.rem(n,2)
        for y in x: y.wait()
        @pl.when(n+1<2*M)
        def _():
            for y in loads(n+1)[0]: y.start()
        low=pick_of(slv[pl.ds(s,1),:],cap).astype(F32).astype(BF)
        def body(i):
            sl=pl.ds(pl.multiple_of(i*step,step),step)
            d=(nt(gb[b],wg[sl,:])+nt(ub[b],wu[sl,:])).astype(BF)
            dst[:,sl]=tn(low,d).astype(BF)
        loop(W//step,body)
    pltpu.sync_copy(slot,slv)
    for x in wl: x.wait()
    pl.semaphore_wait(bar,H+(e>0).astype(jnp.int32)+(e<E-1).astype(jnp.int32))
    def zstep(k):
        o=order(k)
        for j in range(1,H):
            c2(j,o).wait_recv()
            add_into(own.at[h,o],r2.at[j-1,o])
        @pl.when(o>e)
        def _():
            @pl.when(e>0)
            def _():
                cz(o,e-1,o).wait_recv(); add_into(own.at[h,o],rz.at[o])
            cz(o,e+1,o).start()
        @pl.when(o<e)
        def _():
            @pl.when(e<E-1)
            def _():
                cz(o,e+1,o).wait_recv(); add_into(own.at[h,o],rz.at[o])
            cz(o,e-1,jnp.where(o==e-1,E,o)).start()
    def pair(m):
        hh,o=place(m)
        @pl.when(m>=NS)
        def _(): c1(m-NS).wait_send()
        compute(2*m,snd.at[lax.rem(m,NS)])
        c1(m).start()
        compute(2*m+1,own.at[hh,o])
        c1(m).wait_recv()
        add_into(own.at[hh,o],r1.at[hh,o])
        for j in range(1,H):
            @pl.when(m//E==j-1)
            def _(): c2(j,o).start()
        @pl.when(m//E==H-1)
        def _(): zstep(lax.rem(m,E))
    loop(M,pair)
    for m in range(max(0,M-NS),M): c1(m).wait_send()
    @pl.when(e>0)
    def _():
        cz(e,e-1,e).wait_recv(); add_into(own.at[h,e],rz.at[e])
    @pl.when(e<E-1)
    def _():
        cz(e,e+1,E).wait_recv(); add_into(own.at[h,e],rz.at[E])
    out=pltpu.make_async_copy(own.at[h,e],o_ref,o_sem); out.start()
    def drain(k):
        for j in range(1,H): c2(j,order(k)).wait_send()
        @pl.when(k<E-1)
        def _(): cz(order(k),e,order(k)).wait_send()
    loop(E,drain)
    out.wait()


def back_call(slot,dgp,dup,gw,uw,C,E,T,cids):
    S,cap,FF=dgp.shape; D=gw.shape[0]; H=C//2
    dma=pltpu.SemaphoreType.DMA; V=lambda *s: pltpu.VMEM(s,BF)
    blocks=2*H*E+(H-1)*E+E+4
    parts=1
    while 2*(blocks*T*D//parts+2*D//parts*FF+4*cap*FF)>60*2**20: parts*=2
    W=D//parts
    def part(i):
        a,b=(gw,uw) if parts==1 else (gw[i*W:(i+1)*W],uw[i*W:(i+1)*W])
        return pl.pallas_call(functools.partial(back_kernel,H,E,cap),
            out_shape=jax.ShapeDtypeStruct((T,W),BF),
            in_specs=[pl.BlockSpec(memory_space=pl.ANY)]*5,
            out_specs=pl.BlockSpec(memory_space=pl.ANY),
            scratch_shapes=[V(H,E,T,W),V(H,E,T,W),V(H-1,E,T,W),V(E+1,T,W),V(3,T,W),V(2,cap,FF),V(2,cap,FF),pltpu.VMEM((S,T),jnp.int32),V(W,FF),V(W,FF),
                dma((2,2)),dma((2,)),dma((H*E,)),dma((H,E)),dma((H-1,E)),dma((H-1,E)),dma((E,)),dma((E+1,)),dma(())],
            cost_estimate=pl.CostEstimate(flops=2*S*cap*(2*W*FF+T*W),bytes_accessed=S*4*cap*FF,transcendentals=0),
            compiler_params=pltpu.CompilerParams(collective_id=cids[i],has_side_effects=True,vmem_limit_bytes=61*2**20),
            name="back")(slot,dgp,dup,a,b)
    out=[part(i) for i in range(parts)]
    return out[0] if parts==1 else jnp.concatenate(out,axis=1)

def fwd_kernel(H,E,T,cap,in_vmem,slot,rows,cot,gw,uw,dw,recv,hid,dout,dgp,dup,moe,dg,*scr):
    if in_vmem: allr=scr[0]; scr=scr[1:]; rb=None
    else: allr=scr[0]; rb=scr[1]; scr=scr[2:]
    (slv,wg,wu,wd,cb,srecv,shid,sdout,sdgp,sdup,smoe,sdg,cr,w_sem,c_sem,l_sem,o_sem,up_s,dn_s,up_r,dn_r,x_s,x_r,b_s,b_r)=scr
    c=lax.axis_index("ctx"); e=lax.axis_index("exp")
    h=c//2; l=c%2; C=2*H; S=C*E
    D=wg.shape[0]; FF=wg.shape[1]; EXT=allr.shape[1]
    expert=c*E+e
    def xpeer(j): return lax.rem(h+j,H)
    def idx(hh,ll,ee): return (hh*2+ll)*E+ee
    bar=pltpu.get_barrier_semaphore()
    pl.semaphore_signal(bar,inc=1,device_id={"ctx":h*2+1-l},device_id_type=MESH)
    for j in range(1,H):
        pl.semaphore_signal(bar,inc=1,device_id={"ctx":xpeer(j)*2+l},device_id_type=MESH)
    @pl.when(e>0)
    def _(): pl.semaphore_signal(bar,inc=1,device_id={"exp":e-1},device_id_type=MESH)
    @pl.when(e<E-1)
    def _(): pl.semaphore_signal(bar,inc=1,device_id={"exp":e+1},device_id_type=MESH)
    order=by_distance(e,E)
    def near(k): return order(E-1-k)
    own=idx(h,l,e)
    wl=[pltpu.make_async_copy(a,b,w_sem.at[i]) for i,(a,b) in enumerate(((gw,wg),(uw,wu),(dw,wd)))]
    first=pltpu.make_async_copy(rows,allr.at[own],w_sem.at[3])
    first.start()
    for x in wl: x.start()
    def job(n):
        m=jnp.maximum(n-2,0)
        r=jnp.where(n<2,0,1+m//(2*H)); t=jnp.where(n<2,n,lax.rem(m,2*H))
        t=jnp.where(r==E,t+2,t)
        j=t//2
        return r,t,j,lax.rem(t,2),jnp.where(j==0,r,r-1)
    def hi(j): return jnp.where(j==0,h,lax.rem(h+H-j,H))
    def sender(n):
        r,t,j,s,k=job(n)
        return idx(hi(j),jnp.where(s==1,1-l,l),near(k))
    def cload(n): return pltpu.make_async_copy(cot.at[sender(n)],cb.at[lax.rem(n,2)],c_sem.at[lax.rem(n,2)])
    cload(0).start()
    def rc(i,ss,rs,**kw): return pltpu.make_async_remote_copy(allr.at[i],allr.at[i],ss,rs,device_id=kw,device_id_type=MESH)
    def up(ee): return rc(idx(h,l,ee),up_s.at[ee],up_r.at[ee],exp=e+1)
    def dn(ee): return rc(idx(h,l,ee),dn_s.at[ee],dn_r.at[ee],exp=e-1)
    def xs(j,ee): return rc(idx(h,l,ee),x_s.at[j-1,ee],x_r.at[j-1,ee],ctx=xpeer(j)*2+l)
    def xr(j,ee):
        return rc(idx(hi(j),l,ee),x_s.at[j-1,ee],x_r.at[j-1,ee],ctx=hi(j)*2+l)
    def bs(j,ee): return rc(idx(hi(j),l,ee),b_s.at[j,ee],b_r.at[j,ee],ctx=h*2+1-l)
    def br(j,ee): return rc(idx(hi(j),1-l,ee),b_s.at[j,ee],b_r.at[j,ee],ctx=h*2+1-l)
    outs=[(srecv,recv),(shid,hid),(sdout,dout),(sdgp,dgp),(sdup,dup),(smoe,moe),(sdg,dg)]
    def odma(n):
        s=sender(n); b=lax.rem(n,2)
        return [pltpu.make_async_copy(a.at[b],o.at[s],o_sem.at[i,b]) for i,(a,o) in enumerate(outs)]
    def compute(n):
        s=sender(n); b=lax.rem(n,2)
        if in_vmem: rw=allr.at[s]
        else:
            cp=pltpu.make_async_copy(allr.at[s],rb,l_sem); cp.start(); cp.wait(); rw=rb
        cload(n).wait()
        @pl.when(n+1<S)
        def _(): cload(n+1).start()
        @pl.when(n>=2)
        def _():
            for x in odma(n-2): x.wait()
        ct=cb.at[b]
        pk=pick_of(slv[pl.ds(s,1),:],cap); pf=pk.astype(F32); low=pf.astype(BF)
        gm=rw[T:EXT,:T].astype(F32)
        g=jnp.sum(jnp.where(lax.broadcasted_iota(jnp.int32,gm.shape,0)==expert,gm,0.0),axis=0,keepdims=True)
        gsel=jnp.where(pk,jnp.broadcast_to(g,(cap,T)),0.0)
        grow=jnp.sum(gsel,axis=1,keepdims=True)
        comb=gsel.astype(BF)
        step=512
        for m in range(0,D,step):
            srecv[b,:,m:m+step]=nn(low,rw[:T,m:m+step]).astype(BF)
            q=nn(low,ct[:,m:m+step])
            sdout[b,:,m:m+step]=(q*grow).astype(BF)
            cr[:,m:m+step]=q.astype(BF)
        half=FF//2
        for m in range(0,FF,half):
            gp=nn(srecv[b],wg[:,m:m+half]); upp=nn(srecv[b],wu[:,m:m+half])
            dh=nt(sdout[b],wd[m:m+half,:])
            sg=jax.nn.sigmoid(gp); si=gp*sg
            shid[b,:,m:m+half]=(si*upp).astype(BF)
            sdgp[b,:,m:m+half]=(dh*upp*sg*(1.0+gp*(1.0-sg))).astype(BF)
            sdup[b,:,m:m+half]=(dh*si).astype(BF)
        acc=jnp.zeros((cap,1),F32)
        for m in range(0,D,step):
            ev=nn(shid[b],wd[:,m:m+step]).astype(BF)
            acc=acc+jnp.sum(cr[:,m:m+step].astype(F32)*ev.astype(F32),axis=1,keepdims=True)
            smoe[b,:,m:m+step]=tn(comb,ev).astype(BF)
        sdg[b]=jnp.sum(pf*acc,axis=0,keepdims=True)
        for x in odma(n): x.start()
    pltpu.sync_copy(slot,slv)
    first.wait()
    pl.semaphore_wait(bar,H+(e>0).astype(jnp.int32)+(e<E-1).astype(jnp.int32))
    @pl.when(e<E-1)
    def _(): up(e).start()
    @pl.when(e>0)
    def _(): dn(e).start()
    for j in range(1,H): xs(j,e).start()
    bs(0,e).start()
    for x in wl: x.wait()
    def step_(n):
        r,t,j,sib_,k=job(n)
        @pl.when(jnp.logical_and(t==0,r>0))
        def _():
            @pl.when(e>=r)
            def _():
                up(e-r).wait_recv()
                @pl.when(e<E-1)
                def _(): up(e-r).start()
                for q in range(1,H): xs(q,e-r).start()
                bs(0,e-r).start()
            @pl.when(e+r<E)
            def _():
                dn(e+r).wait_recv()
                @pl.when(e>0)
                def _(): dn(e+r).start()
                for q in range(1,H): xs(q,e+r).start()
                bs(0,e+r).start()
        @pl.when(jnp.logical_and(sib_==0,j>0))
        def _():
            xr(j,near(k)).wait_recv(); bs(j,near(k)).start()
        @pl.when(sib_==1)
        def _(): br(j,near(k)).wait_recv()
        compute(n)
    loop(S,step_)
    for x in odma(S-2)+odma(S-1): x.wait()
    def drain(ee):
        @pl.when(jnp.logical_and(e<E-1,ee<=e))
        def _(): up(ee).wait_send()
        @pl.when(jnp.logical_and(e>0,ee>=e))
        def _(): dn(ee).wait_send()
        for j in range(1,H): xs(j,ee).wait_send()
        for j in range(H): bs(j,ee).wait_send()
    loop(E,drain)


def fwd_call(slot,rows,cot,gw,uw,dw,cap,C,E,T,cid=4):
    EXT,D=rows.shape; S=C*E; H=C//2; FF=gw.shape[1]
    dma=pltpu.SemaphoreType.DMA; V=lambda *s: pltpu.VMEM(s,BF)
    in_vmem=S*EXT*D*2<=28*2**20
    A=pl.BlockSpec(memory_space=pl.ANY)
    sd=lambda a,b,dt=BF: jax.ShapeDtypeStruct((S,a,b),dt)
    out_shape=[sd(cap,D),sd(cap,FF),sd(cap,D),sd(cap,FF),sd(cap,FF),sd(T,D),sd(1,T,F32)]
    land=[V(S,EXT,D)] if in_vmem else [V(EXT,D)]
    if not in_vmem: out_shape=out_shape+[sd(EXT,D)]
    body=functools.partial(fwd_kernel,H,E,T,cap,in_vmem)
    r=pl.pallas_call(body,out_shape=out_shape,in_specs=[A]*6,out_specs=[A]*len(out_shape),
        scratch_shapes=land+[pltpu.VMEM((S,T),jnp.int32),V(D,FF),V(D,FF),V(FF,D),V(2,T,D),V(2,cap,D),V(2,cap,FF),V(2,cap,D),V(2,cap,FF),V(2,cap,FF),V(2,T,D),pltpu.VMEM((2,1,T),F32),V(cap,D),
            dma((4,)),dma((2,)),dma(()),dma((7,2)),dma((E,)),dma((E,)),dma((E,)),dma((E,)),dma((H-1,E)),dma((H-1,E)),dma((H,E)),dma((H,E))],
        cost_estimate=pl.CostEstimate(flops=2*S*cap*(4*D*FF+3*T*D),bytes_accessed=S*2*(T*D+2*cap*D+3*cap*FF+T*D)+6*D*FF,transcendentals=S*cap*FF),
        compiler_params=pltpu.CompilerParams(collective_id=cid,has_side_effects=True,vmem_limit_bytes=61*2**20),name="experts_fwd")(slot,rows,cot,gw,uw,dw)
    return r[:7]


def mask_bias(lab_r,lab_c,i0,bq,K):
    lr=lab_r[:,:K]; lc=lab_c
    row=lax.broadcasted_iota(jnp.int32,(bq,K),0)+i0; col=lax.broadcasted_iota(jnp.int32,(bq,K),1)
    ok=(col<=row)&((lr==0)|(lr==lc))
    return jnp.where(ok,0.0,-1e30).astype(F32)

def attn_fwd_kernel(heads,bq,scale,raw,rr,cos,sin,lab_r,lab_c,gains,qo,ko,vo,mix,bias):
    G=raw.shape[0]; cols=heads*HEAD
    rb=min(128,G)
    def prep(i,_):
        sl=pl.ds(pl.multiple_of(i*rb,rb),rb)
        cs,sn=cos[sl,:],sin[sl,:]
        for t,o in ((0,qo),(1,ko)):
            r=rr[sl,t:t+1]
            for hd in range(heads):
                a=hd*HEAD
                v=raw[sl,t*cols+a:t*cols+a+HEAD]*r*gains[t:t+1,a:a+HEAD]
                o[sl,a:a+HEAD]=(v*cs+pltpu.roll(v,HEAD//2,1)*sn).astype(BF)
        vo[sl,:]=raw[sl,2*cols:].astype(BF)
        return 0
    lax.fori_loop(0,G//rb,prep,0)
    def block(i,K):
        rows=pl.ds(pl.multiple_of(i*bq,bq),bq)
        bias[:,:K]=mask_bias(lab_r,lab_c[rows,:],i*bq,bq,K)
        def head(hd,_):
            ln=pl.ds(pl.multiple_of(hd*HEAD,HEAD),HEAD)
            s=nt(qo[rows,ln],ko[:K,ln])*scale+bias[:,:K]
            p=jnp.exp(s-jnp.max(s,axis=1,keepdims=True))
            pr=(p*(1.0/jnp.sum(p,axis=1,keepdims=True))).astype(BF)
            mix[rows,ln]=nn(pr,vo[:K,ln]).astype(BF)
            return 0
        lax.fori_loop(0,heads,head,0)
    per=G//bq//3
    for g in range(3):
        loop(per,lambda i,g=g: block(i+g*per,(g+1)*per*bq))

def attn_fwd(raw,rr,cos,sin,lab_r,lab_c,gains,heads,bq=128):
    G=raw.shape[0]; cols=heads*HEAD
    o=jax.ShapeDtypeStruct((G,cols),BF)
    V=pl.BlockSpec(memory_space=pltpu.VMEM)
    return pl.pallas_call(functools.partial(attn_fwd_kernel,heads,bq,HEAD**-0.5),out_shape=[o]*4,in_specs=[V]*7,out_specs=[V]*4,
        scratch_shapes=[pltpu.VMEM((bq,G),F32)],
        cost_estimate=pl.CostEstimate(flops=2*2*heads*G*G*HEAD,bytes_accessed=G*cols*20,transcendentals=heads*G*G),
        compiler_params=pltpu.CompilerParams(vmem_limit_bytes=48*2**20),name="attn_fwd")(raw,rr,cos,sin,lab_r,lab_c,gains)

def attn_bwd_kernel(heads,bq,scale,q,k,v,dm,cos,sin,lab_r,lab_c,dq,dk,dv,bias,ak,av):
    G=q.shape[0]
    ak[...]=jnp.zeros_like(ak); av[...]=jnp.zeros_like(av)
    def block(i,K):
        rows=pl.ds(pl.multiple_of(i*bq,bq),bq)
        bias[:,:K]=mask_bias(lab_r,lab_c[rows,:],i*bq,bq,K)
        def head(hd,_):
            ln=pl.ds(pl.multiple_of(hd*HEAD,HEAD),HEAD)
            qb=q[rows,ln]; kb=k[:K,ln]; db=dm[rows,ln]
            s=nt(qb,kb)*scale+bias[:,:K]
            p=jnp.exp(s-jnp.max(s,axis=1,keepdims=True))
            p=p*(1.0/jnp.sum(p,axis=1,keepdims=True))
            dp=nt(db,v[:K,ln])
            ds=(p*(dp-jnp.sum(p*dp,axis=1,keepdims=True))).astype(BF)
            g=nn(ds,kb)*scale
            dq[rows,ln]=g*cos[rows,:]-pltpu.roll(g,HEAD//2,1)*sin[rows,:]
            ak[:K,ln]+=tn(ds,qb)
            av[:K,ln]+=tn(p.astype(BF),db)
            return 0
        lax.fori_loop(0,heads,head,0)
    per=G//bq//3
    for g in range(3):
        loop(per,lambda i,g=g: block(i+g*per,(g+1)*per*bq))
    rb=min(128,G)
    def fin(i,_):
        sl=pl.ds(pl.multiple_of(i*rb,rb),rb)
        for hd in range(heads):
            a=hd*HEAD
            g=ak[sl,a:a+HEAD]*scale
            dk[sl,a:a+HEAD]=g*cos[sl,:]-pltpu.roll(g,HEAD//2,1)*sin[sl,:]
        dv[sl,:]=av[sl,:].astype(BF)
        return 0
    lax.fori_loop(0,G//rb,fin,0)

def attn_bwd(q,k,v,dm,cos,sin,lab_r,lab_c,heads,bq=128):
    G,cols=q.shape
    V=pl.BlockSpec(memory_space=pltpu.VMEM)
    f=jax.ShapeDtypeStruct((G,cols),F32)
    return pl.pallas_call(functools.partial(attn_bwd_kernel,heads,bq,HEAD**-0.5),out_shape=[f,f,jax.ShapeDtypeStruct((G,cols),BF)],in_specs=[V]*8,out_specs=[V]*3,
        scratch_shapes=[pltpu.VMEM((bq,G),F32),pltpu.VMEM((G,cols),F32),pltpu.VMEM((G,cols),F32)],
        cost_estimate=pl.CostEstimate(flops=5*2*heads*G*G*HEAD,bytes_accessed=G*cols*20,transcendentals=heads*G*G),
        compiler_params=pltpu.CompilerParams(vmem_limit_bytes=48*2**20),name="attn_bwd")(q,k,v,dm,cos,sin,lab_r,lab_c)

def ctx_barrier(H,c,h,l):
    bar=pltpu.get_barrier_semaphore()
    pl.semaphore_signal(bar,inc=1,device_id={"ctx":h*2+1-l},device_id_type=MESH)
    for j in range(1,H):
        pl.semaphore_signal(bar,inc=1,device_id={"ctx":lax.rem(h+j,H)*2+l},device_id_type=MESH)
    pl.semaphore_wait(bar,H)

def ag_ctx_kernel(H,Q,x,o,xs,xr,bs,br,lsem):
    c=lax.axis_index("ctx"); h=c//2; l=c%2
    T=x.shape[0]; R=T//Q
    loc=pltpu.make_async_copy(x,o.at[c],lsem); loc.start()
    ctx_barrier(H,c,h,l)
    sib=h*2+1-l
    def sl(q): return pl.ds(q*R,R)
    def rc(a,b,s,r,to): return pltpu.make_async_remote_copy(a,b,s,r,device_id={"ctx":to},device_id_type=MESH)
    def xc(j,q): return rc(x.at[sl(q)],o.at[c,sl(q)],xs.at[j-1,q],xr.at[j-1,q],lax.rem(h+j,H)*2+l)
    def xw(j,q):
        p=lax.rem(h+H-j,H)*2+l; return rc(x.at[sl(q)],o.at[p,sl(q)],xs.at[j-1,q],xr.at[j-1,q],p)
    def bc(j,q):
        p=c if j==0 else lax.rem(h+H-j,H)*2+l
        src=x if j==0 else o.at[p]
        return rc(src.at[sl(q)],o.at[p,sl(q)],bs.at[j,q],br.at[j,q],sib)
    def bw(j,q):
        p=sib if j==0 else lax.rem(h+H-j,H)*2+1-l
        return rc(x.at[sl(q)],o.at[p,sl(q)],bs.at[j,q],br.at[j,q],sib)
    for q in range(Q):
        for j in range(1,H): xc(j,q).start()
    for q in range(Q): bc(0,q).start()
    for q in range(Q):
        for j in range(1,H):
            xw(j,q).wait_recv(); bc(j,q).start()
    for j in range(H):
        for q in range(Q):
            bw(j,q).wait_recv(); bc(j,q).wait_send()
            if j>0: xc(j,q).wait_send()
    loc.wait()

def ag_ctx(x,C,cid,Q=4):
    T,D=x.shape; H=C//2; dma=pltpu.SemaphoreType.DMA
    A=pl.BlockSpec(memory_space=pl.ANY)
    return pl.pallas_call(functools.partial(ag_ctx_kernel,H,Q),out_shape=jax.ShapeDtypeStruct((C,T,D),x.dtype),in_specs=[A],out_specs=A,
        scratch_shapes=[dma((H-1,Q)),dma((H-1,Q)),dma((H,Q)),dma((H,Q)),dma(())],
        compiler_params=pltpu.CompilerParams(collective_id=cid,has_side_effects=True),name="ag_ctx")(x)

def rs_ctx_kernel(H,Q,x,o,own,r1,r2,ld,s1,q1,s2,q2,osem):
    c=lax.axis_index("ctx"); h=c//2; l=c%2
    T=own.shape[1]; R=T//Q
    def sl(q): return pl.ds(q*R,R)
    hs=[lax.rem(h+j,H) for j in range(1,H)]+[h]
    def load(i): return pltpu.make_async_copy(x.at[hs[i]*2+l],own.at[hs[i]],ld.at[i])
    for i in range(H): load(i).start()
    ctx_barrier(H,c,h,l)
    def c1(i,q): return pltpu.make_async_remote_copy(x.at[hs[i]*2+1-l,sl(q)],r1.at[hs[i],sl(q)],s1.at[hs[i],q],q1.at[hs[i],q],device_id={"ctx":h*2+1-l},device_id_type=MESH)
    def c2(j,q): return pltpu.make_async_remote_copy(own.at[hs[j-1],sl(q)],r2.at[j-1,sl(q)],s2.at[j-1,q],q2.at[j-1,q],device_id={"ctx":hs[j-1]*2+l},device_id_type=MESH)
    for i in range(H):
        for q in range(Q): c1(i,q).start()
    for i in range(H):
        load(i).wait()
        for q in range(Q):
            c1(i,q).wait_recv()
            add_into(own.at[hs[i],sl(q)],r1.at[hs[i],sl(q)])
            if i<H-1: c2(i+1,q).start()
    for q in range(Q):
        for j in range(1,H):
            c2(j,q).wait_recv()
            add_into(own.at[h,sl(q)],r2.at[j-1,sl(q)])
    out=pltpu.make_async_copy(own.at[h],o,osem); out.start()
    for q in range(Q):
        for i in range(H): c1(i,q).wait_send()
        for j in range(1,H): c2(j,q).wait_send()
    out.wait()

def rs_ctx(x,cid,Q=4):
    C,T,D=x.shape; H=C//2; dma=pltpu.SemaphoreType.DMA
    A=pl.BlockSpec(memory_space=pl.ANY)
    return pl.pallas_call(functools.partial(rs_ctx_kernel,H,Q),out_shape=jax.ShapeDtypeStruct((T,D),x.dtype),in_specs=[A],out_specs=A,
        scratch_shapes=[pltpu.VMEM((H,T,D),BF),pltpu.VMEM((H,T,D),BF),pltpu.VMEM((H-1,T,D),BF),dma((H,)),dma((H,Q)),dma((H,Q)),dma((H-1,Q)),dma((H-1,Q)),dma(())],
        compiler_params=pltpu.CompilerParams(collective_id=cid,has_side_effects=True,vmem_limit_bytes=40*2**20),name="rs_ctx")(x)


def dot_nn(a, b):
    return lax.dot_general(a, b, (((1,), (0,)), ((), ())), preferred_element_type=F32)


def dot_tn(a, b):
    return lax.dot_general(a, b, (((0,), (0,)), ((), ())), preferred_element_type=F32)


def dot_nt(a, b):
    return lax.dot_general(a, b, (((1,), (1,)), ((), ())), preferred_element_type=F32)


def low_dp(grad, n_dp):
    low = grad.astype(BF)
    if n_dp != 2:
        return (lax.psum(low, "dp"),)
    return low, lax.ppermute(low, "dp", [(0, 1), (1, 0)])


def per_device(
    hidden_in,
    segments,
    routes,
    attn_gain,
    query_weight,
    key_weight,
    value_weight,
    query_gain,
    key_gain,
    output_weight,
    ffn_gain,
    router_weight,
    gate_weight,
    up_weight,
    down_weight,
    cotangent,
):
    n_dp, n_ctx, n_exp = (lax.axis_size(a) for a in ALL)
    tok, width = hidden_in.shape[2:]
    topk = routes.shape[3]
    experts = n_ctx * n_exp
    cap = (5 * tok * topk + 4 * experts - 1) // (4 * experts)
    cap = -(-cap // 16) * 16
    group = segments.shape[2]
    shard = query_weight.shape[0]
    cols = width // n_ctx
    piece = cols // n_dp
    heads = cols // HEAD
    ctx_me = lax.axis_index("ctx")
    exp_me = lax.axis_index("exp")
    expert_me = ctx_me * n_exp + exp_me

    def own_cols(vec):
        return lax.dynamic_index_in_dim(
            vec.reshape(n_dp, n_ctx, piece), ctx_me, 1, keepdims=False
        ).reshape(cols)

    packed = jnp.stack([query_weight, key_weight, value_weight], axis=1)
    packed = packed.reshape(shard, 3, n_dp, n_ctx, piece).transpose(3, 0, 1, 2, 4)
    packed = lax.all_to_all(packed, "ctx", split_axis=0, concat_axis=0, tiled=True)
    packed = packed.reshape(n_ctx * shard, 3 * cols)
    qkv_w = lax.all_gather(packed, ROWS, axis=0, tiled=True)
    qkv_w = (
        qkv_w.reshape(n_dp, n_exp, n_ctx, shard, 3 * cols)
        .transpose(0, 2, 1, 3, 4)
        .reshape(width, 3 * cols)
    )
    out_w = lax.all_gather(output_weight, ROWS, axis=0, tiled=True)

    own_routes = routes[0, 0]
    expert_ids = jnp.arange(experts, dtype=jnp.int32)
    hits = jnp.sum((own_routes[:, :, None] == expert_ids).astype(jnp.int32), axis=1)
    tokens = jnp.arange(tok, dtype=jnp.int32)
    lower = (tokens[:, None] > tokens[None, :]).astype(BF)
    earlier = dot_nn(lower, hits.astype(BF)).astype(jnp.int32)
    slot_local = jnp.where(hits > 0, earlier, -1).T
    slot = lax.all_to_all(slot_local, MOE, split_axis=0, concat_axis=0, tiled=True)
    slot = slot.reshape(experts, tok)
    cot = cotangent[0, 0]
    cot_all = lax.all_gather(cot, MOE, axis=0, tiled=False)

    hidden = hidden_in[0, 0].astype(F32)
    labels = segments[0, 0]
    index = jnp.arange(group, dtype=jnp.int32)
    before = jnp.sum((labels[None, :] < labels[:, None]).astype(jnp.int32), axis=1)
    positions = index - before + jnp.where(labels > 0, PROMPT, 0).astype(jnp.int32)
    half = HEAD // 2
    frequency = THETA ** (-(jnp.arange(half, dtype=F32) * 2.0 / HEAD))
    angles = positions.astype(F32)[:, None] * frequency[None, :]
    cos, sin = jnp.cos(angles), jnp.sin(angles)
    cos = jnp.concatenate([cos, cos], axis=1)
    sin = jnp.concatenate([-sin, sin], axis=1)
    label_row, label_col = labels[None, :], labels[:, None]
    attn_gain_f = attn_gain.astype(F32)
    ffn_gain_f = ffn_gain.astype(F32)
    q_gain = own_cols(query_gain.astype(F32))
    k_gain = own_cols(key_gain.astype(F32))

    attn_r = lax.rsqrt(jnp.mean(hidden * hidden, axis=-1, keepdims=True) + EPS)
    normed = (hidden * attn_r * attn_gain_f).astype(BF)
    normed_g = ag_ctx(normed, n_ctx, 5).reshape(group, width)
    raw = dot_nn(normed_g, qkv_w)
    q_raw, k_raw = raw[:, :cols], raw[:, cols : 2 * cols]
    squares = lax.psum(
        jnp.stack([jnp.sum(q_raw * q_raw, axis=1), jnp.sum(k_raw * k_raw, axis=1)]), "ctx"
    )
    inv = lax.rsqrt(squares / width + EPS)
    q_r, k_r = inv[0][:, None], inv[1][:, None]
    q_rot, k_rot, v_low, mix = attn_fwd(
        raw, inv.T, cos, sin, label_row, label_col, jnp.stack([q_gain, k_gain]), heads
    )
    branch = rs_ctx(dot_nn(mix, out_w).astype(BF).reshape(n_ctx, tok, width), 6)
    residual = hidden + branch.astype(F32)

    ffn_r = lax.rsqrt(jnp.mean(residual * residual, axis=-1, keepdims=True) + EPS)
    ffn_normed = (residual * ffn_r * ffn_gain_f).astype(BF)
    logits = dot_nn(ffn_normed, router_weight)
    router_prob = jax.nn.softmax(logits, axis=-1)
    gates = jnp.where(hits > 0, router_prob, 0.0).astype(BF)
    padded = jnp.zeros((experts, width), BF).at[:, :tok].set(gates.T)
    rows_ext = jnp.concatenate([ffn_normed, padded], axis=0)
    gate_mat, up_mat, down_mat = gate_weight[0], up_weight[0], down_weight[0]
    received, expert_hidden, d_out, d_gate_pre, d_up_pre, moe_part, d_gate_at = fwd_call(
        slot, rows_ext, cot_all, gate_mat, up_mat, down_mat, cap, n_ctx, n_exp, tok
    )
    total = experts * cap

    d_gate = lax.all_to_all(
        d_gate_at.reshape(experts, tok), MOE, split_axis=0, concat_axis=0, tiled=True
    ).T
    d_tokens = back_call(slot, d_gate_pre, d_up_pre, gate_mat, up_mat, n_ctx, n_exp, tok, (1, 8))
    moe_part, d_tokens = lax.optimization_barrier((moe_part, d_tokens))
    moe_out = lax.psum_scatter(
        moe_part.reshape(experts * tok, width), MOE, scatter_dimension=0, tiled=True
    )
    received = received.reshape(total, width)
    down_grad = dot_tn(expert_hidden.reshape(total, -1), d_out.reshape(total, width))
    gate_grad = dot_tn(received, d_gate_pre.reshape(total, -1))
    up_grad = dot_tn(received, d_up_pre.reshape(total, -1))
    wide = [low_dp(g, n_dp) for g in (gate_grad, up_grad, down_grad)]

    d_router = d_gate
    d_logits = (
        router_prob * (d_router - jnp.sum(router_prob * d_router, axis=-1, keepdims=True))
    ).astype(BF)
    router_grad = dot_tn(d_logits, ffn_normed)
    d_ffn = d_tokens.astype(F32) + dot_nt(d_logits, router_weight)
    ffn_gain_grad = jnp.sum(d_ffn * residual * ffn_r, axis=0)
    weighted = d_ffn * ffn_gain_f
    d_residual = cot.astype(F32) + (
        weighted * ffn_r
        - residual * ffn_r**3 * jnp.mean(residual * weighted, axis=-1, keepdims=True)
    )
    d_branch = d_residual.astype(BF)

    d_branch_g = ag_ctx(d_branch, n_ctx, 7).reshape(group, width)
    out_grad = dot_tn(mix, d_branch_g)
    d_mix = dot_nt(d_branch_g, out_w).astype(BF)
    d_qn, d_kn, d_v = attn_bwd(q_rot, k_rot, v_low, d_mix, cos, sin, label_row, label_col, heads)
    q_gain_part = jnp.sum(d_qn * q_raw * q_r, axis=0)
    k_gain_part = jnp.sum(d_kn * k_raw * k_r, axis=0)
    d_qw, d_kw = d_qn * q_gain, d_kn * k_gain
    dots = (
        lax.psum(jnp.stack([jnp.sum(q_raw * d_qw, axis=1), jnp.sum(k_raw * d_kw, axis=1)]), "ctx")
        / width
    )
    d_q_raw = d_qw * q_r - q_raw * q_r**3 * dots[0][:, None]
    d_k_raw = d_kw * k_r - k_raw * k_r**3 * dots[1][:, None]
    d_raw = jnp.concatenate(
        [d_q_raw.astype(BF), d_k_raw.astype(BF), d_v], axis=1
    )
    d_raw, moe_out = lax.optimization_barrier((d_raw, moe_out))
    output = (residual + moe_out.astype(F32)).astype(BF)
    d_part_n = dot_nt(d_raw, qkv_w).astype(BF).reshape(n_ctx, tok, width)
    qkv_grad = dot_tn(normed_g, d_raw).astype(BF).reshape(n_dp, n_ctx, n_exp, shard, 3 * cols)
    out_part = out_grad.astype(BF).reshape(n_dp, n_exp, shard, width)
    qkv_sum, out_sum, d_normed = tail(qkv_grad, out_part, d_part_n)
    d_normed = d_normed.astype(F32)
    wide, d_normed = lax.optimization_barrier((wide, d_normed))
    gate_sum, up_sum, down_sum = (sum(x.astype(F32) for x in pair) for pair in wide)
    attn_gain_grad = jnp.sum(d_normed * hidden * attn_r, axis=0)
    weighted = d_normed * attn_gain_f
    hidden_grad = (
        d_residual
        + weighted * attn_r
        - hidden * attn_r**3 * jnp.mean(hidden * weighted, axis=-1, keepdims=True)
    ).astype(BF)

    qkv_sum = qkv_sum.reshape(n_ctx, shard, 3, n_dp, piece)
    qkv_sum = qkv_sum.transpose(2, 1, 3, 0, 4).reshape(3, shard, width).astype(F32)
    out_sum = out_sum.astype(F32)

    spread = jnp.zeros((2, n_dp, n_ctx, piece), F32)
    spread = lax.dynamic_update_slice(
        spread,
        jnp.stack([q_gain_part, k_gain_part]).reshape(2, n_dp, 1, piece),
        (0, 0, ctx_me, 0),
    ).reshape(2, width)
    small = jnp.concatenate(
        [router_grad, spread, attn_gain_grad[None], ffn_gain_grad[None]], axis=0
    )
    pad = -small.shape[0] % 8
    small = sums(jnp.pad(small, ((0, pad), (0, 0))), (n_dp, n_ctx, n_exp))
    late, early = small[experts:], small
    return (
        output[None, None],
        hidden_grad[None, None],
        late[2],
        qkv_sum[0],
        qkv_sum[1],
        qkv_sum[2],
        late[0],
        late[1],
        out_sum,
        late[3],
        early[:experts].T,
        gate_sum[None],
        up_sum[None],
        down_sum[None],
    )


def solution(mesh):
    tokens = P("dp", "exp", "ctx", None)
    rows = P(ALL, None)
    expert = P(MOE, None, None)
    return jax.shard_map(
        per_device,
        mesh=mesh,
        in_specs=(
            tokens,
            P("dp", "exp", None),
            tokens,
            P(),
            rows,
            rows,
            rows,
            P(),
            P(),
            rows,
            P(),
            P(),
            expert,
            expert,
            expert,
            tokens,
        ),
        out_specs=(
            tokens,
            tokens,
            P(),
            rows,
            rows,
            rows,
            P(),
            P(),
            rows,
            P(),
            P(),
            expert,
            expert,
            expert,
        ),
        check_vma=False,
    )
```

time: 2070 us -> 1220 us (0.59)
  waiting for transfers between devices: 1270 us -> 102 us
  Pallas kernels: 0 us -> 784 us
  matrix products: 479 us -> 134 us
  other arithmetic: 136 us -> 67.6 us
  blocking collectives: 89.2 us -> 55.5 us
  local copies, waits for them, and re-layouts: 65.1 us -> 33.1 us
    pallas_call x0 -> x9, Pallas kernels: none -> 784 us  [the longest x1 176 us: tail(): pl.pallas_call(functools.partial(tail_kernel, N, C, E), out_shape=[jax.Sh...]
    reduce_scatter x5 -> x0, waiting for transfers between devices: 530 us -> none  [the longest x1 232 us: per_device(): lax.psum_scatter(d_part.reshape(experts * tok, width), MOE, scatter_dimen...]
    reduce_scatter x1, waiting for transfers between devices: 244 us -> 0.02 us  [per_device(): lax.psum_scatter(moe_part.reshape(experts * tok, width), MOE, scatter_dim...]
    psum x2 -> x0, waiting for transfers between devices: 199 us -> none  [the longest x1 116 us: per_device(): lax.psum(jnp.concatenate([router_grad, ffn_gain_grad[None]], axis=0), ALL)]
    dot_general x9 -> x0, matrix products: 161 us -> none  [the longest x2 43.7 us: pick_rows(): lax.dot_general(pick_low, x, (((2,), (1,)), ((0,), (0,))), preferred_elem...]
    all_gather x3 -> x0, waiting for transfers between devices: 157 us -> none  [the longest x1 115 us: per_device(): rows_all = lax.all_gather(ffn_normed, MOE, axis=0, tiled=False)]
    dot_general x7 -> x4, matrix products: 98.3 us -> 16.3 us  [dot_nn(): lax.dot_general(a, b, (((1,), (0,)), ((), ())), preferred_element_type=F32)]
    dot_general x6 -> x3, matrix products: 109 us -> 27 us  [dot_nt(): lax.dot_general(a, b, (((1,), (1,)), ((), ())), preferred_element_type=F32)]
  transfers between devices with their start and end apart: 17 -> 9, of which waited for: 14 -> 2; matrix products, arithmetic and copies ran while one was open for 24% -> 15% of each run, Pallas kernels for 0% -> 34%
where the time goes in v2:
time: 1220 us; the launch traced here: 1210 us
  Pallas kernels  784 us (64%)
  matrix products  134 us (11%)
  waiting for transfers between devices  102 us (8%)
  other arithmetic  67.6 us (6%)
  blocking collectives  55.5 us (5%)
  local copies, waits for them, and re-layouts  33.1 us (3%)
  starting transfers between devices  17.2 us (1%)
  between operations  15.4 us (1%)
    pallas_call x1, Pallas kernels, tail(): pl.pallas_call(functools.partial(tail_kernel, N, C, E), out_shape=[jax.Sh...  176 us
    pallas_call x1, Pallas kernels, fwd_call(): pl.pallas_call(body, out_shape=out_shape, in_specs=[A] * 6, out_specs=[A]...  174 us
    pallas_call x1, Pallas kernels, part(): pl.pallas_call(functools.partial(back_kernel, H, E, cap), out_shape=jax.S...  165 us
    pallas_call x2, Pallas kernels, ag_ctx(): pl.pallas_call(functools.partial(ag_ctx_kernel, H, Q), out_shape=jax.Shap...  99.9 us
    dot_general x6, matrix products, dot_tn(): lax.dot_general(a, b, (((0,), (0,)), ((), ())), preferred_element_type=F32)  90.8 us
    all_gather x1, waiting for transfers between devices, per_device(): cot_all = lax.all_gather(cot, MOE, axis=0, tiled=False)  68.2 us
    pallas_call x1, Pallas kernels, attn_bwd(): pl.pallas_call(functools.partial(attn_bwd_kernel, heads, bq, HEAD ** (-0....  53.4 us
    pallas_call x1, Pallas kernels, attn_fwd(): pl.pallas_call(functools.partial(attn_fwd_kernel, heads, bq, HEAD ** (-0....  41.7 us
  transfers between devices with their start and end apart: 9, of which 2 were waited for; matrix products, arithmetic and copies ran while one was open for 15% of the time, Pallas kernels for 34%

profile of v2, /device:TPU:8, one launch (start us, length us, event | category | flops | bytes accessed | tf_op | source)
XLA Modules:
  0.0 1208.6 jit_solution(708821368639472980)
XLA Ops:
  12.5 14.3 %all_to_all.25 = bf16[4,64,3,2,256]{4,3,2,1,0:T(2,128)(2,1)S(1)} all-to-all(bf16[4,64,3,2,256]{4,3,2,1,0:T(2,128)(2,1)S(1)} %maximum_bitcast_fusion), channel_id=1, replica_groups=mesh['dp'=2,'ctx'=4,'exp'=4] {'ctx'}, dimensions={0} | all-to-all | bytes 1572864 | tf_op jit(solution)/shard_map/all_to_all | solution.py:702
  43.5 49.0 %ag_ctx.2 = bf16[4,384,2048]{2,1,0:T(8,128)(2,1)} custom-call(bf16[384,2048]{1,0:T(8,128)(2,1)} %fusion.3.x), custom_call_target="tpu_custom_call" | custom-call | tf_op jit(solution)/shard_map/ag_ctx/pallas_call | solution.py:603
  94.3 31.9 %all-gather.5.cloned.1.call-done = bf16[2048,1536]{1,0:T(8,128)(2,1)} async-done(((bf16[256,1536]{1,0:T(8,128)(2,1)}), bf16[2048,1536]{1,0:T(8,128)(2,1)}) %all-gather.5.cloned.1.call-update) | async-done | bytes 6291472 | tf_op jit(solution)/shard_map/all_gather | solution.py:704
  130.8 10.1 fusion.32.raw
  146.1 20.7 %psum.14 = f32[2,1536]{0,1:T(8,128)} all-reduce(f32[2,1536]{0,1:T(8,128)} %copy.80), channel_id=1, replica_groups=mesh['dp'=2,'ctx'=4,'exp'=4] {'ctx'}, use_global_device_ids=true, to_apply=%region_3.4 | all-reduce | flops 3072 | bytes 24576 | tf_op jit(solution)/shard_map/psum | solution.py:746
  168.9 41.7 %attn_fwd.1 = (bf16[1536,512]{1,0:T(8,128)(2,1)S(1)}, bf16[1536,512]{1,0:T(8,128)(2,1)}, bf16[1536,512]{1,0:T(8,128)(2,1)}, bf16[1536,512]{1,0:T(8,128)(2,1)}) custom-call(f32[1536,1536]{1,0:T(8,128)} %copy-done.19, f32[1536,2]{1,0:T(8,128)S(1)} %get-tuple-element.106.rr, f32[1536,128]{1,0:T(8,128)S(1)} %get-tuple-element.121.cos, ...), custom_call_target="tpu_custom_call" | custom-call | flops 4831838208 | bytes 15728640 | tf_op jit(solution)/shard_map/attn_fwd/pallas_call | solution.py:515
  217.3 38.3 %rs_ctx.1 = bf16[384,2048]{1,0:T(8,128)(2,1)S(1)} custom-call(bf16[4,384,2048]{2,1,0:T(8,128)(2,1)S(1)} %bitcast.128), custom_call_target="tpu_custom_call" | custom-call | tf_op jit(solution)/shard_map/rs_ctx/pallas_call | solution.py:638
  260.7 68.2 %all-gather.9.cloned.1.call-done = bf16[16,1,384,2048]{3,2,1,0:T(8,128)(2,1)} async-done(((bf16[1,1,384,2048]{3,2,1,0:T(8,128)(2,1)}), bf16[16,1,384,2048]{3,2,1,0:T(8,128)(2,1)}) %all-gather.9.cloned.1.call-update) | async-done | bytes 25165840 | tf_op jit(solution)/shard_map/all_gather | solution.py:722
  328.9 173.7 %experts_fwd.1 = (bf16[16,240,2048]{2,1,0:T(8,128)(2,1)}, bf16[16,240,1024]{2,1,0:T(8,128)(2,1)}, bf16[16,240,2048]{2,1,0:T(8,128)(2,1)}, bf16[16,240,1024]{2,1,...) custom-call(s32[16,384]{1,0:T(8,128)} %bitcast.153, ...), custom_call_target="tpu_custom_call" | custom-call | flops 82543902720 | bytes 117964800 | tf_op jit(solution)/shard_map/experts_fwd/pallas_call | solution.py:467
  502.7 165.4 %back.1 = bf16[384,2048]{1,0:T(8,128)(2,1)} custom-call(s32[16,384]{1,0:T(8,128)} %bitcast.154, bf16[16,240,1024]{2,1,0:T(8,128)(2,1)} %get-tuple-element.59.dgp, bf16[16,240,1024]{2,1,0:T(8,128)(2,1)} %get-tuple-element.60.dup, bf16[2048,1024]{1,0:T(8,128)(2,1)} %bitcast.166, bf16[2048,1024]{1,0:T(8,128)(2,1)} %bitcast.168), custom_call_target="tpu_custom_call" | custom-call | flops 38252052480 | bytes 15728640 | tf_op jit(solution)/shard_map/back/pallas_call | solution.py:311
  678.1 26.3 %bitcast_convert_fusion.1 = bf16[2048,1024]{1,0:T(8,128)(2,1)} fusion(bf16[16,240,2048]{2,1,0:T(8,128)(2,1)} %get-tuple-element.68, bf16[16,240,1024]{2,1,0:T(8,128)(2,1)} %get-tuple-element.60.dup), kind=kOutput, calls=%fused_computation.2 | convolution fusion | flops 16108224512 | bytes 27787264 | tf_op jit(solution)/shard_map/dot_general | solution.py:648
  704.4 22.8 %bitcast_convert_fusion.2 = bf16[2048,1024]{1,0:T(8,128)(2,1)} fusion(bf16[16,240,2048]{2,1,0:T(8,128)(2,1)} %get-tuple-element.68, bf16[16,240,1024]{2,1,0:T(8,128)(2,1)} %get-tuple-element.59.dgp), kind=kOutput, calls=%fused_computation.3 | convolution fusion | flops 16108224512 | bytes 27787264 | tf_op jit(solution)/shard_map/dot_general | solution.py:648
  727.3 19.9 %bitcast_convert_fusion = bf16[1024,2048]{1,0:T(8,128)(2,1)} fusion(bf16[16,240,1024]{2,1,0:T(8,128)(2,1)S(1)} %bitcast.172, bf16[16,240,2048]{2,1,0:T(8,128)(2,1)S(1)} %bitcast.170), kind=kOutput, calls=%fused_computation.1 | convolution fusion | flops 16108224512 | bytes 27787264 | tf_op jit(solution)/shard_map/dot_general | solution.py:648
  758.5 50.9 %ag_ctx.3 = bf16[4,384,2048]{2,1,0:T(8,128)(2,1)} custom-call(bf16[384,2048]{1,0:T(8,128)(2,1)} %fusion.25.x), custom_call_target="tpu_custom_call" | custom-call | tf_op jit(solution)/shard_map/ag_ctx/pallas_call | solution.py:603
  809.5 8.4 convolution_convert_fusion.4.dm
  817.9 53.4 %attn_bwd.1 = (f32[1536,512]{1,0:T(8,128)}, f32[1536,512]{1,0:T(8,128)}, bf16[1536,512]{1,0:T(8,128)(2,1)S(1)}) custom-call(bf16[1536,512]{1,0:T(8,128)(2,1)S(1)} %copy-done.12, bf16[1536,512]{1,0:T(8,128)(2,1)} %get-tuple-element.56.k, bf16[1536,512]{1,0:T(8,128)(2,1)} %get-tuple-element.57.v, bf16[1536,512]{1,0:T(8,128)(2,1)} %convolution_convert_fusion.4.dm, ...), custom_call_target="tpu_custom_call" | custom-call | flops 12079595520 | bytes 15728640 | tf_op jit(solution)/shard_map/attn_bwd/pallas_call | solution.py:558
  877.8 20.5 %psum.15 = f32[2,1536]{0,1:T(8,128)} all-reduce(f32[2,1536]{0,1:T(8,128)S(1)} %copy.85), channel_id=1, replica_groups=mesh['dp'=2,'ctx'=4,'exp'=4] {'ctx'}, use_global_device_ids=true, to_apply=%region_14.15 | all-reduce | flops 3072 | bytes 24576 | tf_op jit(solution)/shard_map/psum | solution.py:806
  914.8 15.2 %convolution_convert_fusion = bf16[1536,2048]{1,0:T(8,128)(2,1)} fusion(bf16[1536,1536]{1,0:T(8,128)(2,1)} %pad_maximum_fusion, bf16[2048,1536]{1,0:T(8,128)(2,1)} %bitcast.136), kind=kOutput, calls=%fused_computation.7 | convolution fusion | flops 9666822144 | bytes 17301504 | tf_op jit(solution)/shard_map/dot_general | solution.py:652
  930.0 15.2 %convolution_convert_fusion.1 = bf16[2048,1536]{1,0:T(8,128)(2,1)} fusion(bf16[1536,2048]{1,0:T(8,128)(2,1)} %bitcast.139, bf16[1536,1536]{1,0:T(8,128)(2,1)} %pad_maximum_fusion), kind=kOutput, calls=%fused_computation.8 | convolution fusion | flops 9666822144 | bytes 17301504 | tf_op jit(solution)/shard_map/dot_general | solution.py:648
  945.2 176.0 %tail.1 = (bf16[4,64,1536]{2,1,0:T(8,128)(2,1)}, bf16[64,2048]{1,0:T(8,128)(2,1)}, bf16[384,2048]{1,0:T(8,128)(2,1)}) custom-call(bf16[2,4,4,64,1536]{4,3,2,1,0:T(8,128)(2,1)} %bitcast.134, bf16[2,4,64,2048]{3,2,1,0:T(8,128)(2,1)} %bitcast.145, bf16[4,384,2048]{2,1,0:T(8,128)(2,1)} %bitcast.133), custom_call_target="tpu_custom_call" | custom-call | tf_op jit(solution)/shard_map/tail/pallas_call | solution.py:159
  1124.8 35.8 %sums.1 = f32[24,2048]{1,0:T(8,128)S(1)} custom-call(f32[24,2048]{1,0:T(8,128)S(1)} %select_maximum_fusion.x_ref), custom_call_target="tpu_custom_call" | custom-call | tf_op jit(solution)/shard_map/sums/pallas_call | solution.py:192
  1170.9 8.8 add_bitcast_fusion.2
  1179.7 8.8 add_bitcast_fusion.1
  1188.6 9.0 add_bitcast_fusion
  (240 shorter events, 109.0 us)
Async XLA Ops:
  7.2 250.4 %copy-start = (bf16[2048,16]{0,1:T(8,128)(2,1)S(1)}, bf16[2048,16]{0,1:T(8,128)(2,1)}, u32[]{:S(2)}) copy-start(bf16[2048,16]{0,1:T(8,128)(2,1)} %param.29) | copy-start | bytes 196612
  7.2 119.0 %all-gather.5.cloned.1.call-start = ((), (), s32[]{:S(2)}) async-start(), calls=%async_computation.4 | async-start | bytes 7077888 | tf_op jit(solution)/shard_map/all_gather | solution.py:704
  12.4 23.7 %copy-start.13 = (bf16[1,1,384,2048]{3,2,1,0:T(8,128)(2,1)S(1)}, bf16[1,1,384,2048]{3,2,1,0:T(8,128)(2,1)}, u32[]{:S(2)}) copy-start(bf16[1,1,384,2048]{3,2,1,0:T(8,128)(2,1)} %param.18) | copy-start | bytes 4718596
  28.2 183.5 %all-gather.7.cloned.1.call-start = ((), (), s32[]{:S(2)}) async-start(), calls=%async_computation.5 | async-start | bytes 2359296 | tf_op jit(solution)/shard_map/all_gather | solution.py:710
  29.0 300.0 %all-gather.9.cloned.1.call-start = ((), (), s32[]{:S(2)}) async-start(), calls=%async_computation.7 | async-start | bytes 26738688 | tf_op jit(solution)/shard_map/all_gather | solution.py:722
  30.6 63.1 %all-to-all-start.1 = ((s32[16,1,384]{2,1,0:T(1,128)}), s32[16,1,384]{2,1,0:T(1,128)S(1)}, u32[]{:S(2)}, u32[]{:S(2)}) async-start(s32[16,1,384]{2,1,0:T(1,128)} %copy.83), calls=%async_computation.1 | async-start | bytes 49152 | tf_op jit(solution)/shard_map/all_to_all | solution.py:719
  35.9 878.8 %reduce-scatter.2.cloned.1.call-start = ((), (), s32[]{:S(2)}) async-start(), calls=%async_computation.6 | async-start | bytes 26738688 | tf_op jit(solution)/shard_map/reduce_scatter | solution.py:775
  41.6 127.4 %copy-start.7 = (f32[1536,128]{1,0:T(8,128)}, f32[1536,128]{1,0:T(8,128)S(1)}, u32[]{:S(2)}) copy-start(f32[1536,128]{1,0:T(8,128)S(1)} %get-tuple-element.121.cos) | copy-start | bytes 2359300
  43.2 213.6 %copy-start.38 = (f32[2048]{0:T(1024)}, f32[2048]{0:T(1024)S(1)}, u32[]{:S(2)}) copy-start(f32[2048]{0:T(1024)S(1)} %convert_element_type.151) | copy-start | bytes 24580
  43.5 125.4 %copy-start.5 = (s32[1536,1]{1,0:T(8,128)}, s32[1536,1]{1,0:T(8,128)S(1)}, u32[]{:S(2)}) copy-start(s32[1536,1]{1,0:T(8,128)S(1)} %copy.82.lab_c) | copy-start | bytes 18436
  217.3 38.3 %copy-start.15 = (bf16[1,1,384,2048]{3,2,1,0:T(8,128)(2,1)S(1)}, bf16[1,1,384,2048]{3,2,1,0:T(8,128)(2,1)}, u32[]{:S(2)}) copy-start(bf16[1,1,384,2048]{3,2,1,0:T(8,128)(2,1)} %param.18) | copy-start | bytes 4718596
  258.2 244.5 %copy-start.40 = (f32[384]{0:T(512)}, f32[384]{0:T(512)S(1)}, u32[]{:S(2)}) copy-start(f32[384]{0:T(512)S(1)} %get-tuple-element.118) | copy-start | bytes 4612
  258.8 243.9 %copy-start.42 = (f32[384]{0:T(512)}, f32[384]{0:T(512)S(1)}, u32[]{:S(2)}) copy-start(f32[384]{0:T(512)S(1)} %fusion.21) | copy-start | bytes 4612
  669.9 80.8 %all-to-all-start.2 = ((f32[16,1,384]{2,1,0:T(1,128)}), f32[16,1,384]{2,1,0:T(1,128)S(1)}, u32[]{:S(2)}, u32[]{:S(2)}) async-start(f32[16,1,384]{2,1,0:T(1,128)} %get-tuple-element.62), calls=%async_computation.2 | async-start | bytes 49152 | tf_op jit(solution)/shard_map/all_to_all | solution.py:770
  678.1 49.1 %slice-start.2 = ((s8[15728640]{0:T(1024)(128)(4,1)}), s8[4194304]{0:T(1024)(128)(4,1)S(1)}, s32[]{:S(2)}) async-start(s8[15728640]{0:T(1024)(128)(4,1)} %bitcast.169), calls=%async_computation.10 | async-start | bytes 8388608
  678.1 49.1 %slice-start.3 = ((s8[15728640]{0:T(1024)(128)(4,1)}), s8[4194304]{0:T(1024)(128)(4,1)S(1)}, s32[]{:S(2)}) async-start(s8[15728640]{0:T(1024)(128)(4,1)} %bitcast.169), calls=%async_computation.11 | async-start | bytes 8388608
  678.1 49.1 %slice-start.6 = ((s8[7864320]{0:T(1024)(128)(4,1)}), s8[4194304]{0:T(1024)(128)(4,1)S(1)}, s32[]{:S(2)}) async-start(s8[7864320]{0:T(1024)(128)(4,1)} %bitcast.171), calls=%async_computation.14 | async-start | bytes 8388608
  747.2 376.0 %collective-permute-start.2 = (bf16[1024,2048]{1,0:T(8,128)(2,1)}, bf16[1024,2048]{1,0:T(8,128)(2,1)}, u32[]{:S(2)}, u32[]{:S(2)}) collective-permute-start(bf16[1024,2048]{1,0:T(8,128)(2,1)} %bitcast_convert_fusion), channel_id=1, source_target_pairs={{0,16},{16,0},{1,17},{17,1},{2,18},{18,2},{3,19},{19,3},{4,20},{20... | collective-permute-start | bytes 12582920 | tf_op jit(solution)/shard_map/ppermute | solution.py:659
  748.8 374.4 %collective-permute-start = (bf16[2048,1024]{1,0:T(8,128)(2,1)}, bf16[2048,1024]{1,0:T(8,128)(2,1)}, u32[]{:S(2)}, u32[]{:S(2)}) collective-permute-start(bf16[2048,1024]{1,0:T(8,128)(2,1)} %bitcast_convert_fusion.2), channel_id=1, source_target_pairs={{0,16},{16,0},{1,17},{17,1},{2,18},{18,2},{3,19},{19,3},{4,20},{20... | collective-permute-start | bytes 12582920 | tf_op jit(solution)/shard_map/ppermute | solution.py:659
  749.3 373.9 %collective-permute-start.1 = (bf16[2048,1024]{1,0:T(8,128)(2,1)}, bf16[2048,1024]{1,0:T(8,128)(2,1)}, u32[]{:S(2)}, u32[]{:S(2)}) collective-permute-start(bf16[2048,1024]{1,0:T(8,128)(2,1)} %bitcast_convert_fusion.1), channel_id=1, source_target_pairs={{0,16},{16,0},{1,17},{17,1},{2,18},{18,2},{3,19},{19,3},{4,20},{20... | collective-permute-start | bytes 12582920 | tf_op jit(solution)/shard_map/ppermute | solution.py:659
  817.8 53.4 %copy-start.49 = (f32[2,1,256]{2,1,0:T(1,128)S(1)}, f32[2,1,256]{2,1,0:T(1,128)}, u32[]{:S(2)}) copy-start(f32[2,1,256]{2,1,0:T(1,128)} %copy-done.48) | copy-start | bytes 6148
  817.9 53.4 %copy-start.51 = (f32[2,1,256]{2,1,0:T(1,128)S(1)}, f32[2,1,256]{2,1,0:T(1,128)}, u32[]{:S(2)}) copy-start(f32[2,1,256]{2,1,0:T(1,128)} %copy-done.50) | copy-start | bytes 6148
  1123.1 38.7 %copy-start.35 = (bf16[64,2048]{1,0:T(8,128)(2,1)S(1)}, bf16[64,2048]{1,0:T(8,128)(2,1)}, u32[]{:S(2)}) copy-start(bf16[64,2048]{1,0:T(8,128)(2,1)} %get-tuple-element.75) | copy-start | bytes 786436
  1123.1 39.5 %copy-start.32 = (bf16[4,64,1536]{2,1,0:T(8,128)(2,1)S(1)}, bf16[4,64,1536]{2,1,0:T(8,128)(2,1)}, u32[]{:S(2)}) copy-start(bf16[4,64,1536]{2,1,0:T(8,128)(2,1)} %get-tuple-element.74) | copy-start | bytes 2359300
  (53 other events, 525.8 us)
Sparse Core Ops, SparseCore 0:
  28.3 97.8 all-gather.4
  128.3 48.9 all-gather.6
  178.9 150.0 all-gather.8
  668.2 244.6 reduce-scatter.1

commit v3 on v2

--- a/solution.py
+++ b/solution.py
@@ -54,7 +54,7 @@
         add_into(dst.at[i],src.at[i]); return 0
     lax.fori_loop(0,dst.shape[0],body,0)
 
-def tail_kernel(N,C,E,gq,go,dn,oq,oo,od,own_q,own_o,own_d,yq,yo,uq,uo,vq,vo,d1,d2,ld,ldd,ys,yr,zs,zu,zd,s1,r1,s2,r2,a_s,a_r,osem):
+def tail_kernel(N,C,E,gq,go,dn,hid,dres,gain,sm,oq,oo,od,osm,own_q,own_o,own_d,yq,yo,uq,uo,vq,vo,d1,d2,ld,ldd,ys,yr,zs,zu,zd,s1,r1,s2,r2,a_s,a_r,osem,hv,rv,gv,b0,b1,b2,t_s,t_r):
     p=lax.axis_index("dp"); c=lax.axis_index("ctx"); e=lax.axis_index("exp")
     H=C//2; h=c//2; l=c%2
     def dpeer(j): return lax.rem(p+j,N)
@@ -64,10 +64,7 @@
     def sig(**kw): pl.semaphore_signal(bar,inc=1,device_id=kw,device_id_type=MESH)
     for j in range(1,N): sig(dp=dpeer(j))
     for j in range(1,C): sig(ctx=cpeer(j))
-    @pl.when(e>0)
-    def _(): sig(exp=e-1)
-    @pl.when(e<E-1)
-    def _(): sig(exp=e+1)
+    for j in range(1,E): sig(exp=lax.rem(e+j,E))
     order=by_distance(e,E)
     def rc(src,dst,ss,rs,**kw): return pltpu.make_async_remote_copy(src,dst,ss,rs,device_id=kw,device_id_type=MESH)
     def loads(o): return [pltpu.make_async_copy(gq.at[p,:,o],own_q.at[o],ld.at[0,o]),pltpu.make_async_copy(go.at[p,o],own_o.at[o],ld.at[1,o])]
@@ -83,9 +80,11 @@
     hs=[hpeer(j) for j in range(1,H)]+[h]
     def start_loads(k):
         for x in loads(k): x.start()
+    side=[pltpu.make_async_copy(hid,hv,osem.at[3]),pltpu.make_async_copy(dres,rv,osem.at[4]),pltpu.make_async_copy(gain,gv,osem.at[5]),pltpu.make_async_copy(sm,b0.at[p],osem.at[6])]
+    for x in side: x.start()
     loop(E,start_loads)
     for hh in hs: loadd(hh).start()
-    pl.semaphore_wait(bar,(N-1)+(C-1)+(e>0).astype(jnp.int32)+(e<E-1).astype(jnp.int32))
+    pl.semaphore_wait(bar,(N-1)+(C-1)+(E-1))
     for j in range(1,N):
         for x in cy(j,order(0)): x.start()
     for hh in hs: c1(hh).start()
@@ -117,13 +116,45 @@
                     for x in cd(o): x.wait_recv()
                     add3(own_q.at[o],vq.at[o]); add3(own_o.at[o],vo.at[o])
                 for x in cd(o): x.start()
+    small=((b0,"dp",N,p),(b1,"ctx",C,c),(b2,"exp",E,e))
+    def hop(t,j):
+        b,a,n,i=small[t]
+        return rc(b.at[i],b.at[i],t_s.at[t,j-1],t_r.at[t,j-1],**{a:lax.rem(i+j,n)})
+    def gathered(t):
+        b,a,n,i=small[t]
+        for j in range(1,n):
+            q=lax.rem(i+n-j,n)
+            rc(b.at[q],b.at[q],t_s.at[t,j-1],t_r.at[t,j-1],**{a:q}).wait_recv()
+        x=b[0]
+        for j in range(1,n): x=x+b[j]
+        return x
+    def send(t):
+        for j in range(1,small[t][2]): hop(t,j).start()
+    T,D=hv.shape; RB=16
+    lastrow=b0.shape[1]-1
+    def epilogue(i):
+        sl=pl.ds(pl.multiple_of(i*RB,RB),RB)
+        d=own_d[h,sl,:].astype(F32); x=hv[sl,:].astype(F32)
+        r=lax.rsqrt(jnp.mean(x*x,axis=1,keepdims=True)+EPS)
+        b0[p,lastrow:,:]+=jnp.sum(d*x*r,axis=0,keepdims=True)
+        w=d*gv[...]
+        own_d[h,sl,:]=(rv[sl,:]+(w*r-x*(r*r*r)*jnp.mean(x*w,axis=1,keepdims=True))).astype(BF)
     def lines(k):
         line(k)
         @pl.when(k==0)
         def _():
             for j in range(1,H):
                 c2(j).wait_recv(); add_into(own_d.at[h],d2.at[j-1])
+            for x in side: x.wait()
+            loop(T//RB,epilogue)
+            send(0)
             pltpu.make_async_copy(own_d.at[h],od,osem.at[0]).start()
+        @pl.when(k==1)
+        def _():
+            b1[c]=gathered(0); send(1)
+        @pl.when(k==2)
+        def _():
+            b2[e]=gathered(1); send(2)
     loop(E,lines)
     @pl.when(e>0)
     def _():
@@ -151,49 +182,25 @@
         ca(j).wait_send();
         src=lax.rem(c+C-j,C)
         rc(own_q.at[e,c],oq.at[src],a_s.at[j-1],a_r.at[j-1],ctx=src).wait_recv()
-    pltpu.make_async_copy(own_d.at[h],od,osem.at[0]).wait(); l1.wait(); l2.wait()
-
-def tail(gq,go,dn,cid=2):
-    N,C,E,S,W3=gq.shape; D=go.shape[-1]; T=dn.shape[1]; H=C//2
-    dma=pltpu.SemaphoreType.DMA; V=lambda *s: pltpu.VMEM(s,BF)
+    for t in range(3):
+        for j in range(1,small[t][2]): hop(t,j).wait_send()
+    b0[0]=gathered(2)
+    so=pltpu.make_async_copy(b0.at[0],osm,osem.at[7]); so.start()
+    pltpu.make_async_copy(own_d.at[h],od,osem.at[0]).wait(); l1.wait(); l2.wait(); so.wait()
+
+def tail(gq,go,dn,hid,dres,gain,sm,cid=2):
+    N,C,E,S,W3=gq.shape; D=go.shape[-1]; T=dn.shape[1]; H=C//2; R=sm.shape[0]
+    dma=pltpu.SemaphoreType.DMA; V=lambda *s: pltpu.VMEM(s,BF); FV=lambda *s: pltpu.VMEM(s,F32)
+    M=max(N,C,E)-1
     return pl.pallas_call(functools.partial(tail_kernel,N,C,E),
-        out_shape=[jax.ShapeDtypeStruct((C,S,W3),BF),jax.ShapeDtypeStruct((S,D),BF),jax.ShapeDtypeStruct((T,D),BF)],
-        in_specs=[pl.BlockSpec(memory_space=pl.ANY)]*3,
-        out_specs=[pl.BlockSpec(memory_space=pl.ANY)]*3,
+        out_shape=[jax.ShapeDtypeStruct((C,S,W3),BF),jax.ShapeDtypeStruct((S,D),BF),jax.ShapeDtypeStruct((T,D),BF),jax.ShapeDtypeStruct((R,D),F32)],
+        in_specs=[pl.BlockSpec(memory_space=pl.ANY)]*7,
+        out_specs=[pl.BlockSpec(memory_space=pl.ANY)]*4,
         scratch_shapes=[V(E,C,S,W3),V(E,S,D),V(H,T,D),V(N-1,E,C,S,W3),V(N-1,E,S,D),V(E,C,S,W3),V(E,S,D),V(E,C,S,W3),V(E,S,D),V(H,T,D),V(H-1,T,D),
-            dma((2,E)),dma((H,)),dma((2,N-1,E)),dma((2,N-1,E)),dma((2,E)),dma((2,E)),dma((2,E)),dma((H,)),dma((H,)),dma((H-1,)),dma((H-1,)),dma((C-1,)),dma((C-1,)),dma((3,))],
-        compiler_params=pltpu.CompilerParams(collective_id=cid,has_side_effects=True,vmem_limit_bytes=60*2**20),
-        name="tail")(gq,go,dn)
-
-def sums_kernel(sizes,x_ref,o_ref,*scr):
-    names=("dp","ctx","exp")
-    bufs=scr[:3]; ss=scr[3:6]; rs=scr[6:9]
-    bar=pltpu.get_barrier_semaphore(); cnt=0
-    me=[lax.axis_index(a) for a in names]
-    for a,n,i in zip(names,sizes,me):
-        for j in range(1,n):
-            pl.semaphore_signal(bar,inc=1,device_id={a:lax.rem(i+j,n)},device_id_type=MESH); cnt+=1
-    pl.semaphore_wait(bar,cnt)
-    for t,(a,n,i) in enumerate(zip(names,sizes,me)):
-        buf=bufs[t]
-        buf[i]=x_ref[...] if t==0 else o_ref[...]
-        def cp(j): return pltpu.make_async_remote_copy(buf.at[i],buf.at[i],ss[t].at[j-1],rs[t].at[j-1],device_id={a:lax.rem(i+j,n)},device_id_type=MESH)
-        for j in range(1,n): cp(j).start()
-        for j in range(1,n):
-            src=lax.rem(i+n-j,n)
-            pltpu.make_async_remote_copy(buf.at[src],buf.at[src],ss[t].at[j-1],rs[t].at[j-1],device_id={a:src},device_id_type=MESH).wait_recv()
-        acc=buf[0]
-        for j in range(1,n): acc=acc+buf[j]
-        o_ref[...]=acc
-        for j in range(1,n): cp(j).wait_send()
-
-def sums(x,sizes,cid=3):
-    R,D=x.shape; dma=pltpu.SemaphoreType.DMA
-    return pl.pallas_call(functools.partial(sums_kernel,sizes),out_shape=jax.ShapeDtypeStruct((R,D),F32),
-        in_specs=[pl.BlockSpec(memory_space=pltpu.VMEM)],out_specs=pl.BlockSpec(memory_space=pltpu.VMEM),
-        scratch_shapes=[pltpu.VMEM((n,R,D),F32) for n in sizes]+[dma((n-1,)) for n in sizes]*2,
-        compiler_params=pltpu.CompilerParams(collective_id=cid,has_side_effects=True,vmem_limit_bytes=32*2**20),name="sums")(x)
-
+            dma((2,E)),dma((H,)),dma((2,N-1,E)),dma((2,N-1,E)),dma((2,E)),dma((2,E)),dma((2,E)),dma((H,)),dma((H,)),dma((H-1,)),dma((H-1,)),dma((C-1,)),dma((C-1,)),dma((8,)),
+            V(T,D),FV(T,D),FV(1,D),FV(N,R,D),FV(C,R,D),FV(E,R,D),dma((3,M)),dma((3,M))],
+        compiler_params=pltpu.CompilerParams(collective_id=cid,has_side_effects=True,vmem_limit_bytes=61*2**20),
+        name="tail")(gq,go,dn,hid,dres,gain,sm)
 
 def nn(a,b): return lax.dot_general(a,b,(((1,),(0,)),((),())),preferred_element_type=F32)
 def tn(a,b): return lax.dot_general(a,b,(((0,),(0,)),((),())),preferred_element_type=F32)
@@ -203,7 +210,9 @@
     T=slot_row.shape[1]
     return jnp.broadcast_to(slot_row,(cap,T))==lax.broadcasted_iota(jnp.int32,(cap,T),0)
 
-def back_kernel(H,E,cap,slot,dgp,dup,gw,uw,o_ref,own,r1,r2,rz,snd,gb,ub,slv,wg,wu,ld_sem,w_sem,s1,q1,s2,q2,s3,qz,o_sem):
+def back_kernel(H,E,cap,X,slot,dgp,dup,gw,uw,*rest):
+    ex_in,o_ref,ex_out=rest[:X],rest[X],rest[X+1:2*X+1]
+    own,r1,r2,rz,snd,gb,ub,slv,wg,wu,ld_sem,w_sem,s1,q1,s2,q2,s3,qz,o_sem=rest[2*X+1:2*X+20]
     c=lax.axis_index("ctx"); e=lax.axis_index("exp")
     h=c//2; l=c%2
     T,W=own.shape[2:]; FF=wg.shape[1]
@@ -217,6 +226,10 @@
     def _(): pl.semaphore_signal(bar,inc=1,device_id={"exp":e-1},device_id_type=MESH)
     @pl.when(e<E-1)
     def _(): pl.semaphore_signal(bar,inc=1,device_id={"exp":e+1},device_id_type=MESH)
+    def ex(i):
+        es,er=rest[2*X+20:]
+        return pltpu.make_async_remote_copy(ex_in[i],ex_out[i],es.at[i],er.at[i],device_id={"dp":1-lax.axis_index("dp")},device_id_type=MESH)
+    if X: pl.semaphore_signal(bar,inc=1,device_id={"dp":1-lax.axis_index("dp")},device_id_type=MESH)
     order=by_distance(e,E)
     wl=[pltpu.make_async_copy(gw,wg,w_sem.at[0]),pltpu.make_async_copy(uw,wu,w_sem.at[1])]
     for x in wl: x.start()
@@ -250,7 +263,8 @@
         loop(W//step,body)
     pltpu.sync_copy(slot,slv)
     for x in wl: x.wait()
-    pl.semaphore_wait(bar,H+(e>0).astype(jnp.int32)+(e<E-1).astype(jnp.int32))
+    pl.semaphore_wait(bar,H+min(X,1)+(e>0).astype(jnp.int32)+(e<E-1).astype(jnp.int32))
+    for i in range(X): ex(i).start()
     def zstep(k):
         o=order(k)
         for j in range(1,H):
@@ -297,28 +311,34 @@
         def _(): cz(order(k),e,order(k)).wait_send()
     loop(E,drain)
     out.wait()
-
-
-def back_call(slot,dgp,dup,gw,uw,C,E,T,cids):
+    for i in range(X): ex(i).wait()
+
+
+def back_call(slot,dgp,dup,gw,uw,swap,C,E,T,cids):
     S,cap,FF=dgp.shape; D=gw.shape[0]; H=C//2
     dma=pltpu.SemaphoreType.DMA; V=lambda *s: pltpu.VMEM(s,BF)
     blocks=2*H*E+(H-1)*E+E+4
     parts=1
     while 2*(blocks*T*D//parts+2*D//parts*FF+4*cap*FF)>60*2**20: parts*=2
     W=D//parts
+    A=pl.BlockSpec(memory_space=pl.ANY)
     def part(i):
         a,b=(gw,uw) if parts==1 else (gw[i*W:(i+1)*W],uw[i*W:(i+1)*W])
-        return pl.pallas_call(functools.partial(back_kernel,H,E,cap),
-            out_shape=jax.ShapeDtypeStruct((T,W),BF),
-            in_specs=[pl.BlockSpec(memory_space=pl.ANY)]*5,
-            out_specs=pl.BlockSpec(memory_space=pl.ANY),
+        ex=tuple(swap) if i==0 else ()
+        X=len(ex)
+        return pl.pallas_call(functools.partial(back_kernel,H,E,cap,X),
+            out_shape=[jax.ShapeDtypeStruct((T,W),BF)]+[jax.ShapeDtypeStruct(g.shape,g.dtype) for g in ex],
+            in_specs=[A]*(5+X),
+            out_specs=[A]*(1+X),
             scratch_shapes=[V(H,E,T,W),V(H,E,T,W),V(H-1,E,T,W),V(E+1,T,W),V(3,T,W),V(2,cap,FF),V(2,cap,FF),pltpu.VMEM((S,T),jnp.int32),V(W,FF),V(W,FF),
-                dma((2,2)),dma((2,)),dma((H*E,)),dma((H,E)),dma((H-1,E)),dma((H-1,E)),dma((E,)),dma((E+1,)),dma(())],
+                dma((2,2)),dma((2,)),dma((H*E,)),dma((H,E)),dma((H-1,E)),dma((H-1,E)),dma((E,)),dma((E+1,)),dma(())]+([dma((X,)),dma((X,))] if X else []),
             cost_estimate=pl.CostEstimate(flops=2*S*cap*(2*W*FF+T*W),bytes_accessed=S*4*cap*FF,transcendentals=0),
             compiler_params=pltpu.CompilerParams(collective_id=cids[i],has_side_effects=True,vmem_limit_bytes=61*2**20),
-            name="back")(slot,dgp,dup,a,b)
+            name="back")(slot,dgp,dup,a,b,*ex)
     out=[part(i) for i in range(parts)]
-    return out[0] if parts==1 else jnp.concatenate(out,axis=1)
+    tok=out[0][0] if parts==1 else jnp.concatenate([o[0] for o in out],axis=1)
+    return tok,out[0][1:]
+
 
 def fwd_kernel(H,E,T,cap,in_vmem,slot,rows,cot,gw,uw,dw,recv,hid,dout,dgp,dup,moe,dg,*scr):
     if in_vmem: allr=scr[0]; scr=scr[1:]; rb=None
@@ -478,52 +498,86 @@
     ok=(col<=row)&((lr==0)|(lr==lc))
     return jnp.where(ok,0.0,-1e30).astype(F32)
 
-def attn_fwd_kernel(heads,bq,scale,raw,rr,cos,sin,lab_r,lab_c,gains,qo,ko,vo,mix,bias):
-    G=raw.shape[0]; cols=heads*HEAD
-    rb=min(128,G)
-    def prep(i,_):
-        sl=pl.ds(pl.multiple_of(i*rb,rb),rb)
+def eye_mask():
+    return lax.broadcasted_iota(jnp.int32,(HEAD,HEAD),0)==lax.broadcasted_iota(jnp.int32,(HEAD,HEAD),1)
+
+def to_row(col):
+    return jnp.sum(jnp.where(eye_mask(),jnp.broadcast_to(col,(HEAD,HEAD)),0.0),axis=0,keepdims=True)
+
+def to_col(row):
+    return jnp.sum(jnp.where(eye_mask(),jnp.broadcast_to(row,(HEAD,HEAD)),0.0),axis=1,keepdims=True)
+
+def greet_ctx(C):
+    c=lax.axis_index("ctx"); bar=pltpu.get_barrier_semaphore()
+    for j in range(1,C): pl.semaphore_signal(bar,inc=1,device_id={"ctx":lax.rem(c+j,C)},device_id_type=MESH)
+
+def sum_ctx(C,buf,ss,rs):
+    c=lax.axis_index("ctx")
+    pl.semaphore_wait(pltpu.get_barrier_semaphore(),C-1)
+    def cp(j): return pltpu.make_async_remote_copy(buf.at[c],buf.at[c],ss.at[j-1],rs.at[j-1],device_id={"ctx":lax.rem(c+j,C)},device_id_type=MESH)
+    for j in range(1,C): cp(j).start()
+    for j in range(1,C):
+        q=lax.rem(c+C-j,C)
+        pltpu.make_async_remote_copy(buf.at[q],buf.at[q],ss.at[j-1],rs.at[j-1],device_id={"ctx":q},device_id_type=MESH).wait_recv()
+    acc=buf[0]
+    for j in range(1,C): acc=acc+buf[j]
+    for j in range(1,C): cp(j).wait_send()
+    return acc
+
+def attn_fwd_kernel(C,heads,bq,scale,raw,cos,sin,lab_r,lab_c,gains,qo,ko,vo,mix,inv,bias,buf,ss,rs):
+    G=raw.shape[0]; cols=heads*HEAD; nb=G//HEAD
+    c=lax.axis_index("ctx")
+    greet_ctx(C)
+    def squares(i):
+        sl=pl.ds(pl.multiple_of(i*HEAD,HEAD),HEAD)
+        for t in range(2):
+            v=raw[sl,t*cols:(t+1)*cols]
+            buf[c,pl.ds(t*nb+i,1),:]=to_row(jnp.sum(v*v,axis=1,keepdims=True))
+        vo[sl,:]=raw[sl,2*cols:].astype(BF)
+    loop(nb,squares)
+    inv[...]=lax.rsqrt(sum_ctx(C,buf,ss,rs)/(C*cols)+EPS)
+    def prep(i):
+        sl=pl.ds(pl.multiple_of(i*HEAD,HEAD),HEAD)
         cs,sn=cos[sl,:],sin[sl,:]
         for t,o in ((0,qo),(1,ko)):
-            r=rr[sl,t:t+1]
+            r=to_col(inv[pl.ds(t*nb+i,1),:])
             for hd in range(heads):
                 a=hd*HEAD
                 v=raw[sl,t*cols+a:t*cols+a+HEAD]*r*gains[t:t+1,a:a+HEAD]
                 o[sl,a:a+HEAD]=(v*cs+pltpu.roll(v,HEAD//2,1)*sn).astype(BF)
-        vo[sl,:]=raw[sl,2*cols:].astype(BF)
-        return 0
-    lax.fori_loop(0,G//rb,prep,0)
+    loop(nb,prep)
     def block(i,K):
         rows=pl.ds(pl.multiple_of(i*bq,bq),bq)
         bias[:,:K]=mask_bias(lab_r,lab_c[rows,:],i*bq,bq,K)
-        def head(hd,_):
+        def head(hd):
             ln=pl.ds(pl.multiple_of(hd*HEAD,HEAD),HEAD)
             s=nt(qo[rows,ln],ko[:K,ln])*scale+bias[:,:K]
             p=jnp.exp(s-jnp.max(s,axis=1,keepdims=True))
             pr=(p*(1.0/jnp.sum(p,axis=1,keepdims=True))).astype(BF)
             mix[rows,ln]=nn(pr,vo[:K,ln]).astype(BF)
-            return 0
-        lax.fori_loop(0,heads,head,0)
+        loop(heads,head)
     per=G//bq//3
     for g in range(3):
         loop(per,lambda i,g=g: block(i+g*per,(g+1)*per*bq))
 
-def attn_fwd(raw,rr,cos,sin,lab_r,lab_c,gains,heads,bq=128):
-    G=raw.shape[0]; cols=heads*HEAD
+def attn_fwd(raw,cos,sin,lab_r,lab_c,gains,C,heads,cid,bq=128):
+    G=raw.shape[0]; cols=heads*HEAD; R=2*G//HEAD; dma=pltpu.SemaphoreType.DMA
     o=jax.ShapeDtypeStruct((G,cols),BF)
     V=pl.BlockSpec(memory_space=pltpu.VMEM)
-    return pl.pallas_call(functools.partial(attn_fwd_kernel,heads,bq,HEAD**-0.5),out_shape=[o]*4,in_specs=[V]*7,out_specs=[V]*4,
-        scratch_shapes=[pltpu.VMEM((bq,G),F32)],
+    return pl.pallas_call(functools.partial(attn_fwd_kernel,C,heads,bq,HEAD**-0.5),out_shape=[o]*4+[jax.ShapeDtypeStruct((R,HEAD),F32)],in_specs=[V]*6,out_specs=[V]*5,
+        scratch_shapes=[pltpu.VMEM((bq,G),F32),pltpu.VMEM((C,R,HEAD),F32),dma((C-1,)),dma((C-1,))],
         cost_estimate=pl.CostEstimate(flops=2*2*heads*G*G*HEAD,bytes_accessed=G*cols*20,transcendentals=heads*G*G),
-        compiler_params=pltpu.CompilerParams(vmem_limit_bytes=48*2**20),name="attn_fwd")(raw,rr,cos,sin,lab_r,lab_c,gains)
-
-def attn_bwd_kernel(heads,bq,scale,q,k,v,dm,cos,sin,lab_r,lab_c,dq,dk,dv,bias,ak,av):
-    G=q.shape[0]
+        compiler_params=pltpu.CompilerParams(collective_id=cid,has_side_effects=True,vmem_limit_bytes=48*2**20),name="attn_fwd")(raw,cos,sin,lab_r,lab_c,gains)
+
+def attn_bwd_kernel(C,heads,bq,scale,q,k,v,dm,raw,inv,cos,sin,lab_r,lab_c,gains,draw,gsum,bias,aq,ak,av,buf,ss,rs):
+    G=q.shape[0]; cols=heads*HEAD; nb=G//HEAD
+    c=lax.axis_index("ctx")
+    greet_ctx(C)
     ak[...]=jnp.zeros_like(ak); av[...]=jnp.zeros_like(av)
     def block(i,K):
         rows=pl.ds(pl.multiple_of(i*bq,bq),bq)
         bias[:,:K]=mask_bias(lab_r,lab_c[rows,:],i*bq,bq,K)
-        def head(hd,_):
+        def head(hd):
             ln=pl.ds(pl.multiple_of(hd*HEAD,HEAD),HEAD)
             qb=q[rows,ln]; kb=k[:K,ln]; db=dm[rows,ln]
             s=nt(qb,kb)*scale+bias[:,:K]
@@ -531,34 +585,48 @@
             p=p*(1.0/jnp.sum(p,axis=1,keepdims=True))
             dp=nt(db,v[:K,ln])
             ds=(p*(dp-jnp.sum(p*dp,axis=1,keepdims=True))).astype(BF)
-            g=nn(ds,kb)*scale
-            dq[rows,ln]=g*cos[rows,:]-pltpu.roll(g,HEAD//2,1)*sin[rows,:]
+            aq[rows,ln]=nn(ds,kb)
             ak[:K,ln]+=tn(ds,qb)
             av[:K,ln]+=tn(p.astype(BF),db)
-            return 0
-        lax.fori_loop(0,heads,head,0)
+        loop(heads,head)
     per=G//bq//3
     for g in range(3):
         loop(per,lambda i,g=g: block(i+g*per,(g+1)*per*bq))
-    rb=min(128,G)
-    def fin(i,_):
-        sl=pl.ds(pl.multiple_of(i*rb,rb),rb)
-        for hd in range(heads):
-            a=hd*HEAD
-            g=ak[sl,a:a+HEAD]*scale
-            dk[sl,a:a+HEAD]=g*cos[sl,:]-pltpu.roll(g,HEAD//2,1)*sin[sl,:]
-        dv[sl,:]=av[sl,:].astype(BF)
-        return 0
-    lax.fori_loop(0,G//rb,fin,0)
-
-def attn_bwd(q,k,v,dm,cos,sin,lab_r,lab_c,heads,bq=128):
-    G,cols=q.shape
+    gsum[...]=jnp.zeros_like(gsum)
+    def unrope(i):
+        sl=pl.ds(pl.multiple_of(i*HEAD,HEAD),HEAD)
+        for t,a in ((0,aq),(1,ak)):
+            r=to_col(inv[pl.ds(t*nb+i,1),:])
+            dot=jnp.zeros((HEAD,1),F32)
+            for hd in range(heads):
+                b=hd*HEAD
+                g=a[sl,b:b+HEAD]*scale
+                g=g*cos[sl,:]-pltpu.roll(g,HEAD//2,1)*sin[sl,:]
+                x=raw[sl,t*cols+b:t*cols+b+HEAD]
+                gsum[t:t+1,b:b+HEAD]+=jnp.sum(g*x*r,axis=0,keepdims=True)
+                g=g*gains[t:t+1,b:b+HEAD]
+                a[sl,b:b+HEAD]=g
+                dot=dot+jnp.sum(g*x,axis=1,keepdims=True)
+            buf[c,pl.ds(t*nb+i,1),:]=to_row(dot)
+        draw[sl,2*cols:]=av[sl,:].astype(BF)
+    loop(nb,unrope)
+    buf[0]=sum_ctx(C,buf,ss,rs)/(C*cols)
+    def fin(i):
+        sl=pl.ds(pl.multiple_of(i*HEAD,HEAD),HEAD)
+        for t,a in ((0,aq),(1,ak)):
+            r=to_col(inv[pl.ds(t*nb+i,1),:]); dot=to_col(buf[0,pl.ds(t*nb+i,1),:])
+            m=r*r*r*dot
+            draw[sl,t*cols:(t+1)*cols]=(a[sl,:]*r-raw[sl,t*cols:(t+1)*cols]*m).astype(BF)
+    loop(nb,fin)
+
+def attn_bwd(q,k,v,dm,raw,inv,cos,sin,lab_r,lab_c,gains,C,heads,cid,bq=128):
+    G,cols=q.shape; R=2*G//HEAD; dma=pltpu.SemaphoreType.DMA
     V=pl.BlockSpec(memory_space=pltpu.VMEM)
-    f=jax.ShapeDtypeStruct((G,cols),F32)
-    return pl.pallas_call(functools.partial(attn_bwd_kernel,heads,bq,HEAD**-0.5),out_shape=[f,f,jax.ShapeDtypeStruct((G,cols),BF)],in_specs=[V]*8,out_specs=[V]*3,
-        scratch_shapes=[pltpu.VMEM((bq,G),F32),pltpu.VMEM((G,cols),F32),pltpu.VMEM((G,cols),F32)],
+    acc=pltpu.VMEM((G,cols),F32)
+    return pl.pallas_call(functools.partial(attn_bwd_kernel,C,heads,bq,HEAD**-0.5),out_shape=[jax.ShapeDtypeStruct((G,3*cols),BF),jax.ShapeDtypeStruct((2,cols),F32)],in_specs=[V]*11,out_specs=[V]*2,
+        scratch_shapes=[pltpu.VMEM((bq,G),F32),acc,acc,acc,pltpu.VMEM((C,R,HEAD),F32),dma((C-1,)),dma((C-1,))],
         cost_estimate=pl.CostEstimate(flops=5*2*heads*G*G*HEAD,bytes_accessed=G*cols*20,transcendentals=heads*G*G),
-        compiler_params=pltpu.CompilerParams(vmem_limit_bytes=48*2**20),name="attn_bwd")(q,k,v,dm,cos,sin,lab_r,lab_c)
+        compiler_params=pltpu.CompilerParams(collective_id=cid,has_side_effects=True,vmem_limit_bytes=56*2**20),name="attn_bwd")(q,k,v,dm,raw,inv,cos,sin,lab_r,lab_c,gains)
 
 def ctx_barrier(H,c,h,l):
     bar=pltpu.get_barrier_semaphore()
@@ -638,6 +706,116 @@
     return pl.pallas_call(functools.partial(rs_ctx_kernel,H,Q),out_shape=jax.ShapeDtypeStruct((T,D),x.dtype),in_specs=[A],out_specs=A,
         scratch_shapes=[pltpu.VMEM((H,T,D),BF),pltpu.VMEM((H,T,D),BF),pltpu.VMEM((H-1,T,D),BF),dma((H,)),dma((H,Q)),dma((H,Q)),dma((H-1,Q)),dma((H-1,Q)),dma(())],
         compiler_params=pltpu.CompilerParams(collective_id=cid,has_side_effects=True,vmem_limit_bytes=40*2**20),name="rs_ctx")(x)
+
+
+def front_kernel(N,C,E,Q,wq,wk,wv,wo,nx,qkv,ow,na,a_s,a_r,up_s,up_r,dn_s,dn_r,y_s,y_r,xs_,xr_,bs_,br_,lsem):
+    p=lax.axis_index("dp"); c=lax.axis_index("ctx"); e=lax.axis_index("exp")
+    H=C//2; h=c//2; l=c%2; sib=h*2+1-l
+    D=wq.shape[1]; cols=D//C; piece=cols//N; T=nx.shape[0]; R=T//Q
+    def dpeer(j): return lax.rem(p+j,N)
+    def cpeer(j): return lax.rem(c+j,C)
+    bar=pltpu.get_barrier_semaphore()
+    def sig(**kw): pl.semaphore_signal(bar,inc=1,device_id=kw,device_id_type=MESH)
+    for j in range(1,N): sig(dp=dpeer(j))
+    for j in range(1,C): sig(ctx=cpeer(j))
+    @pl.when(e>0)
+    def _(): sig(exp=e-1)
+    @pl.when(e<E-1)
+    def _(): sig(exp=e+1)
+    def rc(a,b,s,r,**kw): return pltpu.make_async_remote_copy(a,b,s,r,device_id=kw,device_id_type=MESH)
+    W=(wq,wk,wv)
+    def src(t,d,q): return W[t].at[:,pl.ds(pl.multiple_of(d*(D//N)+q*piece,128),piece)]
+    def dst(t,d,q): return qkv.at[p,q,e,:,pl.ds(t*cols+d*piece,piece)]
+    TD=[(t,d) for t in range(3) for d in range(N)]
+    local=[pltpu.make_async_copy(src(t,d,c),dst(t,d,c),lsem.at[i]) for i,(t,d) in enumerate(TD)]
+    local_w=pltpu.make_async_copy(wo,ow.at[p,e],lsem.at[len(TD)])
+    local_n=pltpu.make_async_copy(nx,na.at[c],lsem.at[len(TD)+1])
+    for x in local+[local_w,local_n]: x.start()
+    def away(j,i):
+        t,d=TD[i]; q=cpeer(j)
+        return rc(src(t,d,q),dst(t,d,c),a_s.at[j-1,i],a_r.at[j-1,i],ctx=q)
+    def home(j,i):
+        t,d=TD[i]; q=lax.rem(c+C-j,C)
+        return rc(src(t,d,q),dst(t,d,q),a_s.at[j-1,i],a_r.at[j-1,i],ctx=q)
+    def both(q,ee): return ((0,qkv.at[q,:,ee]),(1,ow.at[q,ee]))
+    def up(i,ee): b=both(p,ee)[i][1]; return rc(b,b,up_s.at[i,ee],up_r.at[i,ee],exp=e+1)
+    def dn(i,ee): b=both(p,ee)[i][1]; return rc(b,b,dn_s.at[i,ee],dn_r.at[i,ee],exp=e-1)
+    def ys(i,j,ee): b=both(p,ee)[i][1]; return rc(b,b,y_s.at[i,j-1,ee],y_r.at[i,j-1,ee],dp=dpeer(j))
+    def yr(i,j,ee): q=lax.rem(p+N-j,N); b=both(q,ee)[i][1]; return rc(b,b,y_s.at[i,j-1,ee],y_r.at[i,j-1,ee],dp=q)
+    def sl(q): return pl.ds(q*R,R)
+    def xc(j,q): return rc(nx.at[sl(q)],na.at[c,sl(q)],xs_.at[j-1,q],xr_.at[j-1,q],ctx=lax.rem(h+j,H)*2+l)
+    def xw(j,q):
+        s=lax.rem(h+H-j,H)*2+l; return rc(nx.at[sl(q)],na.at[s,sl(q)],xs_.at[j-1,q],xr_.at[j-1,q],ctx=s)
+    def bc(j,q):
+        s=c if j==0 else lax.rem(h+H-j,H)*2+l
+        a=nx if j==0 else na.at[s]
+        return rc(a.at[sl(q)],na.at[s,sl(q)],bs_.at[j,q],br_.at[j,q],ctx=sib)
+    def bw(j,q):
+        s=sib if j==0 else lax.rem(h+H-j,H)*2+1-l
+        return rc(nx.at[sl(q)],na.at[s,sl(q)],bs_.at[j,q],br_.at[j,q],ctx=sib)
+    pl.semaphore_wait(bar,(N-1)+(C-1)+(e>0).astype(jnp.int32)+(e<E-1).astype(jnp.int32))
+    for j in range(1,C):
+        for i in range(len(TD)): away(j,i).start()
+    for q in range(Q):
+        for j in range(1,H): xc(j,q).start()
+    for q in range(Q): bc(0,q).start()
+    for x in local: x.wait()
+    local_w.wait()
+    for j in range(1,C):
+        for i in range(len(TD)): home(j,i).wait_recv()
+    for i in range(2):
+        for j in range(1,N): ys(i,j,e).start()
+        @pl.when(e<E-1)
+        def _(): up(i,e).start()
+        @pl.when(e>0)
+        def _(): dn(i,e).start()
+    def rounds(r0):
+        r=r0+1
+        for i in range(2):
+            @pl.when(e>=r)
+            def _():
+                up(i,e-r).wait_recv()
+                @pl.when(e<E-1)
+                def _(): up(i,e-r).start()
+                for j in range(1,N): ys(i,j,e-r).start()
+            @pl.when(e+r<E)
+            def _():
+                dn(i,e+r).wait_recv()
+                @pl.when(e>0)
+                def _(): dn(i,e+r).start()
+                for j in range(1,N): ys(i,j,e+r).start()
+        @pl.when(r0==0)
+        def _():
+            for q in range(Q):
+                for j in range(1,H):
+                    xw(j,q).wait_recv(); bc(j,q).start()
+    loop(E-1,rounds)
+    def finish(ee):
+        for i in range(2):
+            for j in range(1,N):
+                yr(i,j,ee).wait_recv(); ys(i,j,ee).wait_send()
+            @pl.when(jnp.logical_and(e<E-1,ee<=e))
+            def _(): up(i,ee).wait_send()
+            @pl.when(jnp.logical_and(e>0,ee>=e))
+            def _(): dn(i,ee).wait_send()
+    loop(E,finish)
+    for j in range(1,C):
+        for i in range(len(TD)): away(j,i).wait_send()
+    for q in range(Q):
+        for j in range(1,H): xc(j,q).wait_send()
+        for j in range(H):
+            bc(j,q).wait_send(); bw(j,q).wait_recv()
+    local_n.wait()
+
+
+def front(wq,wk,wv,wo,nx,N,C,E,cid,Q=2):
+    S,D=wq.shape; T=nx.shape[0]; H=C//2; dma=pltpu.SemaphoreType.DMA
+    A=pl.BlockSpec(memory_space=pl.ANY)
+    return pl.pallas_call(functools.partial(front_kernel,N,C,E,Q),
+        out_shape=[jax.ShapeDtypeStruct((N,C,E,S,3*D//C),BF),jax.ShapeDtypeStruct((N,E,S,D),BF),jax.ShapeDtypeStruct((C,T,D),BF)],
+        in_specs=[A]*5,out_specs=[A]*3,
+        scratch_shapes=[dma((C-1,3*N)),dma((C-1,3*N)),dma((2,E)),dma((2,E)),dma((2,E)),dma((2,E)),dma((2,N-1,E)),dma((2,N-1,E)),dma((H-1,Q)),dma((H-1,Q)),dma((H,Q)),dma((H,Q)),dma((3*N+2,))],
+        compiler_params=pltpu.CompilerParams(collective_id=cid,has_side_effects=True),name="front")(wq,wk,wv,wo,nx)
 
 
 def dot_nn(a, b):
@@ -697,18 +875,6 @@
             vec.reshape(n_dp, n_ctx, piece), ctx_me, 1, keepdims=False
         ).reshape(cols)
 
-    packed = jnp.stack([query_weight, key_weight, value_weight], axis=1)
-    packed = packed.reshape(shard, 3, n_dp, n_ctx, piece).transpose(3, 0, 1, 2, 4)
-    packed = lax.all_to_all(packed, "ctx", split_axis=0, concat_axis=0, tiled=True)
-    packed = packed.reshape(n_ctx * shard, 3 * cols)
-    qkv_w = lax.all_gather(packed, ROWS, axis=0, tiled=True)
-    qkv_w = (
-        qkv_w.reshape(n_dp, n_exp, n_ctx, shard, 3 * cols)
-        .transpose(0, 2, 1, 3, 4)
-        .reshape(width, 3 * cols)
-    )
-    out_w = lax.all_gather(output_weight, ROWS, axis=0, tiled=True)
-
     own_routes = routes[0, 0]
     expert_ids = jnp.arange(experts, dtype=jnp.int32)
     hits = jnp.sum((own_routes[:, :, None] == expert_ids).astype(jnp.int32), axis=1)
@@ -719,7 +885,6 @@
     slot = lax.all_to_all(slot_local, MOE, split_axis=0, concat_axis=0, tiled=True)
     slot = slot.reshape(experts, tok)
     cot = cotangent[0, 0]
-    cot_all = lax.all_gather(cot, MOE, axis=0, tiled=False)
 
     hidden = hidden_in[0, 0].astype(F32)
     labels = segments[0, 0]
@@ -740,16 +905,18 @@
 
     attn_r = lax.rsqrt(jnp.mean(hidden * hidden, axis=-1, keepdims=True) + EPS)
     normed = (hidden * attn_r * attn_gain_f).astype(BF)
-    normed_g = ag_ctx(normed, n_ctx, 5).reshape(group, width)
+    qkv_w, out_w, normed_g = front(
+        query_weight, key_weight, value_weight, output_weight, normed, n_dp, n_ctx, n_exp, 5
+    )
+    qkv_w = qkv_w.reshape(width, 3 * cols)
+    out_w = out_w.reshape(cols, width)
+    normed_g = normed_g.reshape(group, width)
+    cot, normed_g = lax.optimization_barrier((cot, normed_g))
+    cot_all = lax.all_gather(cot, MOE, axis=0, tiled=False)
     raw = dot_nn(normed_g, qkv_w)
-    q_raw, k_raw = raw[:, :cols], raw[:, cols : 2 * cols]
-    squares = lax.psum(
-        jnp.stack([jnp.sum(q_raw * q_raw, axis=1), jnp.sum(k_raw * k_raw, axis=1)]), "ctx"
-    )
-    inv = lax.rsqrt(squares / width + EPS)
-    q_r, k_r = inv[0][:, None], inv[1][:, None]
-    q_rot, k_rot, v_low, mix = attn_fwd(
-        raw, inv.T, cos, sin, label_row, label_col, jnp.stack([q_gain, k_gain]), heads
+    gains = jnp.stack([q_gain, k_gain])
+    q_rot, k_rot, v_low, mix, inv = attn_fwd(
+        raw, cos, sin, label_row, label_col, gains, n_ctx, heads, 9
     )
     branch = rs_ctx(dot_nn(mix, out_w).astype(BF).reshape(n_ctx, tok, width), 6)
     residual = hidden + branch.astype(F32)
@@ -770,16 +937,20 @@
     d_gate = lax.all_to_all(
         d_gate_at.reshape(experts, tok), MOE, split_axis=0, concat_axis=0, tiled=True
     ).T
-    d_tokens = back_call(slot, d_gate_pre, d_up_pre, gate_mat, up_mat, n_ctx, n_exp, tok, (1, 8))
+    received = received.reshape(total, width)
+    gate_low = dot_tn(received, d_gate_pre.reshape(total, -1)).astype(BF)
+    up_low = dot_tn(received, d_up_pre.reshape(total, -1)).astype(BF)
+    swap = (gate_low, up_low) if n_dp == 2 else ()
+    d_tokens, others = back_call(
+        slot, d_gate_pre, d_up_pre, gate_mat, up_mat, swap, n_ctx, n_exp, tok, (1, 8)
+    )
     moe_part, d_tokens = lax.optimization_barrier((moe_part, d_tokens))
     moe_out = lax.psum_scatter(
         moe_part.reshape(experts * tok, width), MOE, scatter_dimension=0, tiled=True
     )
-    received = received.reshape(total, width)
     down_grad = dot_tn(expert_hidden.reshape(total, -1), d_out.reshape(total, width))
-    gate_grad = dot_tn(received, d_gate_pre.reshape(total, -1))
-    up_grad = dot_tn(received, d_up_pre.reshape(total, -1))
-    wide = [low_dp(g, n_dp) for g in (gate_grad, up_grad, down_grad)]
+    wide = [(a, b) for a, b in zip(swap, others)] or [low_dp(g, n_dp) for g in (gate_low, up_low)]
+    wide = wide + [low_dp(down_grad, n_dp)]
 
     d_router = d_gate
     d_logits = (
@@ -798,64 +969,40 @@
     d_branch_g = ag_ctx(d_branch, n_ctx, 7).reshape(group, width)
     out_grad = dot_tn(mix, d_branch_g)
     d_mix = dot_nt(d_branch_g, out_w).astype(BF)
-    d_qn, d_kn, d_v = attn_bwd(q_rot, k_rot, v_low, d_mix, cos, sin, label_row, label_col, heads)
-    q_gain_part = jnp.sum(d_qn * q_raw * q_r, axis=0)
-    k_gain_part = jnp.sum(d_kn * k_raw * k_r, axis=0)
-    d_qw, d_kw = d_qn * q_gain, d_kn * k_gain
-    dots = (
-        lax.psum(jnp.stack([jnp.sum(q_raw * d_qw, axis=1), jnp.sum(k_raw * d_kw, axis=1)]), "ctx")
-        / width
+    d_raw, gain_parts = attn_bwd(
+        q_rot, k_rot, v_low, d_mix, raw, inv, cos, sin, label_row, label_col, gains, n_ctx, heads, 10
     )
-    d_q_raw = d_qw * q_r - q_raw * q_r**3 * dots[0][:, None]
-    d_k_raw = d_kw * k_r - k_raw * k_r**3 * dots[1][:, None]
-    d_raw = jnp.concatenate(
-        [d_q_raw.astype(BF), d_k_raw.astype(BF), d_v], axis=1
-    )
-    d_raw, moe_out = lax.optimization_barrier((d_raw, moe_out))
-    output = (residual + moe_out.astype(F32)).astype(BF)
+    spread = jnp.zeros((2, n_dp, n_ctx, piece), F32)
+    spread = lax.dynamic_update_slice(
+        spread, gain_parts.reshape(2, n_dp, 1, piece), (0, 0, ctx_me, 0)
+    ).reshape(2, width)
+    small = jnp.concatenate([router_grad, spread, ffn_gain_grad[None]], axis=0)
+    small = jnp.pad(small, ((0, 8 - small.shape[0] % 8), (0, 0)))
     d_part_n = dot_nt(d_raw, qkv_w).astype(BF).reshape(n_ctx, tok, width)
     qkv_grad = dot_tn(normed_g, d_raw).astype(BF).reshape(n_dp, n_ctx, n_exp, shard, 3 * cols)
     out_part = out_grad.astype(BF).reshape(n_dp, n_exp, shard, width)
-    qkv_sum, out_sum, d_normed = tail(qkv_grad, out_part, d_part_n)
-    d_normed = d_normed.astype(F32)
-    wide, d_normed = lax.optimization_barrier((wide, d_normed))
+    qkv_sum, out_sum, hidden_grad, small = tail(
+        qkv_grad, out_part, d_part_n, hidden_in[0, 0], d_residual, attn_gain_f[None], small
+    )
+    wide, moe_out, small = lax.optimization_barrier((wide, moe_out, small))
+    output = (residual + moe_out.astype(F32)).astype(BF)
     gate_sum, up_sum, down_sum = (sum(x.astype(F32) for x in pair) for pair in wide)
-    attn_gain_grad = jnp.sum(d_normed * hidden * attn_r, axis=0)
-    weighted = d_normed * attn_gain_f
-    hidden_grad = (
-        d_residual
-        + weighted * attn_r
-        - hidden * attn_r**3 * jnp.mean(hidden * weighted, axis=-1, keepdims=True)
-    ).astype(BF)
 
     qkv_sum = qkv_sum.reshape(n_ctx, shard, 3, n_dp, piece)
     qkv_sum = qkv_sum.transpose(2, 1, 3, 0, 4).reshape(3, shard, width).astype(F32)
     out_sum = out_sum.astype(F32)
-
-    spread = jnp.zeros((2, n_dp, n_ctx, piece), F32)
-    spread = lax.dynamic_update_slice(
-        spread,
-        jnp.stack([q_gain_part, k_gain_part]).reshape(2, n_dp, 1, piece),
-        (0, 0, ctx_me, 0),
-    ).reshape(2, width)
-    small = jnp.concatenate(
-        [router_grad, spread, attn_gain_grad[None], ffn_gain_grad[None]], axis=0
-    )
-    pad = -small.shape[0] % 8
-    small = sums(jnp.pad(small, ((0, pad), (0, 0))), (n_dp, n_ctx, n_exp))
-    late, early = small[experts:], small
     return (
         output[None, None],
         hidden_grad[None, None],
-        late[2],
+        small[-1],
         qkv_sum[0],
         qkv_sum[1],
         qkv_sum[2],
-        late[0],
-        late[1],
+        small[experts],
+        small[experts + 1],
         out_sum,
-        late[3],
-        early[:experts].T,
+        small[experts + 2],
+        small[:experts].T,
         gate_sum[None],
         up_sum[None],
         down_sum[None],

time: 1220 us -> 1080 us (0.89)
  waiting for transfers between devices: 102 us -> 26.6 us
  blocking collectives: 55.5 us -> 0 us
  Pallas kernels: 784 us -> 823 us
  other arithmetic: 67.6 us -> 43.4 us
  local copies, waits for them, and re-layouts: 33.1 us -> 17.1 us
    pallas_call x4, Pallas kernels: 296 us -> 412 us  [the longest x1 186 us: part(): pl.pallas_call(functools.partial(back_kernel, H, E, cap, X), out_shape=[j...]
    pallas_call x2 -> x1, Pallas kernels: 99.9 us -> 56.3 us  [ag_ctx(): pl.pallas_call(functools.partial(ag_ctx_kernel, H, Q), out_shape=jax.Shap...]
    all_gather x1, waiting for transfers between devices: 68.2 us -> 26.6 us  [per_device(): cot_all = lax.all_gather(cot, MOE, axis=0, tiled=False)]
    psum x2 -> x0, blocking collectives: 41.2 us -> none  [the longest x1 20.7 us: per_device(): lax.psum(jnp.stack([jnp.sum(q_raw * q_raw, axis=1), jnp.sum(k_raw * k_raw...]
    pallas_call x1, Pallas kernels: 176 us -> 142 us  [tail(): pl.pallas_call(functools.partial(tail_kernel, N, C, E), out_shape=[jax.Sh...]
    all_gather x2 -> x0, waiting for transfers between devices: 31.9 us -> none  [the longest x1 31.9 us: per_device(): qkv_w = lax.all_gather(packed, ROWS, axis=0, tiled=True)]
    all_to_all x1 -> x0, blocking collectives: 14.3 us -> none  [per_device(): lax.all_to_all(packed, 'ctx', split_axis=0, concat_axis=0, tiled=True)]
  transfers between devices with their start and end apart: 9 -> 5, of which waited for: 2 -> 1; matrix products, arithmetic and copies ran while one was open for 15% -> 11% of each run, Pallas kernels for 34% -> 33%
where the time goes in v3:
time: 1080 us
  Pallas kernels  823 us (76%)
  matrix products  136 us (13%)
  other arithmetic  43.4 us (4%)
  waiting for transfers between devices  26.6 us (2%)
  local copies, waits for them, and re-layouts  17.1 us (2%)
  between operations  15.2 us (1%)
  starting transfers between devices  13.8 us (1%)
    pallas_call x1, Pallas kernels, part(): pl.pallas_call(functools.partial(back_kernel, H, E, cap, X), out_shape=[j...  186 us
    pallas_call x1, Pallas kernels, fwd_call(): pl.pallas_call(body, out_shape=out_shape, in_specs=[A] * 6, out_specs=[A]...  174 us
    pallas_call x1, Pallas kernels, tail(): pl.pallas_call(functools.partial(tail_kernel, N, C, E), out_shape=[jax.Sh...  142 us
    pallas_call x1, Pallas kernels, front(): pl.pallas_call(functools.partial(front_kernel, N, C, E, Q), out_shape=[ja...  108 us
    dot_general x6, matrix products, dot_tn(): lax.dot_general(a, b, (((0,), (0,)), ((), ())), preferred_element_type=F32)  88.9 us
    pallas_call x1, Pallas kernels, attn_bwd(): pl.pallas_call(functools.partial(attn_bwd_kernel, C, heads, bq, HEAD ** (...  70.8 us
    pallas_call x1, Pallas kernels, ag_ctx(): pl.pallas_call(functools.partial(ag_ctx_kernel, H, Q), out_shape=jax.Shap...  56.3 us
    pallas_call x1, Pallas kernels, attn_fwd(): pl.pallas_call(functools.partial(attn_fwd_kernel, C, heads, bq, HEAD ** (...  46.7 us
  transfers between devices with their start and end apart: 5, of which 1 were waited for; matrix products, arithmetic and copies ran while one was open for 11% of the time, Pallas kernels for 33%

profile of v3, /device:TPU:8, one launch (start us, length us, event | category | flops | bytes accessed | tf_op | source)
XLA Modules:
  0.0 1075.2 jit_solution(16818844514925604544)
XLA Ops:
  12.8 108.4 %front.1 = (bf16[2,4,4,64,1536]{4,3,2,1,0:T(8,128)(2,1)}, bf16[2,4,64,2048]{3,2,1,0:T(8,128)(2,1)}, bf16[4,384,2048]{2,1,0:T(8,128)(2,1)}) custom-call(bf16[64,2048]{1,0:T(8,128)(2,1)} %wq.1, bf16[64,2048]{1,0:T(8,128)(2,1)} %wk.1, bf16[64,2048]{1,0:T(8,128)(2,1)} %wv.1, bf16[64,2048]{1,0:T(8,128)(2,1)} %wo.1, bf16[384,2048]{1,0:T(8,128)(2,1)} %fusion.3.nx), custom_call_target="tpu_custom_call" | custom-call | tf_op jit(solution)/shard_map/front/pallas_call | solution.py:814
  122.1 6.3 all-to-all-start
  133.3 14.4 %fusion.24.raw = f32[1536,1536]{1,0:T(8,128)} fusion(bf16[1536,2048]{1,0:T(8,128)(2,1)S(1)} %bitcast.131, bf16[2048,1536]{1,0:T(8,128)(2,1)} %bitcast.135), kind=kOutput, calls=%fused_computation.73 | convolution fusion | flops 9663676416 | bytes 22020096 | tf_op jit(solution)/shard_map/dot_general | solution.py:822
  147.8 46.7 %attn_fwd.1 = (bf16[1536,512]{1,0:T(8,128)(2,1)S(1)}, bf16[1536,512]{1,0:T(8,128)(2,1)S(1)}, bf16[1536,512]{1,0:T(8,128)(2,1)}, bf16[1536,512]{1,0:T(8,128)(2,1)}, f32[24,128]{1,0:T(8,128)S(1)}) custom-call(f32[1536,1536]{1,0:T(8,128)} %fusion.24.raw, f32[1536,128]{1,0:T(8,128)S(1)} %get-tuple-element.117.cos, f32[1536,128]{1,0:T(8,128)S(1)} %get-tuple-element.118.sin, ...), custom_call_target="tpu_custom_call" | custom-call | flops 4831838208 | bytes 15728640 | tf_op jit(solution)/shard_map/attn_fwd/pallas_call | solution.py:567
  194.5 6.2 convolution_convert_fusion.2
  200.8 39.4 %rs_ctx.1 = bf16[384,2048]{1,0:T(8,128)(2,1)S(1)} custom-call(bf16[4,384,2048]{2,1,0:T(8,128)(2,1)S(1)} %bitcast.104), custom_call_target="tpu_custom_call" | custom-call | tf_op jit(solution)/shard_map/rs_ctx/pallas_call | solution.py:706
  247.3 26.6 %all-gather.3.cloned.1.call-done = bf16[6144,2048]{1,0:T(8,128)(2,1)} async-done(((bf16[384,2048]{1,0:T(8,128)(2,1)}), bf16[6144,2048]{1,0:T(8,128)(2,1)}) %all-gather.3.cloned.1.call-update) | async-done | bytes 25165840 | tf_op jit(solution)/shard_map/all_gather | solution.py:915
  273.9 173.6 %experts_fwd.1 = (bf16[16,240,2048]{2,1,0:T(8,128)(2,1)}, bf16[16,240,1024]{2,1,0:T(8,128)(2,1)}, bf16[16,240,2048]{2,1,0:T(8,128)(2,1)}, bf16[16,240,1024]{2,1,...) custom-call(s32[16,384]{1,0:T(8,128)} %bitcast.120, ...), custom_call_target="tpu_custom_call" | custom-call | flops 82543902720 | bytes 117964800 | tf_op jit(solution)/shard_map/experts_fwd/pallas_call | solution.py:487
  447.5 22.6 %bitcast_convert_fusion.1.rest_1_ = bf16[2048,1024]{1,0:T(8,128)(2,1)} fusion(bf16[16,240,2048]{2,1,0:T(8,128)(2,1)} %get-tuple-element.68, bf16[16,240,1024]{2,1,0:T(8,128)(2,1)} %get-tuple-element.70.dup), kind=kOutput, calls=%fused_computation.2 | convolution fusion | flops 16108224512 | bytes 27787264 | tf_op jit(solution)/shard_map/dot_general | solution.py:826
  470.1 19.5 %bitcast_convert_fusion.2.rest_0_ = bf16[2048,1024]{1,0:T(8,128)(2,1)} fusion(bf16[16,240,2048]{2,1,0:T(8,128)(2,1)S(1)} %copy-done.40, bf16[16,240,1024]{2,1,0:T(8,128)(2,1)S(1)} %copy-done.41), kind=kOutput, calls=%fused_computation.3 | convolution fusion | flops 16108224512 | bytes 27787264 | tf_op jit(solution)/shard_map/dot_general | solution.py:826
  489.7 185.7 %back.1 = (bf16[384,2048]{1,0:T(8,128)(2,1)}, bf16[2048,1024]{1,0:T(8,128)(2,1)}, bf16[2048,1024]{1,0:T(8,128)(2,1)}) custom-call(s32[16,384]{1,0:T(8,128)} %bitcast.121, bf16[16,240,1024]{2,1,0:T(8,128)(2,1)} %get-tuple-element.69.dgp, bf16[16,240,1024]{2,1,0:T(8,128)(2,1)} %get-tuple-element.70.dup, bf16[2048,1024]{1,0:T(8,128)(2,1)} %bitcast.139, ...), custom_call_target="tpu_custom_call" | custom-call | flops 38252052480 | bytes 15728640 | tf_op jit(solution)/shard_map/back/pallas_call | solution.py:329
  675.5 6.8 all-to-all-start.1
  682.3 24.7 %bitcast_convert_fusion = bf16[1024,2048]{1,0:T(8,128)(2,1)} fusion(bf16[16,240,1024]{2,1,0:T(8,128)(2,1)} %get-tuple-element.73, bf16[16,240,2048]{2,1,0:T(8,128)(2,1)} %get-tuple-element.74), kind=kOutput, calls=%fused_computation.1 | convolution fusion | flops 16108224512 | bytes 27787264 | tf_op jit(solution)/shard_map/dot_general | solution.py:826
  715.0 56.3 %ag_ctx.1 = bf16[4,384,2048]{2,1,0:T(8,128)(2,1)} custom-call(bf16[384,2048]{1,0:T(8,128)(2,1)} %get-tuple-element.100.x), custom_call_target="tpu_custom_call" | custom-call | tf_op jit(solution)/shard_map/ag_ctx/pallas_call | solution.py:671
  771.3 8.4 convolution_convert_fusion.4.dm
  779.7 70.8 %attn_bwd.1 = (bf16[1536,1536]{1,0:T(8,128)(2,1)}, f32[2,512]{1,0:T(2,128)}) custom-call(bf16[1536,512]{1,0:T(8,128)(2,1)} %copy-done.8, bf16[1536,512]{1,0:T(8,128)(2,1)} %copy-done.9, bf16[1536,512]{1,0:T(8,128)(2,1)} %get-tuple-element.80.v, bf16[1536,512]{1,0:T(8,128)(2,1)} %convolution_convert_fusion.4.dm, f32[1536,1536]{1,0:T(8,128)} %fusion.24.raw, ...), custom_call_target="tpu_custom_call" | custom-call | flops 12079595520 | bytes 15728640 | tf_op jit(solution)/shard_map/attn_bwd/pallas_call | solution.py:626
  853.8 8.5 convolution_convert_fusion.3
  862.3 13.9 %convolution_convert_fusion = bf16[1536,2048]{1,0:T(8,128)(2,1)} fusion(bf16[1536,1536]{1,0:T(8,128)(2,1)S(1)} %bitcast.145, bf16[2048,1536]{1,0:T(8,128)(2,1)} %bitcast.136), kind=kOutput, calls=%fused_computation.7 | convolution fusion | flops 9666822144 | bytes 17301504 | tf_op jit(solution)/shard_map/dot_general | solution.py:830
  876.2 11.8 %convolution_convert_fusion.1 = bf16[2048,1536]{1,0:T(8,128)(2,1)} fusion(bf16[1536,2048]{1,0:T(8,128)(2,1)S(1)} %bitcast.134, bf16[1536,1536]{1,0:T(8,128)(2,1)S(1)} %bitcast.145), kind=kOutput, calls=%fused_computation.8 | convolution fusion | flops 9666822144 | bytes 17301504 | tf_op jit(solution)/shard_map/dot_general | solution.py:826
  888.0 141.8 %tail.1 = (bf16[4,64,1536]{2,1,0:T(8,128)(2,1)}, bf16[64,2048]{1,0:T(8,128)(2,1)}, bf16[384,2048]{1,0:T(8,128)(2,1)}, f32[24,2048]{1,0:T(8,128)}) custom-call(bf16[2,4,4,64,1536]{4,3,2,1,0:T(8,128)(2,1)} %bitcast.114, bf16[2,4,64,2048]{3,2,1,0:T(8,128)(2,1)} %bitcast.117, bf16[4,384,2048]{2,1,0:T(8,128)(2,1)} %bitcast.113, bf16[384,2048]{1,0:T(8,128)(2,1)} %bitcast.108, ...), custom_call_target="tpu_custom_call" | custom-call | tf_op jit(solution)/shard_map/tail/pallas_call | solution.py:195
  1042.9 4.0 fusion.5
  1046.9 9.0 add_bitcast_fusion
  1055.9 5.5 add_bitcast_fusion.1
  1061.4 5.4 add_bitcast_fusion.2
  (153 shorter events, 43.6 us)
Async XLA Ops:
  7.2 235.8 %copy-start = (bf16[2048,16]{0,1:T(8,128)(2,1)S(1)}, bf16[2048,16]{0,1:T(8,128)(2,1)}, u32[]{:S(2)}) copy-start(bf16[2048,16]{0,1:T(8,128)(2,1)} %param.29) | copy-start | bytes 196612
  7.2 266.7 %all-gather.3.cloned.1.call-start = ((), (), s32[]{:S(2)}) async-start(), calls=%async_computation.4 | async-start | bytes 26738688 | tf_op jit(solution)/shard_map/all_gather | solution.py:915
  9.7 111.5 %copy-start.33 = (s32[1,1,384,8]{2,3,1,0:T(8,128)S(1)}, s32[1,1,384,8]{2,3,1,0:T(8,128)}, u32[]{:S(2)}) copy-start(s32[1,1,384,8]{2,3,1,0:T(8,128)} %param.20) | copy-start | bytes 36868
  9.8 118.7 %copy-start.35 = (bf16[2048]{0:T(1024)(128)(2,1)S(1)}, bf16[2048]{0:T(1024)(128)(2,1)}, u32[]{:S(2)}) copy-start(bf16[2048]{0:T(1024)(128)(2,1)} %param.25) | copy-start | bytes 12292
  9.8 118.7 %copy-start.36 = (bf16[2048]{0:T(1024)(128)(2,1)S(1)}, bf16[2048]{0:T(1024)(128)(2,1)}, u32[]{:S(2)}) copy-start(bf16[2048]{0:T(1024)(128)(2,1)} %param.26) | copy-start | bytes 12292
  9.8 118.7 %copy-start.6 = (s32[1,1,1536]{2,1,0:T(1,128)S(1)}, s32[1,1,1536]{2,1,0:T(1,128)}, u32[]{:S(2)}) copy-start(s32[1,1,1536]{2,1,0:T(1,128)} %param.19) | copy-start | bytes 18436
  122.1 124.6 %all-to-all-start = ((s32[16,1,384]{2,1,0:T(1,128)}), s32[16,1,384]{2,1,0:T(1,128)S(1)}, u32[]{:S(2)}, u32[]{:S(2)}) async-start(s32[16,1,384]{2,1,0:T(1,128)} %copy.53), calls=%async_computation | async-start | bytes 49152 | tf_op jit(solution)/shard_map/all_to_all | solution.py:885
  128.4 913.3 %reduce-scatter.2.cloned.1.call-start = ((), (), s32[]{:S(2)}) async-start(), calls=%async_computation.3 | async-start | bytes 26738688 | tf_op jit(solution)/shard_map/reduce_scatter | solution.py:948
  128.8 18.9 %copy-start.3 = (s32[1536,1]{1,0:T(8,128)}, s32[1536,1]{1,0:T(8,128)S(1)}, u32[]{:S(2)}) copy-start(s32[1536,1]{1,0:T(8,128)S(1)} %copy.52.lab_c) | copy-start | bytes 18436
  128.9 18.9 %copy-start.7 = (f32[2,512]{1,0:T(2,128)}, f32[2,512]{1,0:T(2,128)S(1)}, u32[]{:S(2)}) copy-start(f32[2,512]{1,0:T(2,128)S(1)} %pad_maximum_fusion.2.gains) | copy-start | bytes 12292
  147.8 46.8 %copy-start.39 = (bf16[2,4,64,2048]{3,2,1,0:T(8,128)(2,1)S(1)}, bf16[2,4,64,2048]{3,2,1,0:T(8,128)(2,1)}, u32[]{:S(2)}) copy-start(bf16[2,4,64,2048]{3,2,1,0:T(8,128)(2,1)} %get-tuple-element.66) | copy-start | bytes 6291460
  200.7 39.5 %copy-start.37 = (bf16[2048]{0:T(1024)(128)(2,1)S(1)}, bf16[2048]{0:T(1024)(128)(2,1)}, u32[]{:S(2)}) copy-start(bf16[2048]{0:T(1024)(128)(2,1)} %param.28) | copy-start | bytes 12292
  200.8 40.3 %copy-start.11 = (bf16[1,1,384,2048]{3,2,1,0:T(8,128)(2,1)S(1)}, bf16[1,1,384,2048]{3,2,1,0:T(8,128)(2,1)}, u32[]{:S(2)}) copy-start(bf16[1,1,384,2048]{3,2,1,0:T(8,128)(2,1)} %param.18) | copy-start | bytes 4718596
  447.5 22.6 %copy-start.40 = (bf16[16,240,2048]{2,1,0:T(8,128)(2,1)S(1)}, bf16[16,240,2048]{2,1,0:T(8,128)(2,1)}, u32[]{:S(2)}) copy-start(bf16[16,240,2048]{2,1,0:T(8,128)(2,1)} %get-tuple-element.68) | copy-start | bytes 47185924
  447.5 22.6 %copy-start.41 = (bf16[16,240,1024]{2,1,0:T(8,128)(2,1)S(1)}, bf16[16,240,1024]{2,1,0:T(8,128)(2,1)}, u32[]{:S(2)}) copy-start(bf16[16,240,1024]{2,1,0:T(8,128)(2,1)} %get-tuple-element.69.dgp) | copy-start | bytes 23592964
  675.5 32.3 %all-to-all-start.1 = ((f32[16,1,384]{2,1,0:T(1,128)}), f32[16,1,384]{2,1,0:T(1,128)S(1)}, u32[]{:S(2)}, u32[]{:S(2)}) async-start(f32[16,1,384]{2,1,0:T(1,128)} %get-tuple-element.82), calls=%async_computation.2 | async-start | bytes 49152 | tf_op jit(solution)/shard_map/all_to_all | solution.py:937
  682.2 25.5 %copy-start.21 = (f32[384,16]{0,1:T(8,128)S(1)}, f32[384,16]{0,1:T(8,128)}, u32[]{:S(2)}) copy-start(f32[384,16]{0,1:T(8,128)} %copy-done.20) | copy-start | bytes 73732
  682.2 25.5 %copy-start.28 = (f32[384]{0:T(512)S(1)}, f32[384]{0:T(512)}, u32[]{:S(2)}) copy-start(f32[384]{0:T(512)} %copy-done.27) | copy-start | bytes 4612
  682.2 25.5 %copy-start.30 = (f32[384]{0:T(512)S(1)}, f32[384]{0:T(512)}, u32[]{:S(2)}) copy-start(f32[384]{0:T(512)} %copy-done.29) | copy-start | bytes 4612
  682.3 25.5 %copy-start.2 = (bf16[384,2048]{1,0:T(8,128)(2,1)S(1)}, bf16[384,2048]{1,0:T(8,128)(2,1)}, u32[]{:S(2)}) copy-start(bf16[384,2048]{1,0:T(8,128)(2,1)} %copy-done.1) | copy-start | bytes 4718596
  682.3 25.5 %copy-start.26 = (f32[2048]{0:T(1024)S(1)}, f32[2048]{0:T(1024)}, u32[]{:S(2)}) copy-start(f32[2048]{0:T(1024)} %copy-done.25) | copy-start | bytes 24580
  682.3 25.5 %copy-start.32 = (f32[384]{0:T(512)S(1)}, f32[384]{0:T(512)}, u32[]{:S(2)}) copy-start(f32[384]{0:T(512)} %copy-done.31) | copy-start | bytes 4612
  707.0 334.6 %collective-permute-start = (bf16[1024,2048]{1,0:T(8,128)(2,1)}, bf16[1024,2048]{1,0:T(8,128)(2,1)}, u32[]{:S(2)}, u32[]{:S(2)}) collective-permute-start(bf16[1024,2048]{1,0:T(8,128)(2,1)} %bitcast_convert_fusion), channel_id=1, source_target_pairs={{0,16},{16,0},{1,17},{17,1},{2,18},{18,2},{3,19},{19,3},{4,20},{20... | collective-permute-start | bytes 12582920 | tf_op jit(solution)/shard_map/ppermute | solution.py:837
  853.8 22.5 %slice-start = ((s8[6291456]{0:T(1024)(128)(4,1)}), s8[4194304]{0:T(1024)(128)(4,1)S(1)}, s32[]{:S(2)}) async-start(s8[6291456]{0:T(1024)(128)(4,1)} %bitcast.132), calls=%async_computation.5 | async-start | bytes 8388608
  (27 other events, 151.7 us)
Sparse Core Ops, SparseCore 0:
  121.3 152.4 all-gather.2
  675.6 256.7 reduce-scatter.1

commit v4 on v3

--- a/solution.py
+++ b/solution.py
@@ -54,7 +54,7 @@
         add_into(dst.at[i],src.at[i]); return 0
     lax.fori_loop(0,dst.shape[0],body,0)
 
-def tail_kernel(N,C,E,gq,go,dn,hid,dres,gain,sm,oq,oo,od,osm,own_q,own_o,own_d,yq,yo,uq,uo,vq,vo,d1,d2,ld,ldd,ys,yr,zs,zu,zd,s1,r1,s2,r2,a_s,a_r,osem,hv,rv,gv,b0,b1,b2,t_s,t_r):
+def tail_kernel(N,C,E,nrm,dr,w,go,hid,dres,gain,sm,o1,o2,o3,oo,od,osm,own_q,own_o,own_d,yq,yo,uq,uo,vq,vo,d1,d2,ld,ldd,ys,yr,zs,zu,zd,s1,r1,s2,r2,a_s,a_r,osem,hv,rv,gv,b0,b1,b2,t_s,t_r,nv,drv,wv,sq,sd,m_s):
     p=lax.axis_index("dp"); c=lax.axis_index("ctx"); e=lax.axis_index("exp")
     H=C//2; h=c//2; l=c%2
     def dpeer(j): return lax.rem(p+j,N)
@@ -67,14 +67,13 @@
     for j in range(1,E): sig(exp=lax.rem(e+j,E))
     order=by_distance(e,E)
     def rc(src,dst,ss,rs,**kw): return pltpu.make_async_remote_copy(src,dst,ss,rs,device_id=kw,device_id_type=MESH)
-    def loads(o): return [pltpu.make_async_copy(gq.at[p,:,o],own_q.at[o],ld.at[0,o]),pltpu.make_async_copy(go.at[p,o],own_o.at[o],ld.at[1,o])]
+    def loads(o): return [pltpu.make_async_copy(go.at[p,o],own_o.at[o],ld.at[1,o])]
     def cy(j,o):
         q=dpeer(j)
-        return [rc(gq.at[q,:,o],yq.at[j-1,o],ys.at[0,j-1,o],yr.at[0,j-1,o],dp=q), rc(go.at[q,o],yo.at[j-1,o],ys.at[1,j-1,o],yr.at[1,j-1,o],dp=q)]
+        return [rc(sq.at[j-1,o],yq.at[j-1,o],ys.at[0,j-1,o],yr.at[0,j-1,o],dp=q), rc(go.at[q,o],yo.at[j-1,o],ys.at[1,j-1,o],yr.at[1,j-1,o],dp=q)]
     def cu(o): return [rc(own_q.at[o],uq.at[o],zs.at[0,o],zu.at[0,o],exp=e+1), rc(own_o.at[o],uo.at[o],zs.at[1,o],zu.at[1,o],exp=e+1)]
     def cd(o): return [rc(own_q.at[o],vq.at[o],zs.at[0,o],zd.at[0,o],exp=e-1), rc(own_o.at[o],vo.at[o],zs.at[1,o],zd.at[1,o],exp=e-1)]
-    def loadd(hh): return pltpu.make_async_copy(dn.at[hh*2+l],own_d.at[hh],ldd.at[hh])
-    def c1(hh): return rc(dn.at[hh*2+1-l],d1.at[hh],s1.at[hh],r1.at[hh],ctx=h*2+1-l)
+    def c1(hh): return rc(sd.at[hh],d1.at[hh],s1.at[hh],r1.at[hh],ctx=h*2+1-l)
     def c2(j):
         hh=hpeer(j); return rc(own_d.at[hh],d2.at[j-1],s2.at[j-1],r2.at[j-1],ctx=hh*2+l)
     hs=[hpeer(j) for j in range(1,H)]+[h]
@@ -83,17 +82,39 @@
     side=[pltpu.make_async_copy(hid,hv,osem.at[3]),pltpu.make_async_copy(dres,rv,osem.at[4]),pltpu.make_async_copy(gain,gv,osem.at[5]),pltpu.make_async_copy(sm,b0.at[p],osem.at[6])]
     for x in side: x.start()
     loop(E,start_loads)
-    for hh in hs: loadd(hh).start()
+    big=[pltpu.make_async_copy(a,b,m_s.at[i]) for i,(a,b) in enumerate(((nrm,nv),(dr,drv),(w,wv)))]
+    for x in big: x.start()
+    Dm=wv.shape[0]; W3=wv.shape[1]; S_=own_q.shape[2]; T_=own_d.shape[1]; pc=Dm//(N*C)
+    def grads(q,put):
+        def chunk(cc):
+            cl=pl.ds(pl.multiple_of(q*(Dm//N)+cc*pc,128),pc)
+            st=W3//3
+            for t in range(3):
+                g=tn(nv[:,cl],drv[:,t*st:(t+1)*st]).astype(BF)
+                for ee in range(E): put.at[ee][cc,:,t*st:(t+1)*st]=g[ee*S_:(ee+1)*S_]
+        loop(C,chunk)
+    def dnorm(cc,put):
+        rw=pl.ds(pl.multiple_of(cc*T_,T_),T_)
+        def chunk(n):
+            cl=pl.ds(pl.multiple_of(n*512,512),512)
+            put[:,cl]=nt(drv[rw,:],wv[cl,:]).astype(BF)
+        loop(Dm//512,chunk)
     pl.semaphore_wait(bar,(N-1)+(C-1)+(E-1))
-    for j in range(1,N):
-        for x in cy(j,order(0)): x.start()
-    for hh in hs: c1(hh).start()
-    def start_dp(k):
-        for j in range(1,N):
-            for x in cy(j,order(k+1)): x.start()
-    loop(E-1,start_dp)
+    def start_o(k):
+        for j in range(1,N): cy(j,order(k))[1].start()
+    loop(E,start_o)
+    big[0].wait(); big[1].wait()
+    for j in range(1,N): grads(dpeer(j),sq.at[j-1])
+    def start_q(k):
+        for j in range(1,N): cy(j,order(k))[0].start()
+    loop(E,start_q)
+    big[2].wait()
+    for hh in hs:
+        dnorm(hh*2+1-l,sd.at[hh]); c1(hh).start()
+        dnorm(hh*2+l,own_d.at[hh])
+    grads(p,own_q)
     for i,hh in enumerate(hs):
-        loadd(hh).wait(); c1(hh).wait_recv(); add_into(own_d.at[hh],d1.at[hh])
+        c1(hh).wait_recv(); add_into(own_d.at[hh],d1.at[hh])
         if i<H-1: c2(i+1).start()
     def line(k):
         o=order(k)
@@ -164,10 +185,16 @@
     def _():
         for x in cd(e): x.wait_recv()
         add3(own_q.at[e],vq.at[e]); add3(own_o.at[e],vo.at[e])
-    def ca(j):
-        q=cpeer(j); return rc(own_q.at[e,q],oq.at[c],a_s.at[j-1],a_r.at[j-1],ctx=q)
-    for j in range(1,C): ca(j).start()
-    l1=pltpu.make_async_copy(own_q.at[e,c],oq.at[c],osem.at[1]); l1.start()
+    outs=(o1,o2,o3); cols=W3//3
+    TD=[(t,d) for t in range(3) for d in range(N)]
+    def src(q,t,d): return own_q.at[e,q,:,pl.ds(t*cols+d*pc,pc)]
+    def dst(q,t,d): return outs[t].at[:,pl.ds(pl.multiple_of(d*(Dm//N)+q*pc,128),pc)]
+    def ca(j,i): q=cpeer(j); return rc(src(q,*TD[i]),dst(c,*TD[i]),a_s.at[j-1,i],a_r.at[j-1,i],ctx=q)
+    def cw(j,i): q=lax.rem(c+C-j,C); return rc(src(q,*TD[i]),dst(q,*TD[i]),a_s.at[j-1,i],a_r.at[j-1,i],ctx=q)
+    for j in range(1,C):
+        for i in range(len(TD)): ca(j,i).start()
+    l1=[pltpu.make_async_copy(src(c,*TD[i]),dst(c,*TD[i]),m_s.at[3+i]) for i in range(len(TD))]
+    for x in l1: x.start()
     l2=pltpu.make_async_copy(own_o.at[e],oo,osem.at[2]); l2.start()
     def drain(k):
         for j in range(1,N):
@@ -179,28 +206,31 @@
     for hh in hs: c1(hh).wait_send()
     for j in range(1,H): c2(j).wait_send()
     for j in range(1,C):
-        ca(j).wait_send();
-        src=lax.rem(c+C-j,C)
-        rc(own_q.at[e,c],oq.at[src],a_s.at[j-1],a_r.at[j-1],ctx=src).wait_recv()
+        for i in range(len(TD)):
+            ca(j,i).wait_send(); cw(j,i).wait_recv()
     for t in range(3):
         for j in range(1,small[t][2]): hop(t,j).wait_send()
     b0[0]=gathered(2)
     so=pltpu.make_async_copy(b0.at[0],osm,osem.at[7]); so.start()
-    pltpu.make_async_copy(own_d.at[h],od,osem.at[0]).wait(); l1.wait(); l2.wait(); so.wait()
-
-def tail(gq,go,dn,hid,dres,gain,sm,cid=2):
-    N,C,E,S,W3=gq.shape; D=go.shape[-1]; T=dn.shape[1]; H=C//2; R=sm.shape[0]
+    pltpu.make_async_copy(own_d.at[h],od,osem.at[0]).wait(); l2.wait(); so.wait()
+    for x in l1: x.wait()
+
+def tail(nrm,dr,w,go,hid,dres,gain,sm,C,cid=2):
+    N,E,S,D=go.shape; W3=dr.shape[1]; G=nrm.shape[0]; T=G//C; H=C//2; R=sm.shape[0]
     dma=pltpu.SemaphoreType.DMA; V=lambda *s: pltpu.VMEM(s,BF); FV=lambda *s: pltpu.VMEM(s,F32)
     M=max(N,C,E)-1
+    sd=jax.ShapeDtypeStruct((S,D),BF)
     return pl.pallas_call(functools.partial(tail_kernel,N,C,E),
-        out_shape=[jax.ShapeDtypeStruct((C,S,W3),BF),jax.ShapeDtypeStruct((S,D),BF),jax.ShapeDtypeStruct((T,D),BF),jax.ShapeDtypeStruct((R,D),F32)],
-        in_specs=[pl.BlockSpec(memory_space=pl.ANY)]*7,
-        out_specs=[pl.BlockSpec(memory_space=pl.ANY)]*4,
+        out_shape=[sd]*4+[jax.ShapeDtypeStruct((T,D),BF),jax.ShapeDtypeStruct((R,D),F32)],
+        in_specs=[pl.BlockSpec(memory_space=pl.ANY)]*8,
+        out_specs=[pl.BlockSpec(memory_space=pl.ANY)]*6,
         scratch_shapes=[V(E,C,S,W3),V(E,S,D),V(H,T,D),V(N-1,E,C,S,W3),V(N-1,E,S,D),V(E,C,S,W3),V(E,S,D),V(E,C,S,W3),V(E,S,D),V(H,T,D),V(H-1,T,D),
-            dma((2,E)),dma((H,)),dma((2,N-1,E)),dma((2,N-1,E)),dma((2,E)),dma((2,E)),dma((2,E)),dma((H,)),dma((H,)),dma((H-1,)),dma((H-1,)),dma((C-1,)),dma((C-1,)),dma((8,)),
-            V(T,D),FV(T,D),FV(1,D),FV(N,R,D),FV(C,R,D),FV(E,R,D),dma((3,M)),dma((3,M))],
+            dma((2,E)),dma((H,)),dma((2,N-1,E)),dma((2,N-1,E)),dma((2,E)),dma((2,E)),dma((2,E)),dma((H,)),dma((H,)),dma((H-1,)),dma((H-1,)),dma((C-1,3*N)),dma((C-1,3*N)),dma((8,)),
+            V(T,D),FV(T,D),FV(1,D),FV(N,R,D),FV(C,R,D),FV(E,R,D),dma((3,M)),dma((3,M)),
+            V(G,D),V(G,W3),V(D,W3),V(N-1,E,C,S,W3),V(H,T,D),dma((3+3*N,))],
+        cost_estimate=pl.CostEstimate(flops=4*G*D*W3,bytes_accessed=2*(G*D+G*W3+D*W3),transcendentals=0),
         compiler_params=pltpu.CompilerParams(collective_id=cid,has_side_effects=True,vmem_limit_bytes=61*2**20),
-        name="tail")(gq,go,dn,hid,dres,gain,sm)
+        name="tail")(nrm,dr,w,go,hid,dres,gain,sm)
 
 def nn(a,b): return lax.dot_general(a,b,(((1,),(0,)),((),())),preferred_element_type=F32)
 def tn(a,b): return lax.dot_general(a,b,(((0,),(0,)),((),())),preferred_element_type=F32)
@@ -228,7 +258,7 @@
     def _(): pl.semaphore_signal(bar,inc=1,device_id={"exp":e+1},device_id_type=MESH)
     def ex(i):
         es,er=rest[2*X+20:]
-        return pltpu.make_async_remote_copy(ex_in[i],ex_out[i],es.at[i],er.at[i],device_id={"dp":1-lax.axis_index("dp")},device_id_type=MESH)
+        return pltpu.make_async_remote_copy(ex_in[i].at[:ex_out[i].shape[0]],ex_out[i],es.at[i],er.at[i],device_id={"dp":1-lax.axis_index("dp")},device_id_type=MESH)
     if X: pl.semaphore_signal(bar,inc=1,device_id={"dp":1-lax.axis_index("dp")},device_id_type=MESH)
     order=by_distance(e,E)
     wl=[pltpu.make_async_copy(gw,wg,w_sem.at[0]),pltpu.make_async_copy(uw,wu,w_sem.at[1])]
@@ -327,20 +357,20 @@
         ex=tuple(swap) if i==0 else ()
         X=len(ex)
         return pl.pallas_call(functools.partial(back_kernel,H,E,cap,X),
-            out_shape=[jax.ShapeDtypeStruct((T,W),BF)]+[jax.ShapeDtypeStruct(g.shape,g.dtype) for g in ex],
+            out_shape=[jax.ShapeDtypeStruct((T,W),BF)]+[jax.ShapeDtypeStruct((n,g.shape[1]),g.dtype) for g,n in ex],
             in_specs=[A]*(5+X),
             out_specs=[A]*(1+X),
             scratch_shapes=[V(H,E,T,W),V(H,E,T,W),V(H-1,E,T,W),V(E+1,T,W),V(3,T,W),V(2,cap,FF),V(2,cap,FF),pltpu.VMEM((S,T),jnp.int32),V(W,FF),V(W,FF),
                 dma((2,2)),dma((2,)),dma((H*E,)),dma((H,E)),dma((H-1,E)),dma((H-1,E)),dma((E,)),dma((E+1,)),dma(())]+([dma((X,)),dma((X,))] if X else []),
             cost_estimate=pl.CostEstimate(flops=2*S*cap*(2*W*FF+T*W),bytes_accessed=S*4*cap*FF,transcendentals=0),
             compiler_params=pltpu.CompilerParams(collective_id=cids[i],has_side_effects=True,vmem_limit_bytes=61*2**20),
-            name="back")(slot,dgp,dup,a,b,*ex)
+            name="back")(slot,dgp,dup,a,b,*[g for g,_ in ex])
     out=[part(i) for i in range(parts)]
     tok=out[0][0] if parts==1 else jnp.concatenate([o[0] for o in out],axis=1)
     return tok,out[0][1:]
 
 
-def fwd_kernel(H,E,T,cap,in_vmem,slot,rows,cot,gw,uw,dw,recv,hid,dout,dgp,dup,moe,dg,*scr):
+def fwd_kernel(H,E,T,cap,in_vmem,slot,rows,cot,gw,uw,dw,recv,hid,dout,dgp,dup,moe_a,moe_b,dg,*scr):
     if in_vmem: allr=scr[0]; scr=scr[1:]; rb=None
     else: allr=scr[0]; rb=scr[1]; scr=scr[2:]
     (slv,wg,wu,wd,cb,srecv,shid,sdout,sdgp,sdup,smoe,sdg,cr,w_sem,c_sem,l_sem,o_sem,up_s,dn_s,up_r,dn_r,x_s,x_r,b_s,b_r)=scr
@@ -385,7 +415,7 @@
         return rc(idx(hi(j),l,ee),x_s.at[j-1,ee],x_r.at[j-1,ee],ctx=hi(j)*2+l)
     def bs(j,ee): return rc(idx(hi(j),l,ee),b_s.at[j,ee],b_r.at[j,ee],ctx=h*2+1-l)
     def br(j,ee): return rc(idx(hi(j),1-l,ee),b_s.at[j,ee],b_r.at[j,ee],ctx=h*2+1-l)
-    outs=[(srecv,recv),(shid,hid),(sdout,dout),(sdgp,dgp),(sdup,dup),(smoe,moe),(sdg,dg)]
+    outs=[(srecv,recv),(shid,hid),(sdout,dout),(sdgp,dgp),(sdup,dup),(smoe.at[:,:,:D//2],moe_a),(smoe.at[:,:,D//2:],moe_b),(sdg,dg)]
     def odma(n):
         s=sender(n); b=lax.rem(n,2)
         return [pltpu.make_async_copy(a.at[b],o.at[s],o_sem.at[i,b]) for i,(a,o) in enumerate(outs)]
@@ -480,16 +510,16 @@
     in_vmem=S*EXT*D*2<=28*2**20
     A=pl.BlockSpec(memory_space=pl.ANY)
     sd=lambda a,b,dt=BF: jax.ShapeDtypeStruct((S,a,b),dt)
-    out_shape=[sd(cap,D),sd(cap,FF),sd(cap,D),sd(cap,FF),sd(cap,FF),sd(T,D),sd(1,T,F32)]
+    out_shape=[sd(cap,D),sd(cap,FF),sd(cap,D),sd(cap,FF),sd(cap,FF),sd(T,D//2),sd(T,D//2),sd(1,T,F32)]
     land=[V(S,EXT,D)] if in_vmem else [V(EXT,D)]
     if not in_vmem: out_shape=out_shape+[sd(EXT,D)]
     body=functools.partial(fwd_kernel,H,E,T,cap,in_vmem)
     r=pl.pallas_call(body,out_shape=out_shape,in_specs=[A]*6,out_specs=[A]*len(out_shape),
         scratch_shapes=land+[pltpu.VMEM((S,T),jnp.int32),V(D,FF),V(D,FF),V(FF,D),V(2,T,D),V(2,cap,D),V(2,cap,FF),V(2,cap,D),V(2,cap,FF),V(2,cap,FF),V(2,T,D),pltpu.VMEM((2,1,T),F32),V(cap,D),
-            dma((4,)),dma((2,)),dma(()),dma((7,2)),dma((E,)),dma((E,)),dma((E,)),dma((E,)),dma((H-1,E)),dma((H-1,E)),dma((H,E)),dma((H,E))],
+            dma((4,)),dma((2,)),dma(()),dma((8,2)),dma((E,)),dma((E,)),dma((E,)),dma((E,)),dma((H-1,E)),dma((H-1,E)),dma((H,E)),dma((H,E))],
         cost_estimate=pl.CostEstimate(flops=2*S*cap*(4*D*FF+3*T*D),bytes_accessed=S*2*(T*D+2*cap*D+3*cap*FF+T*D)+6*D*FF,transcendentals=S*cap*FF),
         compiler_params=pltpu.CompilerParams(collective_id=cid,has_side_effects=True,vmem_limit_bytes=61*2**20),name="experts_fwd")(slot,rows,cot,gw,uw,dw)
-    return r[:7]
+    return r[:8]
 
 
 def mask_bias(lab_r,lab_c,i0,bq,K):
@@ -511,9 +541,9 @@
     c=lax.axis_index("ctx"); bar=pltpu.get_barrier_semaphore()
     for j in range(1,C): pl.semaphore_signal(bar,inc=1,device_id={"ctx":lax.rem(c+j,C)},device_id_type=MESH)
 
-def sum_ctx(C,buf,ss,rs):
+def sum_ctx(C,buf,ss,rs,others=0):
     c=lax.axis_index("ctx")
-    pl.semaphore_wait(pltpu.get_barrier_semaphore(),C-1)
+    pl.semaphore_wait(pltpu.get_barrier_semaphore(),C-1+others)
     def cp(j): return pltpu.make_async_remote_copy(buf.at[c],buf.at[c],ss.at[j-1],rs.at[j-1],device_id={"ctx":lax.rem(c+j,C)},device_id_type=MESH)
     for j in range(1,C): cp(j).start()
     for j in range(1,C):
@@ -524,10 +554,69 @@
     for j in range(1,C): cp(j).wait_send()
     return acc
 
-def attn_fwd_kernel(C,heads,bq,scale,raw,cos,sin,lab_r,lab_c,gains,qo,ko,vo,mix,inv,bias,buf,ss,rs):
+class Rows:
+    def __init__(self,N,E,x,o,ls,us,ur,ds_,dr_,ys,yr):
+        self.N,self.E,self.x,self.o=N,E,x,o
+        self.ls,self.us,self.ur,self.ds,self.dr,self.ys,self.yr=ls,us,ur,ds_,dr_,ys,yr
+        self.p=lax.axis_index("dp"); self.e=lax.axis_index("exp")
+        self.peers=(N-1)+(self.e>0).astype(jnp.int32)+(self.e<E-1).astype(jnp.int32)
+    def greet(self):
+        bar=pltpu.get_barrier_semaphore()
+        def sig(**kw): pl.semaphore_signal(bar,inc=1,device_id=kw,device_id_type=MESH)
+        for j in range(1,self.N): sig(dp=lax.rem(self.p+j,self.N))
+        @pl.when(self.e>0)
+        def _(): sig(exp=self.e-1)
+        @pl.when(self.e<self.E-1)
+        def _(): sig(exp=self.e+1)
+        self.local=pltpu.make_async_copy(self.x,self.o.at[self.p,self.e],self.ls)
+        self.local.start()
+    def rc(self,q,ee,s,r,**kw): return pltpu.make_async_remote_copy(self.o.at[q,ee],self.o.at[q,ee],s,r,device_id=kw,device_id_type=MESH)
+    def up(self,ee): return self.rc(self.p,ee,self.us.at[ee],self.ur.at[ee],exp=self.e+1)
+    def dn(self,ee): return self.rc(self.p,ee,self.ds.at[ee],self.dr.at[ee],exp=self.e-1)
+    def across(self,j,ee): return self.rc(self.p,ee,self.ys.at[j-1,ee],self.yr.at[j-1,ee],dp=lax.rem(self.p+j,self.N))
+    def came(self,j,ee):
+        q=lax.rem(self.p+self.N-j,self.N)
+        return self.rc(q,ee,self.ys.at[j-1,ee],self.yr.at[j-1,ee],dp=q)
+    def begin(self):
+        e,E=self.e,self.E
+        self.local.wait()
+        for j in range(1,self.N): self.across(j,e).start()
+        @pl.when(e<E-1)
+        def _(): self.up(e).start()
+        @pl.when(e>0)
+        def _(): self.dn(e).start()
+    def round(self,r):
+        e,E=self.e,self.E
+        @pl.when(e>=r)
+        def _():
+            self.up(e-r).wait_recv()
+            @pl.when(e<E-1)
+            def _(): self.up(e-r).start()
+            for j in range(1,self.N): self.across(j,e-r).start()
+        @pl.when(e+r<E)
+        def _():
+            self.dn(e+r).wait_recv()
+            @pl.when(e>0)
+            def _(): self.dn(e+r).start()
+            for j in range(1,self.N): self.across(j,e+r).start()
+    def finish(self):
+        e,E=self.e,self.E
+        def one(ee):
+            for j in range(1,self.N):
+                self.came(j,ee).wait_recv(); self.across(j,ee).wait_send()
+            @pl.when(jnp.logical_and(e<E-1,ee<=e))
+            def _(): self.up(ee).wait_send()
+            @pl.when(jnp.logical_and(e>0,ee>=e))
+            def _(): self.dn(ee).wait_send()
+        loop(E,one)
+
+
+def attn_fwd_kernel(N,C,E,heads,bq,scale,raw,cos,sin,lab_r,lab_c,gains,wo,qo,ko,vo,mix,inv,ow,bias,buf,ss,rs,*gs):
     G=raw.shape[0]; cols=heads*HEAD; nb=G//HEAD
     c=lax.axis_index("ctx")
     greet_ctx(C)
+    rows_w=Rows(N,E,wo,ow,*gs)
+    rows_w.greet()
     def squares(i):
         sl=pl.ds(pl.multiple_of(i*HEAD,HEAD),HEAD)
         for t in range(2):
@@ -535,7 +624,8 @@
             buf[c,pl.ds(t*nb+i,1),:]=to_row(jnp.sum(v*v,axis=1,keepdims=True))
         vo[sl,:]=raw[sl,2*cols:].astype(BF)
     loop(nb,squares)
-    inv[...]=lax.rsqrt(sum_ctx(C,buf,ss,rs)/(C*cols)+EPS)
+    inv[...]=lax.rsqrt(sum_ctx(C,buf,ss,rs,rows_w.peers)/(C*cols)+EPS)
+    rows_w.begin()
     def prep(i):
         sl=pl.ds(pl.multiple_of(i*HEAD,HEAD),HEAD)
         cs,sn=cos[sl,:],sin[sl,:]
@@ -559,15 +649,18 @@
     per=G//bq//3
     for g in range(3):
         loop(per,lambda i,g=g: block(i+g*per,(g+1)*per*bq))
-
-def attn_fwd(raw,cos,sin,lab_r,lab_c,gains,C,heads,cid,bq=128):
+        if g+1<E: rows_w.round(g+1)
+    for r in range(4,E): rows_w.round(r)
+    rows_w.finish()
+
+def attn_fwd(raw,cos,sin,lab_r,lab_c,gains,wo,N,C,E,heads,cid,bq=256):
     G=raw.shape[0]; cols=heads*HEAD; R=2*G//HEAD; dma=pltpu.SemaphoreType.DMA
     o=jax.ShapeDtypeStruct((G,cols),BF)
-    V=pl.BlockSpec(memory_space=pltpu.VMEM)
-    return pl.pallas_call(functools.partial(attn_fwd_kernel,C,heads,bq,HEAD**-0.5),out_shape=[o]*4+[jax.ShapeDtypeStruct((R,HEAD),F32)],in_specs=[V]*6,out_specs=[V]*5,
-        scratch_shapes=[pltpu.VMEM((bq,G),F32),pltpu.VMEM((C,R,HEAD),F32),dma((C-1,)),dma((C-1,))],
+    V=pl.BlockSpec(memory_space=pltpu.VMEM); A=pl.BlockSpec(memory_space=pl.ANY)
+    return pl.pallas_call(functools.partial(attn_fwd_kernel,N,C,E,heads,bq,HEAD**-0.5),out_shape=[o]*4+[jax.ShapeDtypeStruct((R,HEAD),F32),jax.ShapeDtypeStruct((N,E)+wo.shape,BF)],in_specs=[V]*6+[A],out_specs=[V]*5+[A],
+        scratch_shapes=[pltpu.VMEM((bq,G),F32),pltpu.VMEM((C,R,HEAD),F32),dma((C-1,)),dma((C-1,)),dma(()),dma((E,)),dma((E,)),dma((E,)),dma((E,)),dma((N-1,E)),dma((N-1,E))],
         cost_estimate=pl.CostEstimate(flops=2*2*heads*G*G*HEAD,bytes_accessed=G*cols*20,transcendentals=heads*G*G),
-        compiler_params=pltpu.CompilerParams(collective_id=cid,has_side_effects=True,vmem_limit_bytes=48*2**20),name="attn_fwd")(raw,cos,sin,lab_r,lab_c,gains)
+        compiler_params=pltpu.CompilerParams(collective_id=cid,has_side_effects=True,vmem_limit_bytes=48*2**20),name="attn_fwd")(raw,cos,sin,lab_r,lab_c,gains,wo)
 
 def attn_bwd_kernel(C,heads,bq,scale,q,k,v,dm,raw,inv,cos,sin,lab_r,lab_c,gains,draw,gsum,bias,aq,ak,av,buf,ss,rs):
     G=q.shape[0]; cols=heads*HEAD; nb=G//HEAD
@@ -619,7 +712,7 @@
             draw[sl,t*cols:(t+1)*cols]=(a[sl,:]*r-raw[sl,t*cols:(t+1)*cols]*m).astype(BF)
     loop(nb,fin)
 
-def attn_bwd(q,k,v,dm,raw,inv,cos,sin,lab_r,lab_c,gains,C,heads,cid,bq=128):
+def attn_bwd(q,k,v,dm,raw,inv,cos,sin,lab_r,lab_c,gains,C,heads,cid,bq=256):
     G,cols=q.shape; R=2*G//HEAD; dma=pltpu.SemaphoreType.DMA
     V=pl.BlockSpec(memory_space=pltpu.VMEM)
     acc=pltpu.VMEM((G,cols),F32)
@@ -708,7 +801,7 @@
         compiler_params=pltpu.CompilerParams(collective_id=cid,has_side_effects=True,vmem_limit_bytes=40*2**20),name="rs_ctx")(x)
 
 
-def front_kernel(N,C,E,Q,wq,wk,wv,wo,nx,qkv,ow,na,a_s,a_r,up_s,up_r,dn_s,dn_r,y_s,y_r,xs_,xr_,bs_,br_,lsem):
+def front_kernel(N,C,E,Q,wq,wk,wv,nx,qkv,na,a_s,a_r,up_s,up_r,dn_s,dn_r,y_s,y_r,xs_,xr_,bs_,br_,lsem):
     p=lax.axis_index("dp"); c=lax.axis_index("ctx"); e=lax.axis_index("exp")
     H=C//2; h=c//2; l=c%2; sib=h*2+1-l
     D=wq.shape[1]; cols=D//C; piece=cols//N; T=nx.shape[0]; R=T//Q
@@ -728,16 +821,15 @@
     def dst(t,d,q): return qkv.at[p,q,e,:,pl.ds(t*cols+d*piece,piece)]
     TD=[(t,d) for t in range(3) for d in range(N)]
     local=[pltpu.make_async_copy(src(t,d,c),dst(t,d,c),lsem.at[i]) for i,(t,d) in enumerate(TD)]
-    local_w=pltpu.make_async_copy(wo,ow.at[p,e],lsem.at[len(TD)])
     local_n=pltpu.make_async_copy(nx,na.at[c],lsem.at[len(TD)+1])
-    for x in local+[local_w,local_n]: x.start()
+    for x in local+[local_n]: x.start()
     def away(j,i):
         t,d=TD[i]; q=cpeer(j)
         return rc(src(t,d,q),dst(t,d,c),a_s.at[j-1,i],a_r.at[j-1,i],ctx=q)
     def home(j,i):
         t,d=TD[i]; q=lax.rem(c+C-j,C)
         return rc(src(t,d,q),dst(t,d,q),a_s.at[j-1,i],a_r.at[j-1,i],ctx=q)
-    def both(q,ee): return ((0,qkv.at[q,:,ee]),(1,ow.at[q,ee]))
+    def both(q,ee): return ((0,qkv.at[q,:,ee]),)
     def up(i,ee): b=both(p,ee)[i][1]; return rc(b,b,up_s.at[i,ee],up_r.at[i,ee],exp=e+1)
     def dn(i,ee): b=both(p,ee)[i][1]; return rc(b,b,dn_s.at[i,ee],dn_r.at[i,ee],exp=e-1)
     def ys(i,j,ee): b=both(p,ee)[i][1]; return rc(b,b,y_s.at[i,j-1,ee],y_r.at[i,j-1,ee],dp=dpeer(j))
@@ -760,10 +852,9 @@
         for j in range(1,H): xc(j,q).start()
     for q in range(Q): bc(0,q).start()
     for x in local: x.wait()
-    local_w.wait()
     for j in range(1,C):
         for i in range(len(TD)): home(j,i).wait_recv()
-    for i in range(2):
+    for i in range(1):
         for j in range(1,N): ys(i,j,e).start()
         @pl.when(e<E-1)
         def _(): up(i,e).start()
@@ -771,7 +862,7 @@
         def _(): dn(i,e).start()
     def rounds(r0):
         r=r0+1
-        for i in range(2):
+        for i in range(1):
             @pl.when(e>=r)
             def _():
                 up(i,e-r).wait_recv()
@@ -791,7 +882,7 @@
                     xw(j,q).wait_recv(); bc(j,q).start()
     loop(E-1,rounds)
     def finish(ee):
-        for i in range(2):
+        for i in range(1):
             for j in range(1,N):
                 yr(i,j,ee).wait_recv(); ys(i,j,ee).wait_send()
             @pl.when(jnp.logical_and(e<E-1,ee<=e))
@@ -808,14 +899,14 @@
     local_n.wait()
 
 
-def front(wq,wk,wv,wo,nx,N,C,E,cid,Q=2):
+def front(wq,wk,wv,nx,N,C,E,cid,Q=2):
     S,D=wq.shape; T=nx.shape[0]; H=C//2; dma=pltpu.SemaphoreType.DMA
     A=pl.BlockSpec(memory_space=pl.ANY)
     return pl.pallas_call(functools.partial(front_kernel,N,C,E,Q),
-        out_shape=[jax.ShapeDtypeStruct((N,C,E,S,3*D//C),BF),jax.ShapeDtypeStruct((N,E,S,D),BF),jax.ShapeDtypeStruct((C,T,D),BF)],
-        in_specs=[A]*5,out_specs=[A]*3,
+        out_shape=[jax.ShapeDtypeStruct((N,C,E,S,3*D//C),BF),jax.ShapeDtypeStruct((C,T,D),BF)],
+        in_specs=[A]*4,out_specs=[A]*2,
         scratch_shapes=[dma((C-1,3*N)),dma((C-1,3*N)),dma((2,E)),dma((2,E)),dma((2,E)),dma((2,E)),dma((2,N-1,E)),dma((2,N-1,E)),dma((H-1,Q)),dma((H-1,Q)),dma((H,Q)),dma((H,Q)),dma((3*N+2,))],
-        compiler_params=pltpu.CompilerParams(collective_id=cid,has_side_effects=True),name="front")(wq,wk,wv,wo,nx)
+        compiler_params=pltpu.CompilerParams(collective_id=cid,has_side_effects=True),name="front")(wq,wk,wv,nx)
 
 
 def dot_nn(a, b):
@@ -905,19 +996,17 @@
 
     attn_r = lax.rsqrt(jnp.mean(hidden * hidden, axis=-1, keepdims=True) + EPS)
     normed = (hidden * attn_r * attn_gain_f).astype(BF)
-    qkv_w, out_w, normed_g = front(
-        query_weight, key_weight, value_weight, output_weight, normed, n_dp, n_ctx, n_exp, 5
-    )
+    qkv_w, normed_g = front(query_weight, key_weight, value_weight, normed, n_dp, n_ctx, n_exp, 5)
     qkv_w = qkv_w.reshape(width, 3 * cols)
-    out_w = out_w.reshape(cols, width)
     normed_g = normed_g.reshape(group, width)
     cot, normed_g = lax.optimization_barrier((cot, normed_g))
     cot_all = lax.all_gather(cot, MOE, axis=0, tiled=False)
     raw = dot_nn(normed_g, qkv_w)
     gains = jnp.stack([q_gain, k_gain])
-    q_rot, k_rot, v_low, mix, inv = attn_fwd(
-        raw, cos, sin, label_row, label_col, gains, n_ctx, heads, 9
+    q_rot, k_rot, v_low, mix, inv, out_w = attn_fwd(
+        raw, cos, sin, label_row, label_col, gains, output_weight, n_dp, n_ctx, n_exp, heads, 9
     )
+    out_w = out_w.reshape(cols, width)
     branch = rs_ctx(dot_nn(mix, out_w).astype(BF).reshape(n_ctx, tok, width), 6)
     residual = hidden + branch.astype(F32)
 
@@ -929,7 +1018,7 @@
     padded = jnp.zeros((experts, width), BF).at[:, :tok].set(gates.T)
     rows_ext = jnp.concatenate([ffn_normed, padded], axis=0)
     gate_mat, up_mat, down_mat = gate_weight[0], up_weight[0], down_weight[0]
-    received, expert_hidden, d_out, d_gate_pre, d_up_pre, moe_part, d_gate_at = fwd_call(
+    received, expert_hidden, d_out, d_gate_pre, d_up_pre, moe_a, moe_b, d_gate_at = fwd_call(
         slot, rows_ext, cot_all, gate_mat, up_mat, down_mat, cap, n_ctx, n_exp, tok
     )
     total = experts * cap
@@ -939,18 +1028,25 @@
     ).T
     received = received.reshape(total, width)
     gate_low = dot_tn(received, d_gate_pre.reshape(total, -1)).astype(BF)
+    moe_a = lax.psum_scatter(
+        moe_a.reshape(experts * tok, width // 2), MOE, scatter_dimension=0, tiled=True
+    )
     up_low = dot_tn(received, d_up_pre.reshape(total, -1)).astype(BF)
-    swap = (gate_low, up_low) if n_dp == 2 else ()
+    down_low = dot_tn(expert_hidden.reshape(total, -1), d_out.reshape(total, width)).astype(BF)
+    most = width * 3 // 4
+    swap = ((gate_low, width), (up_low, most)) if n_dp == 2 else ()
+    d_gate_pre, down_low = lax.optimization_barrier((d_gate_pre, down_low))
     d_tokens, others = back_call(
         slot, d_gate_pre, d_up_pre, gate_mat, up_mat, swap, n_ctx, n_exp, tok, (1, 8)
     )
-    moe_part, d_tokens = lax.optimization_barrier((moe_part, d_tokens))
-    moe_out = lax.psum_scatter(
-        moe_part.reshape(experts * tok, width), MOE, scatter_dimension=0, tiled=True
-    )
-    down_grad = dot_tn(expert_hidden.reshape(total, -1), d_out.reshape(total, width))
-    wide = [(a, b) for a, b in zip(swap, others)] or [low_dp(g, n_dp) for g in (gate_low, up_low)]
-    wide = wide + [low_dp(down_grad, n_dp)]
+    down_low, d_tokens = lax.optimization_barrier((down_low, d_tokens))
+    if swap:
+        wide = [(gate_low, others[0]), (up_low[:most], others[1])]
+        rest_up = low_dp(up_low[most:], n_dp)
+    else:
+        wide = [low_dp(gate_low, n_dp), low_dp(up_low[:most], n_dp)]
+        rest_up = low_dp(up_low[most:], n_dp)
+    wide = wide + [rest_up, low_dp(down_low, n_dp)]
 
     d_router = d_gate
     d_logits = (
@@ -966,6 +1062,11 @@
     )
     d_branch = d_residual.astype(BF)
 
+    moe_b, d_branch = lax.optimization_barrier((moe_b, d_branch))
+    moe_b = lax.psum_scatter(
+        moe_b.reshape(experts * tok, width // 2), MOE, scatter_dimension=0, tiled=True
+    )
+    moe_out = jnp.concatenate([moe_a, moe_b], axis=1)
     d_branch_g = ag_ctx(d_branch, n_ctx, 7).reshape(group, width)
     out_grad = dot_tn(mix, d_branch_g)
     d_mix = dot_nt(d_branch_g, out_w).astype(BF)
@@ -978,26 +1079,25 @@
     ).reshape(2, width)
     small = jnp.concatenate([router_grad, spread, ffn_gain_grad[None]], axis=0)
     small = jnp.pad(small, ((0, 8 - small.shape[0] % 8), (0, 0)))
-    d_part_n = dot_nt(d_raw, qkv_w).astype(BF).reshape(n_ctx, tok, width)
-    qkv_grad = dot_tn(normed_g, d_raw).astype(BF).reshape(n_dp, n_ctx, n_exp, shard, 3 * cols)
     out_part = out_grad.astype(BF).reshape(n_dp, n_exp, shard, width)
-    qkv_sum, out_sum, hidden_grad, small = tail(
-        qkv_grad, out_part, d_part_n, hidden_in[0, 0], d_residual, attn_gain_f[None], small
+    query_sum, key_sum, value_sum, out_sum, hidden_grad, small = tail(
+        normed_g, d_raw, qkv_w, out_part, hidden_in[0, 0], d_residual, attn_gain_f[None], small, n_ctx
+    )
+    query_sum, key_sum, value_sum, out_sum = (
+        x.astype(F32) for x in (query_sum, key_sum, value_sum, out_sum)
     )
     wide, moe_out, small = lax.optimization_barrier((wide, moe_out, small))
     output = (residual + moe_out.astype(F32)).astype(BF)
-    gate_sum, up_sum, down_sum = (sum(x.astype(F32) for x in pair) for pair in wide)
-
-    qkv_sum = qkv_sum.reshape(n_ctx, shard, 3, n_dp, piece)
-    qkv_sum = qkv_sum.transpose(2, 1, 3, 0, 4).reshape(3, shard, width).astype(F32)
-    out_sum = out_sum.astype(F32)
+    gate_sum, up_a, up_b, down_sum = (sum(x.astype(F32) for x in pair) for pair in wide)
+    up_sum = jnp.concatenate([up_a, up_b], axis=0)
+
     return (
         output[None, None],
         hidden_grad[None, None],
         small[-1],
-        qkv_sum[0],
-        qkv_sum[1],
-        qkv_sum[2],
+        query_sum,
+        key_sum,
+        value_sum,
         small[experts],
         small[experts + 1],
         out_sum,

time: 1080 us -> 1030 us (0.954)
  Pallas kernels: 823 us -> 778 us
  matrix products: 136 us -> 105 us
  other arithmetic: 43.4 us -> 56.3 us
    pallas_call x1, Pallas kernels: 108 us -> 79.1 us  [front(): pl.pallas_call(functools.partial(front_kernel, N, C, E, Q), out_shape=[ja...]
    dot_general x6 -> x5, matrix products: 88.9 us -> 72.4 us  [dot_tn(): lax.dot_general(a, b, (((0,), (0,)), ((), ())), preferred_element_type=F32)]
    pallas_call x1, Pallas kernels: 70.8 us -> 55.8 us  [attn_bwd(): pl.pallas_call(functools.partial(attn_bwd_kernel, C, heads, bq, HEAD ** (...]
    dot_general x3 -> x2, matrix products: 25.9 us -> 11.5 us  [dot_nt(): lax.dot_general(a, b, (((1,), (1,)), ((), ())), preferred_element_type=F32)]
    pallas_call x1, Pallas kernels: 186 us -> 198 us  [part(): pl.pallas_call(functools.partial(back_kernel, H, E, cap, X), out_shape=[j...]
  transfers between devices with their start and end apart: 5 -> 7, of which waited for: 1 -> 1; matrix products, arithmetic and copies ran while one was open for 11% -> 13% of each run, Pallas kernels for 33% -> 51%
where the time goes in v4:
time: 1030 us; the launch traced here: 1020 us
  Pallas kernels  778 us (76%)
  matrix products  105 us (10%)
  other arithmetic  56.3 us (5%)
  waiting for transfers between devices  36.9 us (4%)
  starting transfers between devices  20.8 us (2%)
  between operations  14.9 us (1%)
    pallas_call x1, Pallas kernels, part(): pl.pallas_call(functools.partial(back_kernel, H, E, cap, X), out_shape=[j...  198 us
    pallas_call x1, Pallas kernels, fwd_call(): pl.pallas_call(body, out_shape=out_shape, in_specs=[A] * 6, out_specs=[A]...  174 us
    pallas_call x1, Pallas kernels, tail(): pl.pallas_call(functools.partial(tail_kernel, N, C, E), out_shape=[sd] *...  142 us
    pallas_call x1, Pallas kernels, front(): pl.pallas_call(functools.partial(front_kernel, N, C, E, Q), out_shape=[ja...  79.1 us
    dot_general x5, matrix products, dot_tn(): lax.dot_general(a, b, (((0,), (0,)), ((), ())), preferred_element_type=F32)  72.4 us
    pallas_call x1, Pallas kernels, attn_bwd(): pl.pallas_call(functools.partial(attn_bwd_kernel, C, heads, bq, HEAD ** (...  55.8 us
    pallas_call x1, Pallas kernels, ag_ctx(): pl.pallas_call(functools.partial(ag_ctx_kernel, H, Q), out_shape=jax.Shap...  49 us
    pallas_call x1, Pallas kernels, attn_fwd(): pl.pallas_call(functools.partial(attn_fwd_kernel, N, C, E, heads, bq, HEA...  43.2 us
  transfers between devices with their start and end apart: 7, of which 1 were waited for; matrix products, arithmetic and copies ran while one was open for 13% of the time, Pallas kernels for 51%

profile of v4, /device:TPU:8, one launch (start us, length us, event | category | flops | bytes accessed | tf_op | source)
XLA Modules:
  0.0 1021.1 jit_solution(2317467150847414810)
XLA Ops:
  12.8 79.1 %front.1 = (bf16[2,4,4,64,1536]{4,3,2,1,0:T(8,128)(2,1)}, bf16[4,384,2048]{2,1,0:T(8,128)(2,1)}) custom-call(bf16[64,2048]{1,0:T(8,128)(2,1)} %wq.1, bf16[64,2048]{1,0:T(8,128)(2,1)} %wk.1, bf16[64,2048]{1,0:T(8,128)(2,1)} %wv.1, bf16[384,2048]{1,0:T(8,128)(2,1)} %fusion.3.nx), custom_call_target="tpu_custom_call" | custom-call | tf_op jit(solution)/shard_map/front/pallas_call | solution.py:905
  92.7 11.3 %all-to-all-start = ((s32[16,1,384]{2,1,0:T(1,128)}), s32[16,1,384]{2,1,0:T(1,128)S(1)}, u32[]{:S(2)}, u32[]{:S(2)}) async-start(s32[16,1,384]{2,1,0:T(1,128)} %copy.44), calls=%async_computation | async-start | bytes 49152 | tf_op jit(solution)/shard_map/all_to_all | solution.py:976
  109.0 14.1 %fusion.23.raw = f32[1536,1536]{1,0:T(8,128)} fusion(bf16[1536,2048]{1,0:T(8,128)(2,1)} %bitcast.124, bf16[2048,1536]{1,0:T(8,128)(2,1)S(1)} %bitcast.123), kind=kOutput, calls=%fused_computation.73 | convolution fusion | flops 9663676416 | bytes 22020096 | tf_op jit(solution)/shard_map/dot_general | solution.py:913
  123.1 43.2 %attn_fwd.1 = (bf16[1536,512]{1,0:T(8,128)(2,1)S(1)}, bf16[1536,512]{1,0:T(8,128)(2,1)S(1)}, bf16[1536,512]{1,0:T(8,128)(2,1)}, bf16[1536,512]{1,0:T(8,128)(2,1)...) custom-call(f32[1536,1536]{1,0:T(8,128)} %fusion.23.raw, f32[1536,128]{1,0:T(8,128)S(1)} %get-tuple-element.132.cos, ...), custom_call_target="tpu_custom_call" | custom-call | flops 4831838208 | bytes 15728640 | tf_op jit(solution)/shard_map/attn_fwd/pallas_call | solution.py:660
  166.3 6.7 convolution_convert_fusion
  173.1 37.7 %rs_ctx.1 = bf16[384,2048]{1,0:T(8,128)(2,1)S(1)} custom-call(bf16[4,384,2048]{2,1,0:T(8,128)(2,1)S(1)} %bitcast.98), custom_call_target="tpu_custom_call" | custom-call | tf_op jit(solution)/shard_map/rs_ctx/pallas_call | solution.py:799
  217.9 36.8 %all-gather.3.cloned.1.call-done = bf16[6144,2048]{1,0:T(8,128)(2,1)} async-done(((bf16[384,2048]{1,0:T(8,128)(2,1)}), bf16[6144,2048]{1,0:T(8,128)(2,1)}) %all-gather.3.cloned.1.call-update) | async-done | bytes 25165840 | tf_op jit(solution)/shard_map/all_gather | solution.py:1003
  254.7 173.6 %experts_fwd.1 = (bf16[16,240,2048]{2,1,0:T(8,128)(2,1)}, bf16[16,240,1024]{2,1,0:T(8,128)(2,1)}, bf16[16,240,2048]{2,1,0:T(8,128)(2,1)}, bf16[16,240,1024]{2,1,...) custom-call(s32[16,384]{1,0:T(8,128)} %bitcast.111, ...), custom_call_target="tpu_custom_call" | custom-call | flops 82543902720 | bytes 117964800 | tf_op jit(solution)/shard_map/experts_fwd/pallas_call | solution.py:517
  428.4 7.1 all-to-all-start.1
  435.8 24.0 %bitcast_convert_fusion.1 = bf16[1024,2048]{1,0:T(8,128)(2,1)} fusion(bf16[16,240,1024]{2,1,0:T(8,128)(2,1)} %get-tuple-element.79, bf16[16,240,2048]{2,1,0:T(8,128)(2,1)} %get-tuple-element.80), kind=kOutput, calls=%fused_computation.3 | convolution fusion | flops 16108224512 | bytes 27787264 | tf_op jit(solution)/shard_map/dot_general | solution.py:917
  459.8 19.1 %bitcast_convert_fusion.2.rest_0_ = bf16[2048,1024]{1,0:T(8,128)(2,1)} fusion(bf16[16,240,2048]{2,1,0:T(8,128)(2,1)S(1)} %copy-done.37, bf16[16,240,1024]{2,1,0:T(8,128)(2,1)S(1)} %copy-done.38), kind=kOutput, calls=%fused_computation.4 | convolution fusion | flops 16108224512 | bytes 27787264 | tf_op jit(solution)/shard_map/dot_general | solution.py:917
  478.9 19.5 %bitcast_convert_fusion.rest_1_ = bf16[2048,1024]{1,0:T(8,128)(2,1)} fusion(bf16[16,240,2048]{2,1,0:T(8,128)(2,1)S(1)} %copy-done.37, bf16[16,240,1024]{2,1,0:T(8,128)(2,1)S(1)} %bitcast.135), kind=kOutput, calls=%fused_computation.2 | convolution fusion | flops 16108224512 | bytes 27787264 | tf_op jit(solution)/shard_map/dot_general | solution.py:917
  498.5 197.8 %back.1 = (bf16[384,2048]{1,0:T(8,128)(2,1)}, bf16[2048,1024]{1,0:T(8,128)(2,1)}, bf16[1536,1024]{1,0:T(8,128)(2,1)}) custom-call(s32[16,384]{1,0:T(8,128)} %bitcast.112, bf16[16,240,1024]{2,1,0:T(8,128)(2,1)} %get-tuple-element.81.dgp, bf16[16,240,1024]{2,1,0:T(8,128)(2,1)} %get-tuple-element.82.dup, bf16[2048,1024]{1,0:T(8,128)(2,1)} %bitcast.128, ...), custom_call_target="tpu_custom_call" | custom-call | flops 38252052480 | bytes 15728640 | tf_op jit(solution)/shard_map/back/pallas_call | solution.py:359
  696.5 3.4 multiply_reduce_fusion
  699.9 3.5 fusion.17
  707.8 49.0 %ag_ctx.1 = bf16[4,384,2048]{2,1,0:T(8,128)(2,1)} custom-call(bf16[384,2048]{1,0:T(8,128)(2,1)} %get-tuple-element.96.x), custom_call_target="tpu_custom_call" | custom-call | tf_op jit(solution)/shard_map/ag_ctx/pallas_call | solution.py:764
  756.8 8.1 convolution_convert_fusion.2.dm
  764.9 55.8 %attn_bwd.1 = (bf16[1536,1536]{1,0:T(8,128)(2,1)}, f32[2,512]{1,0:T(2,128)}) custom-call(bf16[1536,512]{1,0:T(8,128)(2,1)} %copy-done.9, bf16[1536,512]{1,0:T(8,128)(2,1)} %copy-done.10, bf16[1536,512]{1,0:T(8,128)(2,1)} %get-tuple-element.95.v, bf16[1536,512]{1,0:T(8,128)(2,1)} %convolution_convert_fusion.2.dm, f32[1536,1536]{1,0:T(8,128)} %fusion.23.raw, ...), custom_call_target="tpu_custom_call" | custom-call | flops 12079595520 | bytes 15728640 | tf_op jit(solution)/shard_map/attn_bwd/pallas_call | solution.py:719
  824.1 8.1 convolution_convert_fusion.1
  832.3 141.9 %tail.1 = (bf16[64,2048]{1,0:T(8,128)(2,1)}, bf16[64,2048]{1,0:T(8,128)(2,1)}, bf16[64,2048]{1,0:T(8,128)(2,1)}, bf16[64,2048]{1,0:T(8,128)(2,1)}, bf16[384,2048]{1,0:T(8,128)(2,1)}, /*index=5*/f32[24,2048]{1,0:T(8,128)}) custom-call(bf16[1536,2048]{1,0:T(8,128)(2,1)} %bitcast.125, bf16[1536,1536]{1,0:T(8,128)(2,1)} %get-tuple-element.98.dr, ...), custom_call_target="tpu_custom_call" | custom-call | flops 19327352832 | bytes 17301504 | tf_op jit(solution)/shard_map/tail/pallas_call | solution.py:223
  984.2 3.4 fusion.5
  987.6 8.9 add_bitcast_fusion
  999.6 4.5 maximum_bitcast_fusion
  1004.1 8.9 add_bitcast_fusion.1
  (146 shorter events, 40.6 us)
Async XLA Ops:
  7.2 206.4 %copy-start = (bf16[2048,16]{0,1:T(8,128)(2,1)S(1)}, bf16[2048,16]{0,1:T(8,128)(2,1)}, u32[]{:S(2)}) copy-start(bf16[2048,16]{0,1:T(8,128)(2,1)} %param.29) | copy-start | bytes 196612
  7.2 247.5 %all-gather.3.cloned.1.call-start = ((), (), s32[]{:S(2)}) async-start(), calls=%async_computation.6 | async-start | bytes 26738688 | tf_op jit(solution)/shard_map/all_gather | solution.py:1003
  9.7 82.1 %copy-start.31 = (s32[1,1,384,8]{2,3,1,0:T(8,128)S(1)}, s32[1,1,384,8]{2,3,1,0:T(8,128)}, u32[]{:S(2)}) copy-start(s32[1,1,384,8]{2,3,1,0:T(8,128)} %param.20) | copy-start | bytes 36868
  9.8 94.3 %copy-start.33 = (bf16[2048]{0:T(1024)(128)(2,1)S(1)}, bf16[2048]{0:T(1024)(128)(2,1)}, u32[]{:S(2)}) copy-start(bf16[2048]{0:T(1024)(128)(2,1)} %param.25) | copy-start | bytes 12292
  9.8 94.3 %copy-start.34 = (bf16[2048]{0:T(1024)(128)(2,1)S(1)}, bf16[2048]{0:T(1024)(128)(2,1)}, u32[]{:S(2)}) copy-start(bf16[2048]{0:T(1024)(128)(2,1)} %param.26) | copy-start | bytes 12292
  9.8 94.3 %copy-start.6 = (s32[1,1,1536]{2,1,0:T(1,128)S(1)}, s32[1,1,1536]{2,1,0:T(1,128)}, u32[]{:S(2)}) copy-start(s32[1,1,1536]{2,1,0:T(1,128)} %param.19) | copy-start | bytes 18436
  92.7 124.6 %all-to-all-start = ((s32[16,1,384]{2,1,0:T(1,128)}), s32[16,1,384]{2,1,0:T(1,128)S(1)}, u32[]{:S(2)}, u32[]{:S(2)}) async-start(s32[16,1,384]{2,1,0:T(1,128)} %copy.44), calls=%async_computation | async-start | bytes 49152 | tf_op jit(solution)/shard_map/all_to_all | solution.py:976
  104.0 877.3 %reduce-scatter.3.cloned.1.call-start = ((), (), s32[]{:S(2)}) async-start(), calls=%async_computation.4 | async-start | bytes 13369344 | tf_op jit(solution)/shard_map/reduce_scatter | solution.py:1031
  173.0 37.8 %copy-start.35 = (bf16[2048]{0:T(1024)(128)(2,1)S(1)}, bf16[2048]{0:T(1024)(128)(2,1)}, u32[]{:S(2)}) copy-start(bf16[2048]{0:T(1024)(128)(2,1)} %param.28) | copy-start | bytes 12292
  173.1 38.6 %copy-start.12 = (bf16[1,1,384,2048]{3,2,1,0:T(8,128)(2,1)S(1)}, bf16[1,1,384,2048]{3,2,1,0:T(8,128)(2,1)}, u32[]{:S(2)}) copy-start(bf16[1,1,384,2048]{3,2,1,0:T(8,128)(2,1)} %param.18) | copy-start | bytes 4718596
  428.4 267.9 %all-to-all-start.1 = ((f32[16,1,384]{2,1,0:T(1,128)}), f32[16,1,384]{2,1,0:T(1,128)S(1)}, u32[]{:S(2)}, u32[]{:S(2)}) async-start(f32[16,1,384]{2,1,0:T(1,128)} %get-tuple-element.91), calls=%async_computation.2 | async-start | bytes 49152 | tf_op jit(solution)/shard_map/all_to_all | solution.py:1026
  435.5 545.8 %reduce-scatter.5.cloned.1.call-start = ((), (), s32[]{:S(2)}) async-start(), calls=%async_computation.5 | async-start | bytes 13369344 | tf_op jit(solution)/shard_map/reduce_scatter | solution.py:1066
  435.8 24.0 %copy-start.37 = (bf16[16,240,2048]{2,1,0:T(8,128)(2,1)S(1)}, bf16[16,240,2048]{2,1,0:T(8,128)(2,1)}, u32[]{:S(2)}) copy-start(bf16[16,240,2048]{2,1,0:T(8,128)(2,1)} %get-tuple-element.77) | copy-start | bytes 47185924
  435.8 24.0 %copy-start.38 = (bf16[16,240,1024]{2,1,0:T(8,128)(2,1)S(1)}, bf16[16,240,1024]{2,1,0:T(8,128)(2,1)}, u32[]{:S(2)}) copy-start(bf16[16,240,1024]{2,1,0:T(8,128)(2,1)} %get-tuple-element.81.dgp) | copy-start | bytes 23592964
  435.8 43.1 %slice-start.1 = ((s8[7864320]{0:T(1024)(128)(4,1)}), s8[4194304]{0:T(1024)(128)(4,1)S(1)}, s32[]{:S(2)}) async-start(s8[7864320]{0:T(1024)(128)(4,1)} %bitcast.134), calls=%async_computation.8 | async-start | bytes 8388608
  459.8 19.1 %slice-start.2 = ((s8[7864320]{0:T(1024)(128)(4,1)}), s8[3670016]{0:T(1024)(128)(4,1)S(1)}, s32[]{:S(2)}) async-start(s8[7864320]{0:T(1024)(128)(4,1)} %bitcast.134), calls=%async_computation.9 | async-start | bytes 7340032
  498.4 197.9 %copy-start.20 = (f32[384,16]{0,1:T(8,128)S(1)}, f32[384,16]{0,1:T(8,128)}, u32[]{:S(2)}) copy-start(f32[384,16]{0,1:T(8,128)} %copy-done.19) | copy-start | bytes 73732
  498.4 197.9 %copy-start.25 = (f32[384]{0:T(512)S(1)}, f32[384]{0:T(512)}, u32[]{:S(2)}) copy-start(f32[384]{0:T(512)} %copy-done.24) | copy-start | bytes 4612
  498.4 197.9 %copy-start.28 = (f32[384]{0:T(512)S(1)}, f32[384]{0:T(512)}, u32[]{:S(2)}) copy-start(f32[384]{0:T(512)} %copy-done.27) | copy-start | bytes 4612
  498.4 198.0 %copy-start.2 = (bf16[384,2048]{1,0:T(8,128)(2,1)S(1)}, bf16[384,2048]{1,0:T(8,128)(2,1)}, u32[]{:S(2)}) copy-start(bf16[384,2048]{1,0:T(8,128)(2,1)} %copy-done.1) | copy-start | bytes 4718596
  498.4 198.0 %copy-start.23 = (f32[2048]{0:T(1024)S(1)}, f32[2048]{0:T(1024)}, u32[]{:S(2)}) copy-start(f32[2048]{0:T(1024)} %copy-done.22) | copy-start | bytes 24580
  498.4 198.0 %copy-start.30 = (f32[384]{0:T(512)S(1)}, f32[384]{0:T(512)}, u32[]{:S(2)}) copy-start(f32[384]{0:T(512)} %copy-done.29) | copy-start | bytes 4612
  705.7 277.2 %collective-permute-start.1 = (bf16[1024,2048]{1,0:T(8,128)(2,1)}, bf16[1024,2048]{1,0:T(8,128)(2,1)}, u32[]{:S(2)}, u32[]{:S(2)}) collective-permute-start(bf16[1024,2048]{1,0:T(8,128)(2,1)} %bitcast_convert_fusion.1), channel_id=1, source_target_pairs={{0,16},{16,0},{1,17},{17,1},{2,18},{18,2},{3,19},{19,3},{4,20},{20... | collective-permute-start | bytes 12582920 | tf_op jit(solution)/shard_map/ppermute | solution.py:928
  707.2 275.6 %collective-permute-start = (bf16[512,1024]{1,0:T(8,128)(2,1)S(1)}, bf16[512,1024]{1,0:T(8,128)(2,1)}, u32[]{:S(2)}, u32[]{:S(2)}) collective-permute-start(bf16[512,1024]{1,0:T(8,128)(2,1)S(1)} %slice.45), channel_id=1, source_target_pairs={{0,16},{16,0},{1,17},{17,1},{2,18},{18,2},{3,19},{19,3},{4,20},{20... | collective-permute-start | bytes 3145736 | tf_op jit(solution)/shard_map/ppermute | solution.py:928
  (25 other events, 164.2 us)
Sparse Core Ops, SparseCore 0:
  92.0 162.6 all-gather.2
  428.5 162.9 reduce-scatter.2
  703.5 132.2 reduce-scatter.4

commit v5 on v4

--- a/solution.py
+++ b/solution.py
@@ -43,7 +43,7 @@
     assert not lead
     def body(i,_):
         sl=pl.ds(pl.multiple_of(i*rows,rows),rows)
-        dst[sl,:]=(dst[sl,:].astype(F32)+src[sl,:].astype(F32)).astype(dst.dtype)
+        dst[sl,:]=dst[sl,:]+src[sl,:]
         return 0
     lax.fori_loop(0,n,body,0)
 
@@ -653,7 +653,7 @@
     for r in range(4,E): rows_w.round(r)
     rows_w.finish()
 
-def attn_fwd(raw,cos,sin,lab_r,lab_c,gains,wo,N,C,E,heads,cid,bq=256):
+def attn_fwd(raw,cos,sin,lab_r,lab_c,gains,wo,N,C,E,heads,cid,bq=512):
     G=raw.shape[0]; cols=heads*HEAD; R=2*G//HEAD; dma=pltpu.SemaphoreType.DMA
     o=jax.ShapeDtypeStruct((G,cols),BF)
     V=pl.BlockSpec(memory_space=pltpu.VMEM); A=pl.BlockSpec(memory_space=pl.ANY)
@@ -712,7 +712,7 @@
             draw[sl,t*cols:(t+1)*cols]=(a[sl,:]*r-raw[sl,t*cols:(t+1)*cols]*m).astype(BF)
     loop(nb,fin)
 
-def attn_bwd(q,k,v,dm,raw,inv,cos,sin,lab_r,lab_c,gains,C,heads,cid,bq=256):
+def attn_bwd(q,k,v,dm,raw,inv,cos,sin,lab_r,lab_c,gains,C,heads,cid,bq=512):
     G,cols=q.shape; R=2*G//HEAD; dma=pltpu.SemaphoreType.DMA
     V=pl.BlockSpec(memory_space=pltpu.VMEM)
     acc=pltpu.VMEM((G,cols),F32)
@@ -765,24 +765,32 @@
         scratch_shapes=[dma((H-1,Q)),dma((H-1,Q)),dma((H,Q)),dma((H,Q)),dma(())],
         compiler_params=pltpu.CompilerParams(collective_id=cid,has_side_effects=True),name="ag_ctx")(x)
 
-def rs_ctx_kernel(H,Q,x,o,own,r1,r2,ld,s1,q1,s2,q2,osem):
+def rs_ctx_kernel(H,Q,mix,w,o,own,sd,r1,r2,s1,q1,s2,q2,osem):
     c=lax.axis_index("ctx"); h=c//2; l=c%2
-    T=own.shape[1]; R=T//Q
+    T=own.shape[1]; R=T//Q; D=w.shape[1]
     def sl(q): return pl.ds(q*R,R)
     hs=[lax.rem(h+j,H) for j in range(1,H)]+[h]
-    def load(i): return pltpu.make_async_copy(x.at[hs[i]*2+l],own.at[hs[i]],ld.at[i])
-    for i in range(H): load(i).start()
+    def product(cc,put):
+        rw=pl.ds(pl.multiple_of(cc*T,T),T)
+        def chunk(n):
+            cl=pl.ds(pl.multiple_of(n*512,512),512)
+            put[:,cl]=nn(mix[rw,:],w[:,cl]).astype(BF)
+        loop(D//512,chunk)
+    def c1(i,q): return pltpu.make_async_remote_copy(sd.at[hs[i],sl(q)],r1.at[hs[i],sl(q)],s1.at[hs[i],q],q1.at[hs[i],q],device_id={"ctx":h*2+1-l},device_id_type=MESH)
+    def c2(j,q): return pltpu.make_async_remote_copy(own.at[hs[j-1],sl(q)],r2.at[j-1,sl(q)],s2.at[j-1,q],q2.at[j-1,q],device_id={"ctx":hs[j-1]*2+l},device_id_type=MESH)
     ctx_barrier(H,c,h,l)
-    def c1(i,q): return pltpu.make_async_remote_copy(x.at[hs[i]*2+1-l,sl(q)],r1.at[hs[i],sl(q)],s1.at[hs[i],q],q1.at[hs[i],q],device_id={"ctx":h*2+1-l},device_id_type=MESH)
-    def c2(j,q): return pltpu.make_async_remote_copy(own.at[hs[j-1],sl(q)],r2.at[j-1,sl(q)],s2.at[j-1,q],q2.at[j-1,q],device_id={"ctx":hs[j-1]*2+l},device_id_type=MESH)
     for i in range(H):
+        product(hs[i]*2+1-l,sd.at[hs[i]])
         for q in range(Q): c1(i,q).start()
-    for i in range(H):
-        load(i).wait()
-        for q in range(Q):
-            c1(i,q).wait_recv()
-            add_into(own.at[hs[i],sl(q)],r1.at[hs[i],sl(q)])
-            if i<H-1: c2(i+1,q).start()
+        product(hs[i]*2+l,own.at[hs[i]])
+        if i<H-1:
+            for q in range(Q):
+                c1(i,q).wait_recv()
+                add_into(own.at[hs[i],sl(q)],r1.at[hs[i],sl(q)])
+                c2(i+1,q).start()
+    for q in range(Q):
+        c1(H-1,q).wait_recv()
+        add_into(own.at[h,sl(q)],r1.at[h,sl(q)])
     for q in range(Q):
         for j in range(1,H):
             c2(j,q).wait_recv()
@@ -793,12 +801,15 @@
         for j in range(1,H): c2(j,q).wait_send()
     out.wait()
 
-def rs_ctx(x,cid,Q=4):
-    C,T,D=x.shape; H=C//2; dma=pltpu.SemaphoreType.DMA
-    A=pl.BlockSpec(memory_space=pl.ANY)
-    return pl.pallas_call(functools.partial(rs_ctx_kernel,H,Q),out_shape=jax.ShapeDtypeStruct((T,D),x.dtype),in_specs=[A],out_specs=A,
-        scratch_shapes=[pltpu.VMEM((H,T,D),BF),pltpu.VMEM((H,T,D),BF),pltpu.VMEM((H-1,T,D),BF),dma((H,)),dma((H,Q)),dma((H,Q)),dma((H-1,Q)),dma((H-1,Q)),dma(())],
-        compiler_params=pltpu.CompilerParams(collective_id=cid,has_side_effects=True,vmem_limit_bytes=40*2**20),name="rs_ctx")(x)
+
+def rs_ctx(mix,w,C,cid,Q=4):
+    G,cols=mix.shape; D=w.shape[1]; T=G//C; H=C//2; dma=pltpu.SemaphoreType.DMA
+    A=pl.BlockSpec(memory_space=pl.ANY); V=pl.BlockSpec(memory_space=pltpu.VMEM)
+    buf=pltpu.VMEM((H,T,D),BF)
+    return pl.pallas_call(functools.partial(rs_ctx_kernel,H,Q),out_shape=jax.ShapeDtypeStruct((T,D),BF),in_specs=[V,V],out_specs=A,
+        scratch_shapes=[buf,buf,buf,pltpu.VMEM((H-1,T,D),BF),dma((H,Q)),dma((H,Q)),dma((H-1,Q)),dma((H-1,Q)),dma(())],
+        cost_estimate=pl.CostEstimate(flops=2*G*cols*D,bytes_accessed=2*(G*cols+cols*D+T*D),transcendentals=0),
+        compiler_params=pltpu.CompilerParams(collective_id=cid,has_side_effects=True,vmem_limit_bytes=40*2**20),name="rs_ctx")(mix,w)
 
 
 def front_kernel(N,C,E,Q,wq,wk,wv,nx,qkv,na,a_s,a_r,up_s,up_r,dn_s,dn_r,y_s,y_r,xs_,xr_,bs_,br_,lsem):
@@ -909,6 +920,27 @@
         compiler_params=pltpu.CompilerParams(collective_id=cid,has_side_effects=True),name="front")(wq,wk,wv,nx)
 
 
+def add_kernel(split,*refs):
+    g,og,u,oa,ob,d,od,sg,su,sd=refs
+    i=pl.program_id(0)
+    sg[...]=g[...].astype(F32)+og[...].astype(F32)
+    su[...]=u[...].astype(F32)+jnp.where(i<split,oa[...].astype(F32),ob[...].astype(F32))
+    sd[...]=d[...].astype(F32)+od[...].astype(F32)
+
+
+def add_shares(g,og,u,oa,ob,d,od,steps=16):
+    D,FF=g.shape; F2,D2=d.shape
+    r,r2=D//steps,F2//steps
+    split=oa.shape[0]//r
+    wide=pl.BlockSpec((r,FF),lambda i:(i,0)); tall=pl.BlockSpec((r2,D2),lambda i:(i,0))
+    return pl.pallas_call(functools.partial(add_kernel,split),grid=(steps,),
+        in_specs=[wide,wide,wide,pl.BlockSpec((r,FF),lambda i:(jnp.minimum(i,split-1),0)),pl.BlockSpec((r,FF),lambda i:(jnp.maximum(i-split,0),0)),tall,tall],
+        out_specs=[wide,wide,tall],
+        out_shape=[jax.ShapeDtypeStruct((D,FF),F32)]*2+[jax.ShapeDtypeStruct((F2,D2),F32)],
+        cost_estimate=pl.CostEstimate(flops=6*D*FF,bytes_accessed=24*D*FF,transcendentals=0),
+        compiler_params=pltpu.CompilerParams(dimension_semantics=("arbitrary",),vmem_limit_bytes=32*2**20),name="add_shares")(g,og,u,oa,ob,d,od)
+
+
 def dot_nn(a, b):
     return lax.dot_general(a, b, (((1,), (0,)), ((), ())), preferred_element_type=F32)
 
@@ -919,13 +951,6 @@
 
 def dot_nt(a, b):
     return lax.dot_general(a, b, (((1,), (1,)), ((), ())), preferred_element_type=F32)
-
-
-def low_dp(grad, n_dp):
-    low = grad.astype(BF)
-    if n_dp != 2:
-        return (lax.psum(low, "dp"),)
-    return low, lax.ppermute(low, "dp", [(0, 1), (1, 0)])
 
 
 def per_device(
@@ -1007,7 +1032,7 @@
         raw, cos, sin, label_row, label_col, gains, output_weight, n_dp, n_ctx, n_exp, heads, 9
     )
     out_w = out_w.reshape(cols, width)
-    branch = rs_ctx(dot_nn(mix, out_w).astype(BF).reshape(n_ctx, tok, width), 6)
+    branch = rs_ctx(mix, out_w, n_ctx, 6)
     residual = hidden + branch.astype(F32)
 
     ffn_r = lax.rsqrt(jnp.mean(residual * residual, axis=-1, keepdims=True) + EPS)
@@ -1041,12 +1066,10 @@
     )
     down_low, d_tokens = lax.optimization_barrier((down_low, d_tokens))
     if swap:
-        wide = [(gate_low, others[0]), (up_low[:most], others[1])]
-        rest_up = low_dp(up_low[most:], n_dp)
+        pair = lambda x: lax.ppermute(x, "dp", [(0, 1), (1, 0)])
+        wide = (gate_low, others[0], up_low, others[1], pair(up_low[most:]), down_low, pair(down_low))
     else:
-        wide = [low_dp(gate_low, n_dp), low_dp(up_low[:most], n_dp)]
-        rest_up = low_dp(up_low[most:], n_dp)
-    wide = wide + [rest_up, low_dp(down_low, n_dp)]
+        wide = tuple(lax.psum(x, "dp") for x in (gate_low, up_low, down_low))
 
     d_router = d_gate
     d_logits = (
@@ -1088,9 +1111,9 @@
     )
     wide, moe_out, small = lax.optimization_barrier((wide, moe_out, small))
     output = (residual + moe_out.astype(F32)).astype(BF)
-    gate_sum, up_a, up_b, down_sum = (sum(x.astype(F32) for x in pair) for pair in wide)
-    up_sum = jnp.concatenate([up_a, up_b], axis=0)
-
+    gate_sum, up_sum, down_sum = (
+        add_shares(*wide) if n_dp == 2 else (x.astype(F32) for x in wide)
+    )
     return (
         output[None, None],
         hidden_grad[None, None],

time: 1030 us -> 1020 us (level)
  other arithmetic: 56.3 us -> 31.2 us
  Pallas kernels: 778 us -> 790 us
  local copies, waits for them, and re-layouts: 8.64 us -> 19.4 us
    broadcast_in_dim x3 -> x0, other arithmetic: 22.4 us -> none  [the longest x1 8.94 us: per_device(): gate_sum[None]]
    pallas_call x0 -> x1, Pallas kernels: none -> 14 us  [add_shares(): pl.pallas_call(functools.partial(add_kernel, split), grid=(steps,), in_sp...]
    dot_general x4 -> x3, matrix products: 21.5 us -> 14.9 us  [dot_nn(): lax.dot_general(a, b, (((1,), (0,)), ((), ())), preferred_element_type=F32)]
  transfers between devices with their start and end apart: 7 -> 7, of which waited for: 1 -> 1; matrix products, arithmetic and copies ran while one was open for 13% -> 12% of each run, Pallas kernels for 51% -> 52%
where the time goes in v5:
time: 1020 us; the launch traced here: 1010 us
  Pallas kernels  790 us (77%)
  matrix products  98.7 us (10%)
  waiting for transfers between devices  35.1 us (3%)
  other arithmetic  31.2 us (3%)
  starting transfers between devices  21 us (2%)
  local copies, waits for them, and re-layouts  19.4 us (2%)
  between operations  14.9 us (1%)
    pallas_call x1, Pallas kernels, part(): pl.pallas_call(functools.partial(back_kernel, H, E, cap, X), out_shape=[j...  197 us
    pallas_call x1, Pallas kernels, fwd_call(): pl.pallas_call(body, out_shape=out_shape, in_specs=[A] * 6, out_specs=[A]...  173 us
    pallas_call x1, Pallas kernels, tail(): pl.pallas_call(functools.partial(tail_kernel, N, C, E), out_shape=[sd] *...  141 us
    pallas_call x1, Pallas kernels, front(): pl.pallas_call(functools.partial(front_kernel, N, C, E, Q), out_shape=[ja...  79.1 us
    dot_general x5, matrix products, dot_tn(): lax.dot_general(a, b, (((0,), (0,)), ((), ())), preferred_element_type=F32)  72.3 us
    pallas_call x1, Pallas kernels, attn_bwd(): pl.pallas_call(functools.partial(attn_bwd_kernel, C, heads, bq, HEAD ** (...  51.4 us
    pallas_call x1, Pallas kernels, ag_ctx(): pl.pallas_call(functools.partial(ag_ctx_kernel, H, Q), out_shape=jax.Shap...  49 us
    pallas_call x1, Pallas kernels, attn_fwd(): pl.pallas_call(functools.partial(attn_fwd_kernel, N, C, E, heads, bq, HEA...  44.2 us
  transfers between devices with their start and end apart: 7, of which 1 were waited for; matrix products, arithmetic and copies ran while one was open for 12% of the time, Pallas kernels for 52%

profile of v5, /device:TPU:8, one launch (start us, length us, event | category | flops | bytes accessed | tf_op | source)
XLA Modules:
  0.0 1009.9 jit_solution(10215439192370019392)
XLA Ops:
  9.8 3.0 fusion.3.nx
  12.8 79.1 %front.1 = (bf16[2,4,4,64,1536]{4,3,2,1,0:T(8,128)(2,1)}, bf16[4,384,2048]{2,1,0:T(8,128)(2,1)}) custom-call(bf16[64,2048]{1,0:T(8,128)(2,1)} %wq.1, bf16[64,2048]{1,0:T(8,128)(2,1)} %wk.1, bf16[64,2048]{1,0:T(8,128)(2,1)} %wv.1, bf16[384,2048]{1,0:T(8,128)(2,1)} %fusion.3.nx), custom_call_target="tpu_custom_call" | custom-call | tf_op jit(solution)/shard_map/front/pallas_call | solution.py:916
  92.8 11.3 %all-to-all-start = ((s32[16,1,384]{2,1,0:T(1,128)}), s32[16,1,384]{2,1,0:T(1,128)S(1)}, u32[]{:S(2)}, u32[]{:S(2)}) async-start(s32[16,1,384]{2,1,0:T(1,128)} %copy.44), calls=%async_computation | async-start | bytes 49152 | tf_op jit(solution)/shard_map/all_to_all | solution.py:1001
  106.4 2.8 fusion.8
  109.7 14.2 %fusion.23.raw = f32[1536,1536]{1,0:T(8,128)} fusion(bf16[1536,2048]{1,0:T(8,128)(2,1)} %bitcast.122, bf16[2048,1536]{1,0:T(8,128)(2,1)S(1)} %bitcast.121), kind=kOutput, calls=%fused_computation.67 | convolution fusion | flops 9663676416 | bytes 22020096 | tf_op jit(solution)/shard_map/dot_general | solution.py:945
  124.0 44.2 %attn_fwd.1 = (bf16[1536,512]{1,0:T(8,128)(2,1)S(1)}, bf16[1536,512]{1,0:T(8,128)(2,1)S(1)}, bf16[1536,512]{1,0:T(8,128)(2,1)}, bf16[1536,512]{1,0:T(8,128)(2,1)...) custom-call(f32[1536,1536]{1,0:T(8,128)} %fusion.23.raw, f32[1536,128]{1,0:T(8,128)S(1)} %get-tuple-element.136.cos, ...), custom_call_target="tpu_custom_call" | custom-call | flops 4831838208 | bytes 15728640 | tf_op jit(solution)/shard_map/attn_fwd/pallas_call | solution.py:660
  168.2 2.7 copy-done.14
  172.4 40.3 %rs_ctx.1 = bf16[384,2048]{1,0:T(8,128)(2,1)S(1)} custom-call(bf16[1536,512]{1,0:T(8,128)(2,1)S(1)} %copy-done.15, bf16[512,2048]{1,0:T(8,128)(2,1)S(1)} %bitcast.96), custom_call_target="tpu_custom_call" | custom-call | flops 3221225472 | bytes 5242880 | tf_op jit(solution)/shard_map/rs_ctx/pallas_call | solution.py:809
  219.7 35.0 %all-gather.3.cloned.1.call-done = bf16[6144,2048]{1,0:T(8,128)(2,1)} async-done(((bf16[384,2048]{1,0:T(8,128)(2,1)}), bf16[6144,2048]{1,0:T(8,128)(2,1)}) %all-gather.3.cloned.1.call-update) | async-done | bytes 25165840 | tf_op jit(solution)/shard_map/all_gather | solution.py:1028
  254.7 173.4 %experts_fwd.1 = (bf16[16,240,2048]{2,1,0:T(8,128)(2,1)}, bf16[16,240,1024]{2,1,0:T(8,128)(2,1)}, bf16[16,240,2048]{2,1,0:T(8,128)(2,1)}, bf16[16,240,1024]{2,1,...) custom-call(s32[16,384]{1,0:T(8,128)} %bitcast.106, ...), custom_call_target="tpu_custom_call" | custom-call | flops 82543902720 | bytes 117964800 | tf_op jit(solution)/shard_map/experts_fwd/pallas_call | solution.py:517
  428.2 7.2 all-to-all-start.1
  435.9 24.0 %bitcast_convert_fusion.1.refs_5_ = bf16[1024,2048]{1,0:T(8,128)(2,1)} fusion(bf16[16,240,1024]{2,1,0:T(8,128)(2,1)} %get-tuple-element.81, bf16[16,240,2048]{2,1,0:T(8,128)(2,1)} %get-tuple-element.82), kind=kOutput, calls=%fused_computation.2 | convolution fusion | flops 16108224512 | bytes 27787264 | tf_op jit(solution)/shard_map/dot_general | solution.py:949
  459.9 19.1 %bitcast_convert_fusion.2.rest_0_.refs_0_ = bf16[2048,1024]{1,0:T(8,128)(2,1)} fusion(bf16[16,240,2048]{2,1,0:T(8,128)(2,1)S(1)} %copy-done.42, bf16[16,240,1024]{2,1,0:T(8,128)(2,1)S(1)} %copy-done.43), kind=kOutput, calls=%fused_computation.3 | convolution fusion | flops 16108224512 | bytes 27787264 | tf_op jit(solution)/shard_map/dot_general | solution.py:949
  479.0 19.3 %bitcast_convert_fusion.rest_1_.refs_2_ = bf16[2048,1024]{1,0:T(8,128)(2,1)} fusion(bf16[16,240,2048]{2,1,0:T(8,128)(2,1)S(1)} %copy-done.42, bf16[16,240,1024]{2,1,0:T(8,128)(2,1)S(1)} %bitcast.131), kind=kOutput, calls=%fused_computation.1 | convolution fusion | flops 16108224512 | bytes 27787264 | tf_op jit(solution)/shard_map/dot_general | solution.py:949
  498.3 196.8 %back.1 = (bf16[384,2048]{1,0:T(8,128)(2,1)}, bf16[2048,1024]{1,0:T(8,128)(2,1)}, bf16[1536,1024]{1,0:T(8,128)(2,1)}) custom-call(s32[16,384]{1,0:T(8,128)} %bitcast.107, bf16[16,240,1024]{2,1,0:T(8,128)(2,1)} %get-tuple-element.83.dgp, bf16[16,240,1024]{2,1,0:T(8,128)(2,1)} %get-tuple-element.84.dup, bf16[2048,1024]{1,0:T(8,128)(2,1)} %bitcast.126, ...), custom_call_target="tpu_custom_call" | custom-call | flops 38252052480 | bytes 15728640 | tf_op jit(solution)/shard_map/back/pallas_call | solution.py:359
  695.3 3.4 multiply_reduce_fusion
  698.7 3.5 fusion.17
  706.5 49.0 %ag_ctx.1 = bf16[4,384,2048]{2,1,0:T(8,128)(2,1)} custom-call(bf16[384,2048]{1,0:T(8,128)(2,1)} %get-tuple-element.98.x), custom_call_target="tpu_custom_call" | custom-call | tf_op jit(solution)/shard_map/ag_ctx/pallas_call | solution.py:764
  755.5 8.1 convolution_convert_fusion.1.dm
  763.6 51.4 %attn_bwd.1 = (bf16[1536,1536]{1,0:T(8,128)(2,1)}, f32[2,512]{1,0:T(2,128)}) custom-call(bf16[1536,512]{1,0:T(8,128)(2,1)} %copy-done.16, bf16[1536,512]{1,0:T(8,128)(2,1)} %copy-done.17, bf16[1536,512]{1,0:T(8,128)(2,1)} %get-tuple-element.97.v, bf16[1536,512]{1,0:T(8,128)(2,1)} %convolution_convert_fusion.1.dm, f32[1536,1536]{1,0:T(8,128)} %fusion.23.raw, ...), custom_call_target="tpu_custom_call" | custom-call | flops 12079595520 | bytes 15728640 | tf_op jit(solution)/shard_map/attn_bwd/pallas_call | solution.py:719
  818.2 8.2 convolution_convert_fusion
  826.4 141.5 %tail.1 = (bf16[64,2048]{1,0:T(8,128)(2,1)}, bf16[64,2048]{1,0:T(8,128)(2,1)}, bf16[64,2048]{1,0:T(8,128)(2,1)}, bf16[64,2048]{1,0:T(8,128)(2,1)}, bf16[384,2048]{1,0:T(8,128)(2,1)}, /*index=5*/f32[24,2048]{1,0:T(8,128)}) custom-call(bf16[1536,2048]{1,0:T(8,128)(2,1)} %bitcast.123, bf16[1536,1536]{1,0:T(8,128)(2,1)} %get-tuple-element.100.dr, ...), custom_call_target="tpu_custom_call" | custom-call | flops 19327352832 | bytes 17301504 | tf_op jit(solution)/shard_map/tail/pallas_call | solution.py:223
  978.0 3.5 fusion.5
  987.8 14.0 %add_shares.1 = (f32[2048,1024]{1,0:T(8,128)}, f32[2048,1024]{1,0:T(8,128)}, f32[1024,2048]{1,0:T(8,128)}) custom-call(bf16[2048,1024]{1,0:T(8,128)(2,1)S(1)} %copy-done.5, bf16[2048,1024]{1,0:T(8,128)(2,1)S(1)} %copy-done.6, bf16[2048,1024]{1,0:T(8,128)(2,1)S(1)} %copy-done.3, bf16[1536,1024]{1,0:T(8,128)(2,1)S(1)} %copy-done.7, ...), custom_call_target="tpu_custom_call" | custom-call | flops 12582912 | bytes 50331648 | tf_op jit(solution)/shard_map/add_shares/pallas_call | solution.py:936
  (149 shorter events, 40.2 us)
Async XLA Ops:
  7.2 208.1 %copy-start = (bf16[2048,16]{0,1:T(8,128)(2,1)S(1)}, bf16[2048,16]{0,1:T(8,128)(2,1)}, u32[]{:S(2)}) copy-start(bf16[2048,16]{0,1:T(8,128)(2,1)} %param.29) | copy-start | bytes 196612
  7.2 247.5 %all-gather.3.cloned.1.call-start = ((), (), s32[]{:S(2)}) async-start(), calls=%async_computation.6 | async-start | bytes 26738688 | tf_op jit(solution)/shard_map/all_gather | solution.py:1028
  9.7 82.1 %copy-start.36 = (s32[1,1,384,8]{2,3,1,0:T(8,128)S(1)}, s32[1,1,384,8]{2,3,1,0:T(8,128)}, u32[]{:S(2)}) copy-start(s32[1,1,384,8]{2,3,1,0:T(8,128)} %param.20) | copy-start | bytes 36868
  9.8 94.3 %copy-start.38 = (bf16[2048]{0:T(1024)(128)(2,1)S(1)}, bf16[2048]{0:T(1024)(128)(2,1)}, u32[]{:S(2)}) copy-start(bf16[2048]{0:T(1024)(128)(2,1)} %param.25) | copy-start | bytes 12292
  9.8 94.3 %copy-start.39 = (bf16[2048]{0:T(1024)(128)(2,1)S(1)}, bf16[2048]{0:T(1024)(128)(2,1)}, u32[]{:S(2)}) copy-start(bf16[2048]{0:T(1024)(128)(2,1)} %param.26) | copy-start | bytes 12292
  9.8 94.3 %copy-start.11 = (s32[1,1,1536]{2,1,0:T(1,128)S(1)}, s32[1,1,1536]{2,1,0:T(1,128)}, u32[]{:S(2)}) copy-start(s32[1,1,1536]{2,1,0:T(1,128)} %param.19) | copy-start | bytes 18436
  12.8 91.7 %copy-start.40 = (bf16[2048]{0:T(1024)(128)(2,1)S(1)}, bf16[2048]{0:T(1024)(128)(2,1)}, u32[]{:S(2)}) copy-start(bf16[2048]{0:T(1024)(128)(2,1)} %param.28) | copy-start | bytes 12292
  92.8 126.3 %all-to-all-start = ((s32[16,1,384]{2,1,0:T(1,128)}), s32[16,1,384]{2,1,0:T(1,128)S(1)}, u32[]{:S(2)}, u32[]{:S(2)}) async-start(s32[16,1,384]{2,1,0:T(1,128)} %copy.44), calls=%async_computation | async-start | bytes 49152 | tf_op jit(solution)/shard_map/all_to_all | solution.py:1001
  104.0 871.0 %reduce-scatter.3.cloned.1.call-start = ((), (), s32[]{:S(2)}) async-start(), calls=%async_computation.4 | async-start | bytes 13369344 | tf_op jit(solution)/shard_map/reduce_scatter | solution.py:1056
  104.5 109.4 %copy-start.27 = (f32[2048]{0:T(1024)}, f32[2048]{0:T(1024)S(1)}, u32[]{:S(2)}) copy-start(f32[2048]{0:T(1024)S(1)} %convert_element_type.101) | copy-start | bytes 24580
  168.2 44.5 %copy-start.16 = (bf16[1536,512]{1,0:T(8,128)(2,1)}, bf16[1536,512]{1,0:T(8,128)(2,1)S(1)}, u32[]{:S(2)}) copy-start(bf16[1536,512]{1,0:T(8,128)(2,1)S(1)} %get-tuple-element.95.q) | copy-start | bytes 4718596
  168.2 44.5 %copy-start.17 = (bf16[1536,512]{1,0:T(8,128)(2,1)}, bf16[1536,512]{1,0:T(8,128)(2,1)S(1)}, u32[]{:S(2)}) copy-start(bf16[1536,512]{1,0:T(8,128)(2,1)S(1)} %get-tuple-element.96.k) | copy-start | bytes 4718596
  168.2 44.5 %copy-start.18 = (f32[24,128]{1,0:T(8,128)}, f32[24,128]{1,0:T(8,128)S(1)}, u32[]{:S(2)}) copy-start(f32[24,128]{1,0:T(8,128)S(1)} %get-tuple-element.99.inv) | copy-start | bytes 36868
  428.2 266.9 %all-to-all-start.1 = ((f32[16,1,384]{2,1,0:T(1,128)}), f32[16,1,384]{2,1,0:T(1,128)S(1)}, u32[]{:S(2)}, u32[]{:S(2)}) async-start(f32[16,1,384]{2,1,0:T(1,128)} %get-tuple-element.93), calls=%async_computation.2 | async-start | bytes 49152 | tf_op jit(solution)/shard_map/all_to_all | solution.py:1051
  435.4 539.6 %reduce-scatter.5.cloned.1.call-start = ((), (), s32[]{:S(2)}) async-start(), calls=%async_computation.5 | async-start | bytes 13369344 | tf_op jit(solution)/shard_map/reduce_scatter | solution.py:1089
  435.9 43.1 %slice-start = ((s8[7864320]{0:T(1024)(128)(4,1)}), s8[4194304]{0:T(1024)(128)(4,1)S(1)}, s32[]{:S(2)}) async-start(s8[7864320]{0:T(1024)(128)(4,1)} %bitcast.130), calls=%async_computation.7 | async-start | bytes 8388608
  498.3 196.9 %copy-start.25 = (f32[384,16]{0,1:T(8,128)S(1)}, f32[384,16]{0,1:T(8,128)}, u32[]{:S(2)}) copy-start(f32[384,16]{0,1:T(8,128)} %copy-done.24) | copy-start | bytes 73732
  498.3 196.9 %copy-start.30 = (f32[384]{0:T(512)S(1)}, f32[384]{0:T(512)}, u32[]{:S(2)}) copy-start(f32[384]{0:T(512)} %copy-done.29) | copy-start | bytes 4612
  498.3 196.9 %copy-start.33 = (f32[384]{0:T(512)S(1)}, f32[384]{0:T(512)}, u32[]{:S(2)}) copy-start(f32[384]{0:T(512)} %copy-done.32) | copy-start | bytes 4612
  498.3 196.9 %copy-start.2 = (bf16[384,2048]{1,0:T(8,128)(2,1)S(1)}, bf16[384,2048]{1,0:T(8,128)(2,1)}, u32[]{:S(2)}) copy-start(bf16[384,2048]{1,0:T(8,128)(2,1)} %copy-done.1) | copy-start | bytes 4718596
  498.3 196.9 %copy-start.28 = (f32[2048]{0:T(1024)S(1)}, f32[2048]{0:T(1024)}, u32[]{:S(2)}) copy-start(f32[2048]{0:T(1024)} %copy-done.27) | copy-start | bytes 24580
  498.3 196.9 %copy-start.35 = (f32[384]{0:T(512)S(1)}, f32[384]{0:T(512)}, u32[]{:S(2)}) copy-start(f32[384]{0:T(512)} %copy-done.34) | copy-start | bytes 4612
  704.5 272.2 %collective-permute-start.1 = (bf16[1024,2048]{1,0:T(8,128)(2,1)}, bf16[1024,2048]{1,0:T(8,128)(2,1)}, u32[]{:S(2)}, u32[]{:S(2)}) collective-permute-start(bf16[1024,2048]{1,0:T(8,128)(2,1)} %bitcast_convert_fusion.1.refs_5_), channel_id=1, source_target_pairs={{0,16},{16,0},{1,17},{17,1},{2,18},{18,2},{3,19},{19,3},{4,20},{20... | collective-permute-start | bytes 12582920 | tf_op jit(solution)/shard_map/ppermute | solution.py:1069
  706.1 270.7 %collective-permute-start = (bf16[512,1024]{1,0:T(8,128)(2,1)}, bf16[512,1024]{1,0:T(8,128)(2,1)S(1)}, u32[]{:S(2)}, u32[]{:S(2)}) collective-permute-start(bf16[512,1024]{1,0:T(8,128)(2,1)} %slice.40), channel_id=1, source_target_pairs={{0,16},{16,0},{1,17},{17,1},{2,18},{18,2},{3,19},{19,3},{4,20},{20... | collective-permute-start | bytes 3145736 | tf_op jit(solution)/shard_map/ppermute | solution.py:1069
  (29 other events, 255.8 us)
Sparse Core Ops, SparseCore 0:
  92.0 162.6 all-gather.2
  428.3 163.4 reduce-scatter.2
  702.3 132.5 reduce-scatter.4

commit v6 on v5

--- a/solution.py
+++ b/solution.py
@@ -162,7 +162,7 @@
         own_d[h,sl,:]=(rv[sl,:]+(w*r-x*(r*r*r)*jnp.mean(x*w,axis=1,keepdims=True))).astype(BF)
     def lines(k):
         line(k)
-        @pl.when(k==0)
+        @pl.when(k==1)
         def _():
             for j in range(1,H):
                 c2(j).wait_recv(); add_into(own_d.at[h],d2.at[j-1])
@@ -170,10 +170,10 @@
             loop(T//RB,epilogue)
             send(0)
             pltpu.make_async_copy(own_d.at[h],od,osem.at[0]).start()
-        @pl.when(k==1)
+        @pl.when(k==2)
         def _():
             b1[c]=gathered(0); send(1)
-        @pl.when(k==2)
+        @pl.when(k==3)
         def _():
             b2[e]=gathered(1); send(2)
     loop(E,lines)

time: 1020 us -> 1010 us (level)
  no operation moved by 1% of the time
where the time goes in v6:
time: 1010 us
  Pallas kernels  785 us (78%)
  matrix products  98.7 us (10%)
  waiting for transfers between devices  35.1 us (3%)
  other arithmetic  31.2 us (3%)
  starting transfers between devices  21 us (2%)
  local copies, waits for them, and re-layouts  19.4 us (2%)
  between operations  14.9 us (1%)
    pallas_call x1, Pallas kernels, part(): pl.pallas_call(functools.partial(back_kernel, H, E, cap, X), out_shape=[j...  197 us
    pallas_call x1, Pallas kernels, fwd_call(): pl.pallas_call(body, out_shape=out_shape, in_specs=[A] * 6, out_specs=[A]...  173 us
    pallas_call x1, Pallas kernels, tail(): pl.pallas_call(functools.partial(tail_kernel, N, C, E), out_shape=[sd] *...  137 us
    pallas_call x1, Pallas kernels, front(): pl.pallas_call(functools.partial(front_kernel, N, C, E, Q), out_shape=[ja...  79.1 us
    dot_general x5, matrix products, dot_tn(): lax.dot_general(a, b, (((0,), (0,)), ((), ())), preferred_element_type=F32)  72.3 us
    pallas_call x1, Pallas kernels, attn_bwd(): pl.pallas_call(functools.partial(attn_bwd_kernel, C, heads, bq, HEAD ** (...  51.4 us
    pallas_call x1, Pallas kernels, ag_ctx(): pl.pallas_call(functools.partial(ag_ctx_kernel, H, Q), out_shape=jax.Shap...  49 us
    pallas_call x1, Pallas kernels, attn_fwd(): pl.pallas_call(functools.partial(attn_fwd_kernel, N, C, E, heads, bq, HEA...  44.2 us
  transfers between devices with their start and end apart: 7, of which 1 were waited for; matrix products, arithmetic and copies ran while one was open for 12% of the time, Pallas kernels for 52%

profile of v6, /device:TPU:8, one launch (start us, length us, event | category | flops | bytes accessed | tf_op | source)
XLA Modules:
  0.0 1005.3 jit_solution(10988647932625984500)
XLA Ops:
  9.8 3.0 fusion.3.nx
  12.8 79.1 %front.1 = (bf16[2,4,4,64,1536]{4,3,2,1,0:T(8,128)(2,1)}, bf16[4,384,2048]{2,1,0:T(8,128)(2,1)}) custom-call(bf16[64,2048]{1,0:T(8,128)(2,1)} %wq.1, bf16[64,2048]{1,0:T(8,128)(2,1)} %wk.1, bf16[64,2048]{1,0:T(8,128)(2,1)} %wv.1, bf16[384,2048]{1,0:T(8,128)(2,1)} %fusion.3.nx), custom_call_target="tpu_custom_call" | custom-call | tf_op jit(solution)/shard_map/front/pallas_call | solution.py:916
  92.8 11.3 %all-to-all-start = ((s32[16,1,384]{2,1,0:T(1,128)}), s32[16,1,384]{2,1,0:T(1,128)S(1)}, u32[]{:S(2)}, u32[]{:S(2)}) async-start(s32[16,1,384]{2,1,0:T(1,128)} %copy.44), calls=%async_computation | async-start | bytes 49152 | tf_op jit(solution)/shard_map/all_to_all | solution.py:1001
  106.4 2.8 fusion.8
  109.7 14.2 %fusion.23.raw = f32[1536,1536]{1,0:T(8,128)} fusion(bf16[1536,2048]{1,0:T(8,128)(2,1)} %bitcast.122, bf16[2048,1536]{1,0:T(8,128)(2,1)S(1)} %bitcast.121), kind=kOutput, calls=%fused_computation.67 | convolution fusion | flops 9663676416 | bytes 22020096 | tf_op jit(solution)/shard_map/dot_general | solution.py:945
  124.0 44.2 %attn_fwd.1 = (bf16[1536,512]{1,0:T(8,128)(2,1)S(1)}, bf16[1536,512]{1,0:T(8,128)(2,1)S(1)}, bf16[1536,512]{1,0:T(8,128)(2,1)}, bf16[1536,512]{1,0:T(8,128)(2,1)...) custom-call(f32[1536,1536]{1,0:T(8,128)} %fusion.23.raw, f32[1536,128]{1,0:T(8,128)S(1)} %get-tuple-element.136.cos, ...), custom_call_target="tpu_custom_call" | custom-call | flops 4831838208 | bytes 15728640 | tf_op jit(solution)/shard_map/attn_fwd/pallas_call | solution.py:660
  168.2 2.7 copy-done.14
  172.4 40.3 %rs_ctx.1 = bf16[384,2048]{1,0:T(8,128)(2,1)S(1)} custom-call(bf16[1536,512]{1,0:T(8,128)(2,1)S(1)} %copy-done.15, bf16[512,2048]{1,0:T(8,128)(2,1)S(1)} %bitcast.96), custom_call_target="tpu_custom_call" | custom-call | flops 3221225472 | bytes 5242880 | tf_op jit(solution)/shard_map/rs_ctx/pallas_call | solution.py:809
  219.7 35.0 %all-gather.3.cloned.1.call-done = bf16[6144,2048]{1,0:T(8,128)(2,1)} async-done(((bf16[384,2048]{1,0:T(8,128)(2,1)}), bf16[6144,2048]{1,0:T(8,128)(2,1)}) %all-gather.3.cloned.1.call-update) | async-done | bytes 25165840 | tf_op jit(solution)/shard_map/all_gather | solution.py:1028
  254.7 173.4 %experts_fwd.1 = (bf16[16,240,2048]{2,1,0:T(8,128)(2,1)}, bf16[16,240,1024]{2,1,0:T(8,128)(2,1)}, bf16[16,240,2048]{2,1,0:T(8,128)(2,1)}, bf16[16,240,1024]{2,1,...) custom-call(s32[16,384]{1,0:T(8,128)} %bitcast.106, ...), custom_call_target="tpu_custom_call" | custom-call | flops 82543902720 | bytes 117964800 | tf_op jit(solution)/shard_map/experts_fwd/pallas_call | solution.py:517
  428.2 7.2 all-to-all-start.1
  435.9 24.0 %bitcast_convert_fusion.1.refs_5_ = bf16[1024,2048]{1,0:T(8,128)(2,1)} fusion(bf16[16,240,1024]{2,1,0:T(8,128)(2,1)} %get-tuple-element.81, bf16[16,240,2048]{2,1,0:T(8,128)(2,1)} %get-tuple-element.82), kind=kOutput, calls=%fused_computation.2 | convolution fusion | flops 16108224512 | bytes 27787264 | tf_op jit(solution)/shard_map/dot_general | solution.py:949
  459.9 19.1 %bitcast_convert_fusion.2.rest_0_.refs_0_ = bf16[2048,1024]{1,0:T(8,128)(2,1)} fusion(bf16[16,240,2048]{2,1,0:T(8,128)(2,1)S(1)} %copy-done.42, bf16[16,240,1024]{2,1,0:T(8,128)(2,1)S(1)} %copy-done.43), kind=kOutput, calls=%fused_computation.3 | convolution fusion | flops 16108224512 | bytes 27787264 | tf_op jit(solution)/shard_map/dot_general | solution.py:949
  479.0 19.3 %bitcast_convert_fusion.rest_1_.refs_2_ = bf16[2048,1024]{1,0:T(8,128)(2,1)} fusion(bf16[16,240,2048]{2,1,0:T(8,128)(2,1)S(1)} %copy-done.42, bf16[16,240,1024]{2,1,0:T(8,128)(2,1)S(1)} %bitcast.131), kind=kOutput, calls=%fused_computation.1 | convolution fusion | flops 16108224512 | bytes 27787264 | tf_op jit(solution)/shard_map/dot_general | solution.py:949
  498.3 196.8 %back.1 = (bf16[384,2048]{1,0:T(8,128)(2,1)}, bf16[2048,1024]{1,0:T(8,128)(2,1)}, bf16[1536,1024]{1,0:T(8,128)(2,1)}) custom-call(s32[16,384]{1,0:T(8,128)} %bitcast.107, bf16[16,240,1024]{2,1,0:T(8,128)(2,1)} %get-tuple-element.83.dgp, bf16[16,240,1024]{2,1,0:T(8,128)(2,1)} %get-tuple-element.84.dup, bf16[2048,1024]{1,0:T(8,128)(2,1)} %bitcast.126, ...), custom_call_target="tpu_custom_call" | custom-call | flops 38252052480 | bytes 15728640 | tf_op jit(solution)/shard_map/back/pallas_call | solution.py:359
  695.3 3.4 multiply_reduce_fusion
  698.7 3.5 fusion.17
  706.5 49.0 %ag_ctx.1 = bf16[4,384,2048]{2,1,0:T(8,128)(2,1)} custom-call(bf16[384,2048]{1,0:T(8,128)(2,1)} %get-tuple-element.98.x), custom_call_target="tpu_custom_call" | custom-call | tf_op jit(solution)/shard_map/ag_ctx/pallas_call | solution.py:764
  755.5 8.1 convolution_convert_fusion.1.dm
  763.6 51.4 %attn_bwd.1 = (bf16[1536,1536]{1,0:T(8,128)(2,1)}, f32[2,512]{1,0:T(2,128)}) custom-call(bf16[1536,512]{1,0:T(8,128)(2,1)} %copy-done.16, bf16[1536,512]{1,0:T(8,128)(2,1)} %copy-done.17, bf16[1536,512]{1,0:T(8,128)(2,1)} %get-tuple-element.97.v, bf16[1536,512]{1,0:T(8,128)(2,1)} %convolution_convert_fusion.1.dm, f32[1536,1536]{1,0:T(8,128)} %fusion.23.raw, ...), custom_call_target="tpu_custom_call" | custom-call | flops 12079595520 | bytes 15728640 | tf_op jit(solution)/shard_map/attn_bwd/pallas_call | solution.py:719
  818.2 8.2 convolution_convert_fusion
  826.4 136.9 %tail.1 = (bf16[64,2048]{1,0:T(8,128)(2,1)}, bf16[64,2048]{1,0:T(8,128)(2,1)}, bf16[64,2048]{1,0:T(8,128)(2,1)}, bf16[64,2048]{1,0:T(8,128)(2,1)}, bf16[384,2048]{1,0:T(8,128)(2,1)}, /*index=5*/f32[24,2048]{1,0:T(8,128)}) custom-call(bf16[1536,2048]{1,0:T(8,128)(2,1)} %bitcast.123, bf16[1536,1536]{1,0:T(8,128)(2,1)} %get-tuple-element.100.dr, ...), custom_call_target="tpu_custom_call" | custom-call | flops 19327352832 | bytes 17301504 | tf_op jit(solution)/shard_map/tail/pallas_call | solution.py:223
  973.4 3.5 fusion.5
  983.2 14.0 %add_shares.1 = (f32[2048,1024]{1,0:T(8,128)}, f32[2048,1024]{1,0:T(8,128)}, f32[1024,2048]{1,0:T(8,128)}) custom-call(bf16[2048,1024]{1,0:T(8,128)(2,1)S(1)} %copy-done.5, bf16[2048,1024]{1,0:T(8,128)(2,1)S(1)} %copy-done.6, bf16[2048,1024]{1,0:T(8,128)(2,1)S(1)} %copy-done.3, bf16[1536,1024]{1,0:T(8,128)(2,1)S(1)} %copy-done.7, ...), custom_call_target="tpu_custom_call" | custom-call | flops 12582912 | bytes 50331648 | tf_op jit(solution)/shard_map/add_shares/pallas_call | solution.py:936
  (149 shorter events, 40.2 us)
Async XLA Ops:
  7.2 208.1 %copy-start = (bf16[2048,16]{0,1:T(8,128)(2,1)S(1)}, bf16[2048,16]{0,1:T(8,128)(2,1)}, u32[]{:S(2)}) copy-start(bf16[2048,16]{0,1:T(8,128)(2,1)} %param.29) | copy-start | bytes 196612
  7.2 247.5 %all-gather.3.cloned.1.call-start = ((), (), s32[]{:S(2)}) async-start(), calls=%async_computation.6 | async-start | bytes 26738688 | tf_op jit(solution)/shard_map/all_gather | solution.py:1028
  9.7 82.1 %copy-start.36 = (s32[1,1,384,8]{2,3,1,0:T(8,128)S(1)}, s32[1,1,384,8]{2,3,1,0:T(8,128)}, u32[]{:S(2)}) copy-start(s32[1,1,384,8]{2,3,1,0:T(8,128)} %param.20) | copy-start | bytes 36868
  9.8 94.3 %copy-start.38 = (bf16[2048]{0:T(1024)(128)(2,1)S(1)}, bf16[2048]{0:T(1024)(128)(2,1)}, u32[]{:S(2)}) copy-start(bf16[2048]{0:T(1024)(128)(2,1)} %param.25) | copy-start | bytes 12292
  9.8 94.3 %copy-start.39 = (bf16[2048]{0:T(1024)(128)(2,1)S(1)}, bf16[2048]{0:T(1024)(128)(2,1)}, u32[]{:S(2)}) copy-start(bf16[2048]{0:T(1024)(128)(2,1)} %param.26) | copy-start | bytes 12292
  9.8 94.3 %copy-start.11 = (s32[1,1,1536]{2,1,0:T(1,128)S(1)}, s32[1,1,1536]{2,1,0:T(1,128)}, u32[]{:S(2)}) copy-start(s32[1,1,1536]{2,1,0:T(1,128)} %param.19) | copy-start | bytes 18436
  12.8 91.7 %copy-start.40 = (bf16[2048]{0:T(1024)(128)(2,1)S(1)}, bf16[2048]{0:T(1024)(128)(2,1)}, u32[]{:S(2)}) copy-start(bf16[2048]{0:T(1024)(128)(2,1)} %param.28) | copy-start | bytes 12292
  92.8 126.3 %all-to-all-start = ((s32[16,1,384]{2,1,0:T(1,128)}), s32[16,1,384]{2,1,0:T(1,128)S(1)}, u32[]{:S(2)}, u32[]{:S(2)}) async-start(s32[16,1,384]{2,1,0:T(1,128)} %copy.44), calls=%async_computation | async-start | bytes 49152 | tf_op jit(solution)/shard_map/all_to_all | solution.py:1001
  104.0 866.4 %reduce-scatter.3.cloned.1.call-start = ((), (), s32[]{:S(2)}) async-start(), calls=%async_computation.4 | async-start | bytes 13369344 | tf_op jit(solution)/shard_map/reduce_scatter | solution.py:1056
  104.5 109.4 %copy-start.27 = (f32[2048]{0:T(1024)}, f32[2048]{0:T(1024)S(1)}, u32[]{:S(2)}) copy-start(f32[2048]{0:T(1024)S(1)} %convert_element_type.101) | copy-start | bytes 24580
  168.2 44.5 %copy-start.16 = (bf16[1536,512]{1,0:T(8,128)(2,1)}, bf16[1536,512]{1,0:T(8,128)(2,1)S(1)}, u32[]{:S(2)}) copy-start(bf16[1536,512]{1,0:T(8,128)(2,1)S(1)} %get-tuple-element.95.q) | copy-start | bytes 4718596
  168.2 44.5 %copy-start.17 = (bf16[1536,512]{1,0:T(8,128)(2,1)}, bf16[1536,512]{1,0:T(8,128)(2,1)S(1)}, u32[]{:S(2)}) copy-start(bf16[1536,512]{1,0:T(8,128)(2,1)S(1)} %get-tuple-element.96.k) | copy-start | bytes 4718596
  168.2 44.5 %copy-start.18 = (f32[24,128]{1,0:T(8,128)}, f32[24,128]{1,0:T(8,128)S(1)}, u32[]{:S(2)}) copy-start(f32[24,128]{1,0:T(8,128)S(1)} %get-tuple-element.99.inv) | copy-start | bytes 36868
  428.2 266.9 %all-to-all-start.1 = ((f32[16,1,384]{2,1,0:T(1,128)}), f32[16,1,384]{2,1,0:T(1,128)S(1)}, u32[]{:S(2)}, u32[]{:S(2)}) async-start(f32[16,1,384]{2,1,0:T(1,128)} %get-tuple-element.93), calls=%async_computation.2 | async-start | bytes 49152 | tf_op jit(solution)/shard_map/all_to_all | solution.py:1051
  435.4 535.0 %reduce-scatter.5.cloned.1.call-start = ((), (), s32[]{:S(2)}) async-start(), calls=%async_computation.5 | async-start | bytes 13369344 | tf_op jit(solution)/shard_map/reduce_scatter | solution.py:1089
  435.9 43.1 %slice-start = ((s8[7864320]{0:T(1024)(128)(4,1)}), s8[4194304]{0:T(1024)(128)(4,1)S(1)}, s32[]{:S(2)}) async-start(s8[7864320]{0:T(1024)(128)(4,1)} %bitcast.130), calls=%async_computation.7 | async-start | bytes 8388608
  498.3 196.9 %copy-start.25 = (f32[384,16]{0,1:T(8,128)S(1)}, f32[384,16]{0,1:T(8,128)}, u32[]{:S(2)}) copy-start(f32[384,16]{0,1:T(8,128)} %copy-done.24) | copy-start | bytes 73732
  498.3 196.9 %copy-start.30 = (f32[384]{0:T(512)S(1)}, f32[384]{0:T(512)}, u32[]{:S(2)}) copy-start(f32[384]{0:T(512)} %copy-done.29) | copy-start | bytes 4612
  498.3 196.9 %copy-start.33 = (f32[384]{0:T(512)S(1)}, f32[384]{0:T(512)}, u32[]{:S(2)}) copy-start(f32[384]{0:T(512)} %copy-done.32) | copy-start | bytes 4612
  498.3 196.9 %copy-start.2 = (bf16[384,2048]{1,0:T(8,128)(2,1)S(1)}, bf16[384,2048]{1,0:T(8,128)(2,1)}, u32[]{:S(2)}) copy-start(bf16[384,2048]{1,0:T(8,128)(2,1)} %copy-done.1) | copy-start | bytes 4718596
  498.3 196.9 %copy-start.28 = (f32[2048]{0:T(1024)S(1)}, f32[2048]{0:T(1024)}, u32[]{:S(2)}) copy-start(f32[2048]{0:T(1024)} %copy-done.27) | copy-start | bytes 24580
  498.3 196.9 %copy-start.35 = (f32[384]{0:T(512)S(1)}, f32[384]{0:T(512)}, u32[]{:S(2)}) copy-start(f32[384]{0:T(512)} %copy-done.34) | copy-start | bytes 4612
  704.5 267.6 %collective-permute-start.1 = (bf16[1024,2048]{1,0:T(8,128)(2,1)}, bf16[1024,2048]{1,0:T(8,128)(2,1)}, u32[]{:S(2)}, u32[]{:S(2)}) collective-permute-start(bf16[1024,2048]{1,0:T(8,128)(2,1)} %bitcast_convert_fusion.1.refs_5_), channel_id=1, source_target_pairs={{0,16},{16,0},{1,17},{17,1},{2,18},{18,2},{3,19},{19,3},{4,20},{20... | collective-permute-start | bytes 12582920 | tf_op jit(solution)/shard_map/ppermute | solution.py:1069
  706.1 266.1 %collective-permute-start = (bf16[512,1024]{1,0:T(8,128)(2,1)}, bf16[512,1024]{1,0:T(8,128)(2,1)S(1)}, u32[]{:S(2)}, u32[]{:S(2)}) collective-permute-start(bf16[512,1024]{1,0:T(8,128)(2,1)} %slice.40), channel_id=1, source_target_pairs={{0,16},{16,0},{1,17},{17,1},{2,18},{18,2},{3,19},{19,3},{4,20},{20... | collective-permute-start | bytes 3145736 | tf_op jit(solution)/shard_map/ppermute | solution.py:1069
  (29 other events, 255.8 us)
Sparse Core Ops, SparseCore 0:
  92.0 162.6 all-gather.2
  428.3 163.4 reduce-scatter.2
  702.3 132.5 reduce-scatter.4
